TPU v7x, 32 devices: a whole 2x2x4 slice. The times are simulated.
32 devices in a mesh: seq: 8 (over z, y), batch: 4 (over x, core).
Axes of the slice: x: 2, y: 2, z: 4, core: 2. Of those that a mesh axis runs over, the one named last changes fastest.
Arguments:
- inputs: bfloat16 [8, 2048, 768], P('batch', 'seq'), may hold values from -6 to 6
- lengths: int32 [8], P('batch'), may hold values from 512 to 2048, as said below
- cotangent: bfloat16 [8, 2048, 768], P('batch', 'seq'), may hold values from -6 to 6
- local_query: bfloat16 [768, 768], replicated, may hold values from -0.21875 to 0.21875
- local_query_bias: float32 [768], replicated, may hold values from -3 to 3
- local_key: bfloat16 [768, 768], replicated, may hold values from -0.21875 to 0.21875
- local_value: bfloat16 [768, 768], replicated, may hold values from -0.21875 to 0.21875
- local_value_bias: float32 [768], replicated, may hold values from -3 to 3
- local_output: bfloat16 [768, 768], replicated, may hold values from -0.875 to 0.875
- local_output_bias: float32 [768], replicated, may hold values from -3 to 3
- pooled_query: bfloat16 [768, 768], replicated, may hold values from -0.15625 to 0.15625
- pooled_query_bias: float32 [768], replicated, may hold values from -3 to 3
- pooled_output: bfloat16 [768, 768], replicated, may hold values from -1.25 to 1.25
- pooled_output_bias: float32 [768], replicated, may hold values from -3 to 3
- conv_key: float32 [768, 5], replicated, may hold values from -2.5 to 2.5
- conv_value: float32 [768, 5], replicated, may hold values from -2.5 to 2.5
- conv_value_bias: float32 [768], replicated, may hold values from -3 to 3
- norm_gain: float32 [768], replicated, may hold values from 0.5 to 1.5
- norm_shift: float32 [768], replicated, may hold values from -1.75 to 1.75
- expand_weight: bfloat16 [768, 3072], replicated, may hold values from -0.21875 to 0.21875
- expand_bias: float32 [3072], replicated, may hold values from -3 to 3
- reduce_weight: bfloat16 [3072, 768], replicated, may hold values from -0.109375 to 0.109375
- reduce_bias: float32 [768], replicated, may hold values from -3 to 3
- final_gain: float32 [768], replicated, may hold values from 0.5 to 1.5
- final_shift: float32 [768], replicated, may hold values from -1.75 to 1.75
Outputs:
- outputs: bfloat16 [8, 2048, 768], P('batch', 'seq')
- input_grad: bfloat16 [8, 2048, 768], P('batch', 'seq')
- grad_local_query: float32 [768, 768], P('seq')
- grad_local_query_bias: float32 [768], P('seq')
- grad_local_key: float32 [768, 768], P('seq')
- grad_local_value: float32 [768, 768], P('seq')
- grad_local_value_bias: float32 [768], P('seq')
- grad_local_output: float32 [768, 768], P('seq')
- grad_local_output_bias: float32 [768], P('seq')
- grad_pooled_query: float32 [768, 768], P('seq')
- grad_pooled_query_bias: float32 [768], P('seq')
- grad_pooled_output: float32 [768, 768], P('seq')
- grad_pooled_output_bias: float32 [768], P('seq')
- grad_conv_key: float32 [768, 5], P('seq')
- grad_conv_value: float32 [768, 5], P('seq')
- grad_conv_value_bias: float32 [768], P('seq')
- grad_norm_gain: float32 [768], P('seq')
- grad_norm_shift: float32 [768], P('seq')
- grad_expand_weight: float32 [768, 3072], P('seq')
- grad_expand_bias: float32 [3072], P('seq')
- grad_reduce_weight: float32 [3072, 768], P('seq')
- grad_reduce_bias: float32 [768], P('seq')
- grad_final_gain: float32 [768], P('seq')
- grad_final_shift: float32 [768], P('seq')
Inputs may be any that keep to these rules, and one draw needn't show every extreme that they name: `lengths`: each document fills its slots from the first one and is padded at its end; documents b with the same b // 2 form a group, and in each group one document, drawn from the seed, fills all 2048 slots.
All inputs are finite; a program needn't handle non-finite values.
Results may differ from a plain program's by a relative error of at most 0.029.
The roundings to bfloat16 on the way count: a program that leaves them out, or rounds other values in their place, can miss the bound.
Values may be sent and summed in bfloat16 or wider, within the bound.
No kernel may reach another device: no remote copies, remote signals or barrier semaphores. Data moves between devices by JAX's collectives and lax.ppermute only.
A program may use at most 192 MiB of HBM per device.

v0:
```python
import math

import jax
import jax.numpy as jnp
from jax import lax
from jax.sharding import PartitionSpec as P

HEADS = 12
HD = 64
WIN = 128
PWIN = 512
KER = 5
STRIDE = 4


NEGATIVE = -1e30


def padded(cells, sides, width):
    for axis, dim in sides:
        count = lax.axis_size(axis)
        ends = count - 1
        head = lax.slice_in_dim(cells, 0, width, axis=dim)
        tail = lax.slice_in_dim(cells, cells.shape[dim] - width, cells.shape[dim], axis=dim)
        cells = jnp.concatenate(
            [
                lax.ppermute(tail, axis, [(i, (i + 1) % count) for i in range(ends)]),
                cells,
                lax.ppermute(head, axis, [((i + 1) % count, i) for i in range(ends)]),
            ],
            axis=dim,
        )
    return cells


def from_behind(shard, axis, by):
    length = lax.axis_size(axis)
    pairs = [(i, i + by) for i in range(length) if 0 <= i + by < length]
    return lax.ppermute(shard, axis, pairs)


def layer_norm(values, scales, offsets):
    centred = values - jnp.mean(values, axis=-1, keepdims=True)
    spread = jnp.mean(centred * centred, axis=-1, keepdims=True)
    return centred * lax.rsqrt(spread + 1e-05) * scales + offsets


def exact_gelu(values):
    return jax.nn.gelu(values, approximate=False)


def project(operand, matrix):
    return jnp.dot(operand, matrix, preferred_element_type=jnp.float32)


def project_back(operand, matrix):
    return jnp.einsum("ra,ba->rb", operand, matrix, preferred_element_type=jnp.float32)


def weight_grad(operand, gradient):
    return jnp.einsum("ra,rb->ab", operand, gradient, preferred_element_type=jnp.float32)


def column_sum(matrix):
    return jnp.sum(matrix.astype(jnp.float32), axis=0)


def head_split(matrix):
    return matrix.reshape(matrix.shape[0], HEADS, HD)


def add_tuples(former, latter):
    if former is None:
        return latter
    return tuple((left_item + right_item for left_item, right_item in zip(former, latter)))


def local_allowed(query_place, key_place, length):
    half_width = WIN // 2
    nearby = (key_place[None, :] >= query_place[:, None] - half_width) & (
        key_place[None, :] < query_place[:, None] + half_width
    )
    usable = (key_place >= 0) & (key_place < length)
    return nearby & usable[None, :] | (key_place[None, :] == query_place[:, None])


def pooled_allowed(centres, key_place, length):
    half_width = PWIN // 2
    nearby = (key_place[None, :] >= centres[:, None] - half_width) & (
        key_place[None, :] < centres[:, None] + half_width
    )
    usable = (key_place >= 0) & (key_place * STRIDE < length)
    return nearby & usable[None, :] | (key_place[None, :] == centres[:, None])


def masked_scores(query_heads, key_heads, allowed):
    raw_scores = jnp.einsum(
        "qhd,khd->hqk", query_heads, key_heads, preferred_element_type=jnp.float32
    )
    return jnp.where(allowed[None], raw_scores * (1.0 / math.sqrt(HD)), NEGATIVE)


def attend_forward(query_rows, key_rows, value_rows, allowed):
    scores = masked_scores(head_split(query_rows), head_split(key_rows), allowed)
    maximum = jnp.max(scores, axis=-1, keepdims=True)
    exponent = jnp.exp(scores - maximum)
    denominator = jnp.sum(exponent, axis=-1, keepdims=True)
    weights = (exponent / denominator).astype(jnp.bfloat16)
    mixture = jnp.einsum(
        "hqk,khd->qhd", weights, head_split(value_rows), preferred_element_type=jnp.float32
    )
    return (
        mixture.reshape(query_rows.shape[0], -1).astype(jnp.bfloat16),
        maximum + jnp.log(denominator),
    )


def attend_backward(query_rows, key_rows, value_rows, allowed, log_total, grad_mixture):
    query_heads = head_split(query_rows)
    key_heads = head_split(key_rows)
    grad_heads = head_split(grad_mixture)
    weights = jnp.exp(masked_scores(query_heads, key_heads, allowed) - log_total)
    grad_weights = jnp.einsum(
        "qhd,khd->hqk", grad_heads, head_split(value_rows), preferred_element_type=jnp.float32
    )
    row_dots = jnp.sum(weights * grad_weights, axis=-1, keepdims=True)
    grad_raw = (weights * (grad_weights - row_dots) * (1.0 / math.sqrt(HD))).astype(jnp.bfloat16)
    grad_queries = jnp.einsum(
        "hqk,khd->qhd", grad_raw, key_heads, preferred_element_type=jnp.float32
    )
    grad_keys = jnp.einsum(
        "hqk,qhd->khd", grad_raw, query_heads, preferred_element_type=jnp.float32
    )
    grad_values = jnp.einsum(
        "hqk,qhd->khd", weights.astype(jnp.bfloat16), grad_heads, preferred_element_type=jnp.float32
    )
    key_count = key_rows.shape[0]
    return (
        grad_queries.reshape(query_rows.shape[0], -1),
        jnp.stack([grad_keys.reshape(key_count, -1), grad_values.reshape(key_count, -1)]),
    )


def forward_part(tokens, length, grad_rows, weights):
    (
        local_query,
        local_query_bias,
        local_key,
        local_value,
        local_value_bias,
        local_output,
        local_output_bias,
        pooled_query,
        pooled_query_bias,
        pooled_output,
        pooled_output_bias,
        conv_key,
        conv_value,
        conv_value_bias,
        norm_gain,
        norm_shift,
        expand_weight,
        expand_bias,
        reduce_weight,
        reduce_bias,
        final_gain,
        final_shift,
    ) = weights
    row_count = tokens.shape[0]
    model_width = tokens.shape[1]
    offset = lax.axis_index("seq") * row_count
    positions = offset + jnp.arange(row_count, dtype=jnp.int32)
    validity = (positions < length).astype(jnp.float32)[:, None]
    block_rows = min(512, row_count)
    half_local = WIN // 2
    half_pool = PWIN // 2
    pooled_rows = row_count // STRIDE
    pooled_block = block_rows // STRIDE
    local_span = block_rows + 2 * half_local
    pooled_span = pooled_block + 2 * half_pool
    query_one = (project(tokens, local_query) + local_query_bias).astype(jnp.bfloat16)
    key_one = project(tokens, local_key).astype(jnp.bfloat16)
    value_one = (project(tokens, local_value) + local_value_bias).astype(jnp.bfloat16)
    extended = padded(jnp.stack([key_one, value_one]), (("seq", 1),), half_local)
    block_index = 0
    first_row = block_index * block_rows
    key_place = offset + first_row - half_local + jnp.arange(local_span, dtype=jnp.int32)
    allowed = local_allowed(positions, key_place, length)
    mixture, log_total = attend_forward(
        query_one,
        extended[0, first_row : first_row + local_span],
        extended[1, first_row : first_row + local_span],
        allowed,
    )
    local_masks = [allowed]
    local_totals = [log_total]
    local_parts = mixture
    middle = tokens.astype(jnp.float32) + project(local_parts, local_output) + local_output_bias
    middle_low = middle.astype(jnp.bfloat16)
    query_two = (project(middle_low, pooled_query) + pooled_query_bias).astype(jnp.bfloat16)
    extended_place = offset - half_local + jnp.arange(row_count + 2 * half_local, dtype=jnp.int32)
    extended_valid = ((extended_place >= 0) & (extended_place < length)).astype(jnp.float32)
    kernels = jnp.stack([conv_key, conv_value])
    pooled_sum = jnp.zeros((2, pooled_rows, model_width), jnp.float32)
    tap_inputs = []
    tap_masks = []
    for tap_index in range(KER):
        tap_start = half_local - KER // 2 + tap_index
        tap_mask = lax.slice(extended_valid, (tap_start,), (tap_start + row_count,), (STRIDE,))
        tap_values = (
            lax.slice(
                extended, (0, tap_start, 0), (2, tap_start + row_count, model_width), (1, STRIDE, 1)
            ).astype(jnp.float32)
            * tap_mask[None, :, None]
        )
        tap_inputs.append(tap_values)
        tap_masks.append(tap_mask)
        pooled_sum = pooled_sum + tap_values * kernels[:, None, :, tap_index]
    pooled_pair = jnp.stack([pooled_sum[0], pooled_sum[1] + conv_value_bias]).astype(jnp.bfloat16)
    reach_count = (half_pool + pooled_rows - 1) // pooled_rows
    left_pieces = []
    right_pieces = []
    piece_sizes = []
    for distance in range(1, reach_count + 1):
        needed = min(pooled_rows, half_pool - (distance - 1) * pooled_rows)
        piece_sizes.append(needed)
        left_pieces.append(from_behind(pooled_pair[:, pooled_rows - needed :], "seq", distance))
        right_pieces.append(from_behind(pooled_pair[:, :needed], "seq", -distance))
    pooled_extended = jnp.concatenate(left_pieces[::-1] + [pooled_pair] + right_pieces, axis=1)
    block_index = 0
    first_pooled = block_index * pooled_block
    centres = positions // STRIDE
    key_place = (
        offset // STRIDE + first_pooled - half_pool + jnp.arange(pooled_span, dtype=jnp.int32)
    )
    allowed = pooled_allowed(centres, key_place, length)
    mixture, log_total = attend_forward(
        query_two,
        pooled_extended[0, first_pooled : first_pooled + pooled_span],
        pooled_extended[1, first_pooled : first_pooled + pooled_span],
        allowed,
    )
    pooled_masks = [allowed]
    pooled_totals = [log_total]
    summed = middle + project(mixture, pooled_output) + pooled_output_bias
    normed, first_norm_back = jax.vjp(layer_norm, summed, norm_gain, norm_shift)
    normed_low = normed.astype(jnp.bfloat16)
    hidden_pre = project(normed_low, expand_weight) + expand_bias
    hidden, gelu_back = jax.vjp(exact_gelu, hidden_pre)
    hidden_low = hidden.astype(jnp.bfloat16)
    residual_sum = normed + project(hidden_low, reduce_weight) + reduce_bias
    result, final_norm_back = jax.vjp(layer_norm, residual_sum, final_gain, final_shift)
    outputs = (validity * result).astype(jnp.bfloat16)
    grad_rest, grad_final_gain, grad_final_shift = final_norm_back(
        validity * grad_rows.astype(jnp.float32)
    )
    grad_branch = grad_rest.astype(jnp.bfloat16)
    grad_reduce_weight = weight_grad(hidden_low, grad_branch)
    grad_reduce_bias = column_sum(grad_branch)
    (grad_hidden_pre,) = gelu_back(project_back(grad_branch, reduce_weight))
    grad_pre = grad_hidden_pre.astype(jnp.bfloat16)
    grad_expand_weight = weight_grad(normed_low, grad_pre)
    grad_expand_bias = column_sum(grad_pre)
    grad_summed, grad_norm_gain, grad_norm_shift = first_norm_back(
        grad_rest + project_back(grad_pre, expand_weight)
    )
    feed_grads = (
        grad_expand_weight,
        grad_expand_bias,
        grad_reduce_weight,
        grad_reduce_bias,
        grad_norm_gain,
        grad_norm_shift,
        grad_final_gain,
        grad_final_shift,
    )
    kept = {
        "tokens": tokens,
        "query_one": query_one,
        "extended": extended,
        "local_masks": local_masks,
        "local_totals": local_totals,
        "mixture_one": local_parts,
        "middle_low": middle_low,
        "query_two": query_two,
        "pooled_extended": pooled_extended,
        "pooled_masks": pooled_masks,
        "pooled_totals": pooled_totals,
        "mixture_two": mixture,
        "tap_inputs": tap_inputs,
        "tap_masks": tap_masks,
        "kernels": kernels,
        "grad_summed": grad_summed,
        "piece_sizes": piece_sizes,
    }
    return (outputs, feed_grads, kept)


def backward_part(kept, weights):
    (
        local_query,
        local_query_bias,
        local_key,
        local_value,
        local_value_bias,
        local_output,
        local_output_bias,
        pooled_query,
        pooled_query_bias,
        pooled_output,
        pooled_output_bias,
        conv_key,
        conv_value,
        conv_value_bias,
        norm_gain,
        norm_shift,
        expand_weight,
        expand_bias,
        reduce_weight,
        reduce_bias,
        final_gain,
        final_shift,
    ) = weights
    tokens = kept["tokens"]
    query_one = kept["query_one"]
    extended = kept["extended"]
    query_two = kept["query_two"]
    pooled_extended = kept["pooled_extended"]
    mixture_one = kept["mixture_one"]
    mixture_two = kept["mixture_two"]
    grad_summed = kept["grad_summed"]
    piece_sizes = kept["piece_sizes"]
    kernels = kept["kernels"]
    row_count = tokens.shape[0]
    model_width = tokens.shape[1]
    block_rows = min(512, row_count)
    half_local = WIN // 2
    half_pool = PWIN // 2
    pooled_rows = row_count // STRIDE
    pooled_block = block_rows // STRIDE
    local_span = block_rows + 2 * half_local
    pooled_span = pooled_block + 2 * half_pool
    grad_second = grad_summed.astype(jnp.bfloat16)
    grad_pooled_output = weight_grad(mixture_two, grad_second)
    grad_pooled_output_bias = column_sum(grad_second)
    grad_mixture_two = project_back(grad_second, pooled_output).astype(jnp.bfloat16)
    pooled_grads = jnp.zeros((2, pooled_rows + 2 * half_pool, model_width), jnp.float32)
    block_index = 0
    first_pooled = block_index * pooled_block
    grad_queries, grad_pair = attend_backward(
        query_two,
        pooled_extended[0, first_pooled : first_pooled + pooled_span],
        pooled_extended[1, first_pooled : first_pooled + pooled_span],
        kept["pooled_masks"][block_index],
        kept["pooled_totals"][block_index],
        grad_mixture_two,
    )
    query_two_grads = grad_queries
    pooled_grads = pooled_grads.at[:, first_pooled : first_pooled + pooled_span].add(grad_pair)
    grad_query_two = query_two_grads.astype(jnp.bfloat16)
    grad_pooled_query = weight_grad(kept["middle_low"], grad_query_two)
    grad_pooled_query_bias = column_sum(grad_query_two)
    grad_middle = grad_summed + project_back(grad_query_two, pooled_query)
    own_pooled = pooled_grads[:, half_pool : half_pool + pooled_rows]
    left_cursor = half_pool
    right_cursor = half_pool + pooled_rows
    for distance in range(1, len(piece_sizes) + 1):
        needed = piece_sizes[distance - 1]
        returned_left = from_behind(
            pooled_grads[:, left_cursor - needed : left_cursor].astype(jnp.bfloat16),
            "seq",
            -distance,
        ).astype(jnp.float32)
        returned_right = from_behind(
            pooled_grads[:, right_cursor : right_cursor + needed].astype(jnp.bfloat16),
            "seq",
            distance,
        ).astype(jnp.float32)
        own_pooled = (
            own_pooled.at[:, pooled_rows - needed :]
            .add(returned_left)
            .at[:, :needed]
            .add(returned_right)
        )
        left_cursor = left_cursor - needed
        right_cursor = right_cursor + needed
    grad_first = grad_middle.astype(jnp.bfloat16)
    grad_local_output = weight_grad(mixture_one, grad_first)
    grad_local_output_bias = column_sum(grad_first)
    grad_mixture_one = project_back(grad_first, local_output).astype(jnp.bfloat16)
    local_grads = jnp.zeros((2, row_count + 2 * half_local, model_width), jnp.float32)
    block_index = 0
    first_row = block_index * block_rows
    grad_queries, grad_pair = attend_backward(
        query_one,
        extended[0, first_row : first_row + local_span],
        extended[1, first_row : first_row + local_span],
        kept["local_masks"][block_index],
        kept["local_totals"][block_index],
        grad_mixture_one,
    )
    local_grads = local_grads.at[:, first_row : first_row + local_span].add(grad_pair)
    conv_columns = []
    for tap_index in range(KER):
        tap_start = half_local - KER // 2 + tap_index
        conv_columns.append(jnp.sum(own_pooled * kept["tap_inputs"][tap_index], axis=1))
        local_grads = local_grads.at[:, tap_start : tap_start + row_count : STRIDE].add(
            own_pooled
            * kernels[:, None, :, tap_index]
            * kept["tap_masks"][tap_index][None, :, None]
        )
    grad_conv = jnp.stack(conv_columns, axis=-1)
    grad_conv_key = grad_conv[0]
    grad_conv_value = grad_conv[1]
    grad_conv_value_bias = jnp.sum(own_pooled[1], axis=0)
    from_right = from_behind(local_grads[:, :half_local].astype(jnp.bfloat16), "seq", -1).astype(
        jnp.float32
    )
    from_left = from_behind(
        local_grads[:, row_count + half_local :].astype(jnp.bfloat16), "seq", 1
    ).astype(jnp.float32)
    grad_pair_one = local_grads[:, half_local : half_local + row_count]
    grad_pair_one = (
        grad_pair_one.at[:, row_count - half_local :]
        .add(from_right)
        .at[:, :half_local]
        .add(from_left)
    )
    grad_key_one = grad_pair_one[0].astype(jnp.bfloat16)
    grad_value_one = grad_pair_one[1].astype(jnp.bfloat16)
    grad_query_one = grad_queries.astype(jnp.bfloat16)
    grad_local_query = weight_grad(tokens, grad_query_one)
    grad_local_query_bias = column_sum(grad_query_one)
    grad_local_key = weight_grad(tokens, grad_key_one)
    grad_local_value = weight_grad(tokens, grad_value_one)
    grad_local_value_bias = column_sum(grad_value_one)
    input_grad = (
        grad_middle
        + project_back(grad_query_one, local_query)
        + project_back(grad_key_one, local_key)
        + project_back(grad_value_one, local_value)
    ).astype(jnp.bfloat16)
    attention_grads = (
        grad_local_query,
        grad_local_query_bias,
        grad_local_key,
        grad_local_value,
        grad_local_value_bias,
        grad_local_output,
        grad_local_output_bias,
        grad_pooled_query,
        grad_pooled_query_bias,
        grad_pooled_output,
        grad_pooled_output_bias,
        grad_conv_key,
        grad_conv_value,
        grad_conv_value_bias,
    )
    return (input_grad, attention_grads)


def on_device(
    inputs,
    lengths,
    cotangent,
    local_query,
    local_query_bias,
    local_key,
    local_value,
    local_value_bias,
    local_output,
    local_output_bias,
    pooled_query,
    pooled_query_bias,
    pooled_output,
    pooled_output_bias,
    conv_key,
    conv_value,
    conv_value_bias,
    norm_gain,
    norm_shift,
    expand_weight,
    expand_bias,
    reduce_weight,
    reduce_bias,
    final_gain,
    final_shift,
):
    weights = (
        local_query,
        local_query_bias,
        local_key,
        local_value,
        local_value_bias,
        local_output,
        local_output_bias,
        pooled_query,
        pooled_query_bias,
        pooled_output,
        pooled_output_bias,
        conv_key,
        conv_value,
        conv_value_bias,
        norm_gain,
        norm_shift,
        expand_weight,
        expand_bias,
        reduce_weight,
        reduce_bias,
        final_gain,
        final_shift,
    )
    doc_count = inputs.shape[0]
    feed_totals = None
    attention_totals = None
    output_list = []
    input_grad_list = []
    for doc_index in range(doc_count):
        result, feed_grads, kept = forward_part(
            inputs[doc_index], lengths[doc_index], cotangent[doc_index], weights
        )
        output_list.append(result)
        feed_totals = add_tuples(feed_totals, feed_grads)
        doc_input_grad, attention_grads = backward_part(kept, weights)
        input_grad_list.append(doc_input_grad)
        attention_totals = add_tuples(attention_totals, attention_grads)
    outputs = jnp.stack(output_list)
    input_grad = jnp.stack(input_grad_list)
    (
        grad_local_query,
        grad_local_query_bias,
        grad_local_key,
        grad_local_value,
        grad_local_value_bias,
        grad_local_output,
        grad_local_output_bias,
        grad_pooled_query,
        grad_pooled_query_bias,
        grad_pooled_output,
        grad_pooled_output_bias,
        grad_conv_key,
        grad_conv_value,
        grad_conv_value_bias,
    ) = attention_totals
    (
        grad_expand_weight,
        grad_expand_bias,
        grad_reduce_weight,
        grad_reduce_bias,
        grad_norm_gain,
        grad_norm_shift,
        grad_final_gain,
        grad_final_shift,
    ) = feed_totals
    (
        grad_local_query,
        grad_local_query_bias,
        grad_local_key,
        grad_local_value,
        grad_local_value_bias,
        grad_local_output,
        grad_local_output_bias,
        grad_pooled_query,
        grad_pooled_query_bias,
        grad_pooled_output,
        grad_pooled_output_bias,
        grad_conv_key,
        grad_conv_value,
        grad_conv_value_bias,
        grad_expand_weight,
        grad_expand_bias,
        grad_reduce_weight,
        grad_reduce_bias,
        grad_norm_gain,
        grad_norm_shift,
        grad_final_gain,
        grad_final_shift,
    ) = (
        lax.psum_scatter(grad_local_query, "seq", scatter_dimension=0, tiled=True),
        lax.psum_scatter(grad_local_query_bias, "seq", scatter_dimension=0, tiled=True),
        lax.psum_scatter(grad_local_key, "seq", scatter_dimension=0, tiled=True),
        lax.psum_scatter(grad_local_value, "seq", scatter_dimension=0, tiled=True),
        lax.psum_scatter(grad_local_value_bias, "seq", scatter_dimension=0, tiled=True),
        lax.psum_scatter(grad_local_output, "seq", scatter_dimension=0, tiled=True),
        lax.psum_scatter(grad_local_output_bias, "seq", scatter_dimension=0, tiled=True),
        lax.psum_scatter(grad_pooled_query, "seq", scatter_dimension=0, tiled=True),
        lax.psum_scatter(grad_pooled_query_bias, "seq", scatter_dimension=0, tiled=True),
        lax.psum_scatter(grad_pooled_output, "seq", scatter_dimension=0, tiled=True),
        lax.psum_scatter(grad_pooled_output_bias, "seq", scatter_dimension=0, tiled=True),
        lax.psum_scatter(grad_conv_key, "seq", scatter_dimension=0, tiled=True),
        lax.psum_scatter(grad_conv_value, "seq", scatter_dimension=0, tiled=True),
        lax.psum_scatter(grad_conv_value_bias, "seq", scatter_dimension=0, tiled=True),
        lax.psum_scatter(grad_expand_weight, "seq", scatter_dimension=0, tiled=True),
        lax.psum_scatter(grad_expand_bias, "seq", scatter_dimension=0, tiled=True),
        lax.psum_scatter(grad_reduce_weight, "seq", scatter_dimension=0, tiled=True),
        lax.psum_scatter(grad_reduce_bias, "seq", scatter_dimension=0, tiled=True),
        lax.psum_scatter(grad_norm_gain, "seq", scatter_dimension=0, tiled=True),
        lax.psum_scatter(grad_norm_shift, "seq", scatter_dimension=0, tiled=True),
        lax.psum_scatter(grad_final_gain, "seq", scatter_dimension=0, tiled=True),
        lax.psum_scatter(grad_final_shift, "seq", scatter_dimension=0, tiled=True),
    )
    (
        sum_local_query,
        sum_local_query_bias,
        sum_local_key,
        sum_local_value,
        sum_local_value_bias,
        sum_local_output,
        sum_local_output_bias,
        sum_pooled_query,
        sum_pooled_query_bias,
        sum_pooled_output,
        sum_pooled_output_bias,
        sum_conv_key,
        sum_conv_value,
        sum_conv_value_bias,
        sum_expand_weight,
        sum_expand_bias,
        sum_reduce_weight,
        sum_reduce_bias,
        sum_norm_gain,
        sum_norm_shift,
        sum_final_gain,
        sum_final_shift,
    ) = (
        lax.psum(grad_local_query.astype(jnp.bfloat16), "batch").astype(jnp.float32),
        lax.psum(grad_local_query_bias.astype(jnp.bfloat16), "batch").astype(jnp.float32),
        lax.psum(grad_local_key.astype(jnp.bfloat16), "batch").astype(jnp.float32),
        lax.psum(grad_local_value.astype(jnp.bfloat16), "batch").astype(jnp.float32),
        lax.psum(grad_local_value_bias.astype(jnp.bfloat16), "batch").astype(jnp.float32),
        lax.psum(grad_local_output.astype(jnp.bfloat16), "batch").astype(jnp.float32),
        lax.psum(grad_local_output_bias.astype(jnp.bfloat16), "batch").astype(jnp.float32),
        lax.psum(grad_pooled_query.astype(jnp.bfloat16), "batch").astype(jnp.float32),
        lax.psum(grad_pooled_query_bias.astype(jnp.bfloat16), "batch").astype(jnp.float32),
        lax.psum(grad_pooled_output.astype(jnp.bfloat16), "batch").astype(jnp.float32),
        lax.psum(grad_pooled_output_bias.astype(jnp.bfloat16), "batch").astype(jnp.float32),
        lax.psum(grad_conv_key.astype(jnp.bfloat16), "batch").astype(jnp.float32),
        lax.psum(grad_conv_value.astype(jnp.bfloat16), "batch").astype(jnp.float32),
        lax.psum(grad_conv_value_bias.astype(jnp.bfloat16), "batch").astype(jnp.float32),
        lax.psum(grad_expand_weight.astype(jnp.bfloat16), "batch").astype(jnp.float32),
        lax.psum(grad_expand_bias.astype(jnp.bfloat16), "batch").astype(jnp.float32),
        lax.psum(grad_reduce_weight.astype(jnp.bfloat16), "batch").astype(jnp.float32),
        lax.psum(grad_reduce_bias.astype(jnp.bfloat16), "batch").astype(jnp.float32),
        lax.psum(grad_norm_gain.astype(jnp.bfloat16), "batch").astype(jnp.float32),
        lax.psum(grad_norm_shift.astype(jnp.bfloat16), "batch").astype(jnp.float32),
        lax.psum(grad_final_gain.astype(jnp.bfloat16), "batch").astype(jnp.float32),
        lax.psum(grad_final_shift.astype(jnp.bfloat16), "batch").astype(jnp.float32),
    )
    return (
        outputs,
        input_grad,
        sum_local_query,
        sum_local_query_bias,
        sum_local_key,
        sum_local_value,
        sum_local_value_bias,
        sum_local_output,
        sum_local_output_bias,
        sum_pooled_query,
        sum_pooled_query_bias,
        sum_pooled_output,
        sum_pooled_output_bias,
        sum_conv_key,
        sum_conv_value,
        sum_conv_value_bias,
        sum_norm_gain,
        sum_norm_shift,
        sum_expand_weight,
        sum_expand_bias,
        sum_reduce_weight,
        sum_reduce_bias,
        sum_final_gain,
        sum_final_shift,
    )


def solution(mesh):
    return jax.shard_map(
        on_device,
        mesh=mesh,
        in_specs=(
            P("batch", "seq", None),
            P("batch"),
            P("batch", "seq", None),
            P(),
            P(),
            P(),
            P(),
            P(),
            P(),
            P(),
            P(),
            P(),
            P(),
            P(),
            P(),
            P(),
            P(),
            P(),
            P(),
            P(),
            P(),
            P(),
            P(),
            P(),
            P(),
        ),
        out_specs=(
            P("batch", "seq", None),
            P("batch", "seq", None),
            P("seq", None),
            P("seq"),
            P("seq", None),
            P("seq", None),
            P("seq"),
            P("seq", None),
            P("seq"),
            P("seq", None),
            P("seq"),
            P("seq", None),
            P("seq"),
            P("seq", None),
            P("seq", None),
            P("seq"),
            P("seq"),
            P("seq"),
            P("seq", None),
            P("seq"),
            P("seq", None),
            P("seq"),
            P("seq"),
            P("seq"),
        ),
        check_vma=False,
    )
```

profile of v0, /device:TPU:1, one launch (start us, length us, event | category | flops | bytes accessed | tf_op | source)
XLA Modules:
  0.0 1359.1 jit_solution(6488053962684009846)
XLA Ops:
  145.2 9.3 collective-permute-done.9
  198.3 8.5 multiply_convert_fusion.5
  208.6 9.7 multiply_convert_fusion.4
  272.6 13.3 fusion.25
  306.4 13.3 fusion.19
  336.5 8.9 collective-permute-start.27
  377.3 13.1 convert_reduce_fusion.6
  390.4 13.7 %convert_reduce_fusion.7 = (f32[12,64]{1,0:T(8,128)}, bf16[12,64,256]{2,1,0:T(8,128)(2,1)}) fusion(bf16[576,12,64]{0,2,1:T(8,128)(2,1)S(1)} %bitcast.308, f32[12,256,576]{1,2,0:T(8,128)} %fusion.311, f32[12,256,576]{1,2,0:T(8,128)} %copy-done.2, f32[12,256]{1,0:T(8,128)S(1)} %copy-done.158), kind=kOutput, calls=%fused_computation.243 | convolution fusion | flops 239471424 | bytes 15449088 | tf_op jit(solution)/shard_map/hqk,khd->qhd/dot_general | solution.py:128
  429.3 25.0 %convert_reduce_fusion.12 = (f32[12,64]{1,0:T(8,128)}, bf16[12,64,256]{2,1,0:T(8,128)(2,1)}) fusion(bf16[384,12,64]{0,2,1:T(8,128)(2,1)S(1)} %bitcast.326, f32[12,256,384]{2,1,0:T(8,128)} %fusion.314, f32[12,256,384]{2,1,0:T(8,128)} %copy-done.4, f32[12,256]{1,0:T(8,128)S(1)} %copy-done.160), kind=kOutput, calls=%fused_computation.248 | convolution fusion | flops 159844992 | bytes 10435584 | tf_op jit(solution)/shard_map/hqk,khd->qhd/dot_general | solution.py:128
  457.4 24.4 %convert_reduce_fusion.13 = (f32[12,64]{1,0:T(8,128)}, bf16[12,64,256]{2,1,0:T(8,128)(2,1)S(1)}) fusion(bf16[384,12,64]{0,2,1:T(8,128)(2,1)S(1)} %bitcast.324, f32[12,256,384]{2,1,0:T(8,128)} %fusion.312, f32[12,256,384]{2,1,0:T(8,128)} %copy-done.3, f32[12,256]{1,0:T(8,128)S(1)} %copy-done.159), kind=kOutput, calls=%fused_computation.249 | convolution fusion | flops 159844992 | bytes 10435584 | tf_op jit(solution)/shard_map/hqk,khd->qhd/dot_general | solution.py:128
  492.7 25.4 %fusion.65 = f32[12,64,384]{2,1,0:T(8,128)} fusion(bf16[256,12,64]{0,2,1:T(8,128)(2,1)} %bitcast.341, f32[12,256,384]{2,1,0:T(8,128)} %fusion.314, f32[12,256,384]{2,1,0:T(8,128)} %copy-done.4, f32[12,256]{1,0:T(8,128)} %log_add_fusion), kind=kOutput, calls=%fused_computation.84 | convolution fusion | flops 159255936 | bytes 11022336 | tf_op jit(solution)/shard_map/hqk,qhd->khd/dot_general | solution.py:131
  530.8 25.3 %fusion.59 = f32[12,64,384]{2,1,0:T(8,128)} fusion(bf16[256,12,64]{0,2,1:T(8,128)(2,1)} %bitcast.339, f32[12,256,384]{2,1,0:T(8,128)} %fusion.312, f32[12,256,384]{2,1,0:T(8,128)} %copy-done.3, f32[12,256]{1,0:T(8,128)} %log_add_fusion.2), kind=kOutput, calls=%fused_computation.82 | convolution fusion | flops 159255936 | bytes 11022336 | tf_op jit(solution)/shard_map/hqk,qhd->khd/dot_general | solution.py:131
  574.4 9.5 scatter_fusion.5
  583.9 9.5 scatter_fusion.6
  593.4 9.5 scatter_fusion.7
  602.9 9.5 scatter_fusion.8
  612.4 9.7 scatter_fusion.9
  748.5 52.6 %reduce-scatter.31.cloned.1.call-done = f32[96,768]{1,0:T(8,128)} async-done(((f32[768,768]{1,0:T(8,128)}), f32[96,768]{1,0:T(8,128)}) %reduce-scatter.31.cloned.1.call-update) | async-done | bytes 294928
  802.9 69.9 %reduce-scatter.35.cloned.1.call-done = f32[96,768]{1,0:T(8,128)} async-done(((f32[768,768]{1,0:T(8,128)}), f32[96,768]{1,0:T(8,128)}) %reduce-scatter.35.cloned.1.call-update) | async-done | bytes 294928
  874.6 69.9 %reduce-scatter.33.cloned.1.call-done = f32[96,768]{1,0:T(8,128)} async-done(((f32[768,768]{1,0:T(8,128)}), f32[96,768]{1,0:T(8,128)}) %reduce-scatter.33.cloned.1.call-update) | async-done | bytes 294928
  946.4 165.3 %reduce-scatter.27.cloned.1.call-done = f32[96,3072]{1,0:T(8,128)} async-done(((f32[768,3072]{1,0:T(8,128)}), f32[96,3072]{1,0:T(8,128)}) %reduce-scatter.27.cloned.1.call-update) | async-done | bytes 1179664 | tf_op jit(solution)/shard_map/reduce_scatter | solution.py:593
  1113.8 163.7 %reduce-scatter.29.cloned.1.call-done = f32[384,768]{1,0:T(8,128)} async-done(((f32[3072,768]{1,0:T(8,128)}), f32[384,768]{1,0:T(8,128)}) %reduce-scatter.29.cloned.1.call-update) | async-done | bytes 1179664 | tf_op jit(solution)/shard_map/reduce_scatter | solution.py:595
  1279.9 28.7 %all-reduce.12 = (bf16[768]{0:T(1024)(128)(2,1)S(1)}, bf16[768]{0:T(1024)(128)(2,1)S(1)}, bf16[768]{0:T(1024)(128)(2,1)S(1)}, bf16[768]{0:T(1024)(128)(2,1)S(1)}...) all-reduce(f32[768]{0:T(1024)S(1)} %copy-done.178, ...), channel_id=3, replica_groups=mesh['seq'=8,'batch'=4] {'seq'}, use_global_device_ids=true, to_apply=%region_42.43.clone | all-reduce | flops 11520 | bytes 69120
  1309.5 17.5 %all-reduce.13 = (bf16[96]{0:T(256)(128)(2,1)S(1)}, bf16[96]{0:T(256)(128)(2,1)S(1)}, bf16[96]{0:T(256)(128)(2,1)S(1)}, bf16[96]{0:T(256)(128)(2,1)S(1)}, bf16[9...) all-reduce(bf16[96]{0:T(256)(128)(2,1)S(1)} %dynamic-slice.179, ...), channel_id=1, replica_groups=mesh['seq'=8,'batch'=4] {'batch'}, use_global_device_ids=true, to_apply=%region_43.44 | all-reduce | flops 2400 | bytes 9600 | tf_op jit(solution)/shard_map/psum | solution.py:627
  (917 shorter events, 534.4 us)
Async XLA Ops:
  7.2 730.6 %reduce-scatter.39.cloned.1.call-start = ((), (), s32[]{:S(2)}) async-start(), calls=%async_computation.19 | async-start | bytes 442368
  12.1 54.4 %collective-permute-start = (bf16[2,64,768]{2,1,0:T(8,128)(2,1)}, bf16[2,64,768]{2,1,0:T(8,128)(2,1)}, u32[]{:S(2)}, u32[]{:S(2)}) collective-permute-start(bf16[2,64,768]{2,1,0:T(8,128)(2,1)} %get-tuple-element.669), channel_id=1, source_target_pairs={{0,4},{4,8},{8,12},{12,16},{16,20},{20,24},{24,28},{1,5},{5,9},{9,... | collective-permute-start | bytes 589832 | tf_op jit(solution)/shard_map/ppermute | solution.py:27
  16.7 49.7 %collective-permute-start.1 = (bf16[2,64,768]{2,1,0:T(8,128)(2,1)}, bf16[2,64,768]{2,1,0:T(8,128)(2,1)}, u32[]{:S(2)}, u32[]{:S(2)}) collective-permute-start(bf16[2,64,768]{2,1,0:T(8,128)(2,1)} %get-tuple-element.670), channel_id=1, source_target_pairs={{4,0},{8,4},{12,8},{16,12},{20,16},{24,20},{28,24},{5,1},{9,5},{13... | collective-permute-start | bytes 589832 | tf_op jit(solution)/shard_map/ppermute | solution.py:29
  19.9 40.1 %collective-permute-start.10 = (bf16[2,64,768]{2,1,0:T(8,128)(2,1)}, bf16[2,64,768]{2,1,0:T(8,128)(2,1)}, u32[]{:S(2)}, u32[]{:S(2)}) collective-permute-start(bf16[2,64,768]{2,1,0:T(8,128)(2,1)} %get-tuple-element.671), channel_id=1, source_target_pairs={{0,4},{4,8},{8,12},{12,16},{16,20},{20,24},{24,28},{1,5},{5,9},{9,... | collective-permute-start | bytes 589832 | tf_op jit(solution)/shard_map/ppermute | solution.py:27
  24.7 35.3 %collective-permute-start.11 = (bf16[2,64,768]{2,1,0:T(8,128)(2,1)}, bf16[2,64,768]{2,1,0:T(8,128)(2,1)}, u32[]{:S(2)}, u32[]{:S(2)}) collective-permute-start(bf16[2,64,768]{2,1,0:T(8,128)(2,1)} %get-tuple-element.672), channel_id=1, source_target_pairs={{4,0},{8,4},{12,8},{16,12},{20,16},{24,20},{28,24},{5,1},{9,5},{13... | collective-permute-start | bytes 589832 | tf_op jit(solution)/shard_map/ppermute | solution.py:29
  76.8 99.5 %collective-permute-start.19 = (bf16[2,64,768]{2,1,0:T(8,128)(2,1)}, bf16[2,64,768]{2,1,0:T(8,128)(2,1)}, u32[]{:S(2)}, u32[]{:S(2)}) collective-permute-start(bf16[2,64,768]{2,1,0:T(8,128)(2,1)} %pad_maximum_fusion.11), channel_id=1, source_target_pairs={{16,0},{20,4},{24,8},{28,12},{17,1},{21,5},{25,9},{29,13},{18,2},{... | collective-permute-start | bytes 589832 | tf_op jit(solution)/shard_map/ppermute | solution.py:39
  78.1 97.3 %collective-permute-start.18 = (bf16[2,64,768]{2,1,0:T(8,128)(2,1)}, bf16[2,64,768]{2,1,0:T(8,128)(2,1)}, u32[]{:S(2)}, u32[]{:S(2)}) collective-permute-start(bf16[2,64,768]{2,1,0:T(8,128)(2,1)} %pad_maximum_fusion.11), channel_id=1, source_target_pairs={{12,0},{16,4},{20,8},{24,12},{28,16},{13,1},{17,5},{21,9},{25,13},... | collective-permute-start | bytes 589832 | tf_op jit(solution)/shard_map/ppermute | solution.py:39
  79.4 95.0 %collective-permute-start.17 = (bf16[2,64,768]{2,1,0:T(8,128)(2,1)}, bf16[2,64,768]{2,1,0:T(8,128)(2,1)}, u32[]{:S(2)}, u32[]{:S(2)}) collective-permute-start(bf16[2,64,768]{2,1,0:T(8,128)(2,1)} %pad_maximum_fusion.11), channel_id=1, source_target_pairs={{8,0},{12,4},{16,8},{20,12},{24,16},{28,20},{9,1},{13,5},{17,9},{2... | collective-permute-start | bytes 589832 | tf_op jit(solution)/shard_map/ppermute | solution.py:39
  81.4 35.2 %collective-permute-start.3 = (bf16[2,64,768]{2,1,0:T(8,128)(2,1)}, bf16[2,64,768]{2,1,0:T(8,128)(2,1)}, u32[]{:S(2)}, u32[]{:S(2)}) collective-permute-start(bf16[2,64,768]{2,1,0:T(8,128)(2,1)} %pad_maximum_fusion.10), channel_id=1, source_target_pairs={{0,12},{4,16},{8,20},{12,24},{16,28},{1,13},{5,17},{9,21},{13,25},... | collective-permute-start | bytes 589832 | tf_op jit(solution)/shard_map/ppermute | solution.py:39
  292.2 32.4 %collective-permute-start.30 = (bf16[2,64,768]{2,1,0:T(8,128)(2,1)}, bf16[2,64,768]{2,1,0:T(8,128)(2,1)S(1)}, u32[]{:S(2)}, u32[]{:S(2)}) collective-permute-start(bf16[2,64,768]{2,1,0:T(8,128)(2,1)} %get-tuple-element.640), channel_id=1, source_target_pairs={{4,0},{8,4},{12,8},{16,12},{20,16},{24,20},{28,24},{5,1},{9,5},{13... | collective-permute-start | bytes 589832 | tf_op jit(solution)/shard_map/ppermute | solution.py:39
  293.5 37.9 %collective-permute-start.37 = (bf16[2,64,768]{2,1,0:T(8,128)(2,1)}, bf16[2,64,768]{2,1,0:T(8,128)(2,1)}, u32[]{:S(2)}, u32[]{:S(2)}) collective-permute-start(bf16[2,64,768]{2,1,0:T(8,128)(2,1)} %get-tuple-element.641), channel_id=1, source_target_pairs={{0,16},{4,20},{8,24},{12,28},{1,17},{5,21},{9,25},{13,29},{2,18},{... | collective-permute-start | bytes 589832 | tf_op jit(solution)/shard_map/ppermute | solution.py:39
  300.4 32.3 %collective-permute-start.36 = (bf16[2,64,768]{2,1,0:T(8,128)(2,1)}, bf16[2,64,768]{2,1,0:T(8,128)(2,1)}, u32[]{:S(2)}, u32[]{:S(2)}) collective-permute-start(bf16[2,64,768]{2,1,0:T(8,128)(2,1)} %get-tuple-element.642), channel_id=1, source_target_pairs={{16,0},{20,4},{24,8},{28,12},{17,1},{21,5},{25,9},{29,13},{18,2},{... | collective-permute-start | bytes 589832 | tf_op jit(solution)/shard_map/ppermute | solution.py:39
  301.7 33.5 %collective-permute-start.35 = (bf16[2,64,768]{2,1,0:T(8,128)(2,1)}, bf16[2,64,768]{2,1,0:T(8,128)(2,1)}, u32[]{:S(2)}, u32[]{:S(2)}) collective-permute-start(bf16[2,64,768]{2,1,0:T(8,128)(2,1)} %get-tuple-element.643), channel_id=1, source_target_pairs={{0,12},{4,16},{8,20},{12,24},{16,28},{1,13},{5,17},{9,21},{13,25},... | collective-permute-start | bytes 589832 | tf_op jit(solution)/shard_map/ppermute | solution.py:39
  305.1 31.3 %collective-permute-start.34 = (bf16[2,64,768]{2,1,0:T(8,128)(2,1)}, bf16[2,64,768]{2,1,0:T(8,128)(2,1)}, u32[]{:S(2)}, u32[]{:S(2)}) collective-permute-start(bf16[2,64,768]{2,1,0:T(8,128)(2,1)} %get-tuple-element.644), channel_id=1, source_target_pairs={{12,0},{16,4},{20,8},{24,12},{28,16},{13,1},{17,5},{21,9},{25,13},... | collective-permute-start | bytes 589832 | tf_op jit(solution)/shard_map/ppermute | solution.py:39
  370.8 367.9 %reduce-scatter.37.cloned.1.call-start = ((), (), s32[]{:S(2)}) async-start(), calls=%async_computation.18 | async-start | bytes 442368
  374.2 369.4 %reduce-scatter.25.cloned.1.call-start = ((), (), s32[]{:S(2)}) async-start(), calls=%async_computation.12 | async-start | bytes 2654208 | tf_op jit(solution)/shard_map/reduce_scatter | solution.py:588
  377.2 368.0 %reduce-scatter.23.cloned.1.call-start = ((), (), s32[]{:S(2)}) async-start(), calls=%async_computation.11 | async-start | bytes 2654208 | tf_op jit(solution)/shard_map/reduce_scatter | solution.py:586
  407.7 339.2 %reduce-scatter.21.cloned.1.call-start = ((), (), s32[]{:S(2)}) async-start(), calls=%async_computation.10 | async-start | bytes 2654208 | tf_op jit(solution)/shard_map/reduce_scatter | solution.py:584
  415.1 386.1 %reduce-scatter.31.cloned.1.call-start = ((), (), s32[]{:S(2)}) async-start(), calls=%async_computation.15 | async-start | bytes 2654208
  488.0 384.8 %reduce-scatter.35.cloned.1.call-start = ((), (), s32[]{:S(2)}) async-start(), calls=%async_computation.17 | async-start | bytes 2654208
  700.0 244.6 %reduce-scatter.33.cloned.1.call-start = ((), (), s32[]{:S(2)}) async-start(), calls=%async_computation.16 | async-start | bytes 2654208
  705.7 406.0 %reduce-scatter.27.cloned.1.call-start = ((), (), s32[]{:S(2)}) async-start(), calls=%async_computation.13 | async-start | bytes 10616832 | tf_op jit(solution)/shard_map/reduce_scatter | solution.py:593
  714.3 563.2 %reduce-scatter.29.cloned.1.call-start = ((), (), s32[]{:S(2)}) async-start(), calls=%async_computation.14 | async-start | bytes 10616832 | tf_op jit(solution)/shard_map/reduce_scatter | solution.py:595
  723.6 616.2 %all-reduce.17.cloned.1.call-start = ((), (), s32[]{:S(2)}) async-start(), calls=%async_computation.20 | async-start | bytes 4423680 | tf_op jit(solution)/shard_map/psum | solution.py:626
  (274 other events, 5765.7 us)
Sparse Core Ops, SparseCore 0:
  371.0 70.0 reduce-scatter.38
  444.4 60.6 reduce-scatter.36
  508.6 68.4 reduce-scatter.24
  580.4 69.0 reduce-scatter.22
  652.8 76.8 reduce-scatter.20
  733.1 68.0 reduce-scatter.30
  804.6 68.1 reduce-scatter.34
  876.3 68.1 reduce-scatter.32
  948.1 163.4 reduce-scatter.26
  1115.1 162.4 reduce-scatter.28
  1282.2 53.7 all-reduce.16
where the time goes:
time: 1370 us; the launch traced here: 1360 us
  waiting for transfers between devices  565 us (41%)
  matrix products  307 us (22%)
  other arithmetic  174 us (13%)
  local copies, waits for them, and re-layouts  134 us (10%)
  starting transfers between devices  114 us (8%)
  blocking collectives  46.2 us (3%)
  between operations  19.5 us (1%)
    unnamed x16, waiting for transfers between devices  193 us
    reduce_scatter x1, waiting for transfers between devices, on_device(): lax.psum_scatter(grad_expand_weight, 'seq', scatter_dimension=0, tiled=True)  165 us
    reduce_scatter x1, waiting for transfers between devices, on_device(): lax.psum_scatter(grad_reduce_weight, 'seq', scatter_dimension=0, tiled=True)  164 us
    ppermute x36, starting transfers between devices, from_behind(): return lax.ppermute(shard, axis, pairs)  101 us
    scatter-add x10, other arithmetic, backward_part(): local_grads.at[:, tap_start:tap_start + row_count:STRIDE]  79.7 us
    dot_general x4, matrix products, attend_backward(): jnp.einsum('hqk,qhd->khd', grad_raw, query_heads, preferred_element_type=...  77.3 us
    dot_general x4, matrix products, attend_backward(): jnp.einsum('hqk,khd->qhd', grad_raw, key_heads, preferred_element_type=jn...  76.1 us
    ppermute x36, waiting for transfers between devices, from_behind(): return lax.ppermute(shard, axis, pairs)  43.4 us
  transfers between devices with their start and end apart: 51, of which 14 were waited for; matrix products, arithmetic and copies ran while one was open for 34% of the time, Pallas kernels for 0%

commit v1 on v0

v1 whole, which is shorter than its diff:
```python
import functools
import math

import jax
import jax.numpy as jnp
from jax import lax
from jax.experimental import pallas as pl
from jax.experimental.pallas import tpu as pltpu
from jax.sharding import PartitionSpec as P

HEADS = 12
HD = 64
WIN = 128
PWIN = 512
KER = 5
STRIDE = 4
HALF = WIN // 2
REACH = PWIN // 2
NEGATIVE = -1e30
SCALE = 1.0 / math.sqrt(HD)
EPSILON = 1e-05
LANES = 128
TILE = 128
ROWS = 128
CHUNK = 256
VMEM_BYTES = 58 * 1024 * 1024
F32 = jnp.float32
BF16 = jnp.bfloat16


def nn(left, right):
    return jnp.dot(left, right, preferred_element_type=F32)


def nt(left, right):
    return lax.dot_general(left, right, (((1,), (1,)), ((), ())), preferred_element_type=F32)


def tn(left, right):
    return lax.dot_general(left, right, (((0,), (0,)), ((), ())), preferred_element_type=F32)


def column_sum(block):
    return jnp.sum(block.astype(F32), axis=0, keepdims=True)


def call(body, grid, scalars, inputs, outputs, scratch=(), flops=0, moved=0, exps=0):
    def spec(block, index):
        if block is None:
            return pl.BlockSpec(memory_space=pltpu.VMEM)
        return pl.BlockSpec(block, index)

    return pl.pallas_call(
        body,
        grid_spec=pltpu.PrefetchScalarGridSpec(
            num_scalar_prefetch=len(scalars),
            grid=grid,
            in_specs=[spec(block, index) for _, block, index in inputs],
            out_specs=[spec(block, index) for _, _, block, index in outputs],
            scratch_shapes=list(scratch),
        ),
        out_shape=[jax.ShapeDtypeStruct(shape, dtype) for shape, dtype, _, _ in outputs],
        compiler_params=pltpu.CompilerParams(
            dimension_semantics=("arbitrary",) * len(grid), vmem_limit_bytes=VMEM_BYTES
        ),
        cost_estimate=pl.CostEstimate(flops=flops, bytes_accessed=moved, transcendentals=exps),
    )(*scalars, *[array for array, _, _ in inputs])


def whole(array):
    zeros = (0,) * array.ndim
    return (array, array.shape, lambda *_: zeros)


def by_doc(array):
    zeros = (0,) * (array.ndim - 1)
    return (array, (1,) + array.shape[1:], lambda doc, *_: (doc,) + zeros)


def out_doc(shape, dtype):
    zeros = (0,) * (len(shape) - 1)
    return (shape, dtype, (1,) + tuple(shape[1:]), lambda doc, *_: (doc,) + zeros)


def out_whole(shape, dtype):
    zeros = (0,) * len(shape)
    return (shape, dtype, shape, lambda *_: zeros)


def stack_heads(block):
    lane = lax.broadcasted_iota(jnp.int32, block.shape, 1)
    zero = jnp.zeros_like(block)
    return jnp.concatenate(
        [jnp.where(lane < HD, block, zero), jnp.where(lane < HD, zero, block)], axis=0
    )


def unstack(block):
    joined = jnp.concatenate([block[:HD, :TILE], block[HD:, TILE:]], axis=0)
    return joined.T


def positions(shape, dim):
    return lax.broadcasted_iota(jnp.int32, shape, dim)


def project_body(place, x, left, right, wq, bq, wk, wv, bv, ck, cv, bcv, q, kx, vx, pooled, rows):
    doc = pl.program_id(0)
    offset, length = place[0], place[1 + doc]
    own = x[0]
    q[0] = (nn(own, wq[...]) + bq[...]).astype(BF16)
    extended = jnp.concatenate([left[0], own, right[0]], axis=0)
    spot = offset - HALF + positions((extended.shape[0], 1), 0)
    valid = (spot >= 0) & (spot < length)
    count = pooled.shape[2]
    for which, (weight, bias, taps, out) in enumerate(((wk, None, ck, kx), (wv, bv, cv, vx))):
        value = nn(extended, weight[...])
        if bias is not None:
            value = value + bias[...]
        value = value.astype(BF16)
        out[0] = value
        masked = jnp.where(valid, value.astype(F32), 0.0)
        for group in range(value.shape[1] // LANES):
            lanes = slice(group * LANES, (group + 1) * LANES)
            rows[group] = masked[:, lanes]
            total = jnp.zeros((count, LANES), F32)
            for tap in range(KER):
                start = HALF - KER // 2 + tap
                read = rows[group, pl.ds(start, count, stride=STRIDE), :]
                total = total + read * taps[tap : tap + 1, lanes]
            if which == 1:
                total = total + bcv[:, lanes]
            pooled[0, which, :, lanes] = total.astype(BF16)


def project(place, x, left, right, wq, bq, wk, wv, bv, ck, cv, bcv):
    docs, rows, width = x.shape
    extended = rows + WIN
    return call(
        project_body,
        (docs,),
        (place,),
        [by_doc(x), by_doc(left), by_doc(right)]
        + [whole(a) for a in (wq, bq, wk, wv, bv, ck, cv, bcv)],
        [
            out_doc((docs, rows, width), BF16),
            out_doc((docs, extended, width), BF16),
            out_doc((docs, extended, width), BF16),
            out_doc((docs, 2, rows // STRIDE, width), BF16),
        ],
        [pltpu.VMEM((width // LANES, extended, LANES), F32)],
        flops=2 * docs * (rows + 2 * extended) * width * width,
        moved=10**7,
    )


def local_bias(tile, offset, length):
    shape = (TILE + WIN, TILE)
    key = positions(shape, 0)
    query = positions(shape, 1)
    spot = offset + tile * TILE - HALF + key
    allowed = (
        (key >= query) & (key < query + WIN) & (spot >= 0) & (spot < length)
    ) | (key == query + HALF)
    return jnp.where(allowed, 0.0, NEGATIVE)


def softmax_columns(scores):
    top = jnp.max(scores, axis=0, keepdims=True)
    grown = jnp.exp(scores - top)
    return grown * (1.0 / jnp.sum(grown, axis=0, keepdims=True))


def local_forward_body(
    place, q, kx, vx, x, wo, bo, wpq, bpq, mix, probs, middle, middle_low, q2
):
    doc = pl.program_id(0)
    offset, length = place[0], place[1 + doc]
    span = TILE + WIN
    for tile in range(q.shape[1] // TILE):
        half_bias = local_bias(tile, offset, length)
        bias = jnp.concatenate([half_bias, half_bias], axis=1)
        first = tile * TILE
        for pair in range(q.shape[2] // LANES):
            lanes = slice(pair * LANES, (pair + 1) * LANES)
            queries = stack_heads(q[0, first : first + TILE, lanes])
            scores = nt(kx[0, first : first + span, lanes], queries) * SCALE + bias
            chance = softmax_columns(scores)
            probs[0, pair, tile] = chance
            turned = vx[0, first : first + span, lanes].T
            mixed = nn(turned, chance.astype(BF16))
            mix[0, first : first + TILE, lanes] = unstack(mixed).astype(BF16)
    total = x[0].astype(F32) + (nn(mix[0], wo[...]) + bo[...])
    middle[0] = total
    low = total.astype(BF16)
    middle_low[0] = low
    q2[0] = (nn(low, wpq[...]) + bpq[...]).astype(BF16)


def local_forward(place, q, kx, vx, x, wo, bo, wpq, bpq):
    docs, rows, width = q.shape
    pairs, tiles, span = width // LANES, rows // TILE, TILE + WIN
    return call(
        local_forward_body,
        (docs,),
        (place,),
        [by_doc(a) for a in (q, kx, vx, x)] + [whole(a) for a in (wo, bo, wpq, bpq)],
        [
            out_doc((docs, rows, width), BF16),
            out_doc((docs, pairs, tiles, span, 2 * TILE), F32),
            out_doc((docs, rows, width), F32),
            out_doc((docs, rows, width), BF16),
            out_doc((docs, rows, width), BF16),
        ],
        flops=docs * rows * width * (4 * width + 4 * 2 * span),
        moved=2 * 10**7,
        exps=docs * rows * HEADS * span,
    )


def attention_back(keys, values, queries, grads, chance):
    stacked_grads = stack_heads(grads)
    stacked_queries = stack_heads(queries)
    grad_chance = nt(values, stacked_grads)
    dots = jnp.sum(chance * grad_chance, axis=0, keepdims=True)
    grad_raw = (chance * (grad_chance - dots) * SCALE).astype(BF16)
    grad_keys = nn(grad_raw, stacked_queries)
    grad_values = nn(chance.astype(BF16), stacked_grads)
    grad_queries = unstack(nn(keys.T, grad_raw))
    return grad_queries, grad_keys, grad_values


def local_backward_body(
    place, q, kx, vx, probs, gq2, gsum, wpq, wo,
    dq, own, low_left, low_right, gmid, gfirst, vec, gmix, dk, dv,
):
    doc = pl.program_id(0)
    total = gsum[0] + nt(gq2[0], wpq[...])
    gmid[0] = total
    low = total.astype(BF16)
    gfirst[0] = low
    gmix[...] = nt(low, wo[...]).astype(BF16)

    @pl.when(doc == 0)
    def _():
        vec[...] = jnp.zeros_like(vec)

    vec[0:1] += column_sum(gq2[0])
    vec[1:2] += column_sum(low)
    rows = q.shape[1]
    span = TILE + WIN
    dk[...] = jnp.zeros_like(dk)
    dv[...] = jnp.zeros_like(dv)
    for tile in range(rows // TILE):
        first = tile * TILE
        for pair in range(q.shape[2] // LANES):
            lanes = slice(pair * LANES, (pair + 1) * LANES)
            grad_q, grad_k, grad_v = attention_back(
                kx[0, first : first + span, lanes],
                vx[0, first : first + span, lanes],
                q[0, first : first + TILE, lanes],
                gmix[first : first + TILE, lanes],
                probs[0, pair, tile],
            )
            dq[0, first : first + TILE, lanes] = grad_q.astype(BF16)
            dk[first : first + span, lanes] += grad_k
            dv[first : first + span, lanes] += grad_v
    for which, part in enumerate((dk, dv)):
        own[0, which] = part[HALF : HALF + rows]
        low_left[0, which] = part[:HALF].astype(BF16)
        low_right[0, which] = part[HALF + rows :].astype(BF16)


def local_backward(place, q, kx, vx, probs, gq2, gsum, wpq, wo):
    docs, rows, width = q.shape
    span = TILE + WIN
    return call(
        local_backward_body,
        (docs,),
        (place,),
        [by_doc(a) for a in (q, kx, vx, probs, gq2, gsum)] + [whole(wpq), whole(wo)],
        [
            out_doc((docs, rows, width), BF16),
            out_doc((docs, 2, rows, width), F32),
            out_doc((docs, 2, HALF, width), BF16),
            out_doc((docs, 2, HALF, width), BF16),
            out_doc((docs, rows, width), F32),
            out_doc((docs, rows, width), BF16),
            out_whole((8, width), F32),
        ],
        [
            pltpu.VMEM((rows, width), BF16),
            pltpu.VMEM((rows + WIN, width), F32),
            pltpu.VMEM((rows + WIN, width), F32),
        ],
        flops=docs * rows * width * (4 * width + 8 * 2 * span),
        moved=2 * 10**7,
    )


def pooled_forward_body(place, slots, *refs, pieces):
    key_pieces = refs[:pieces]
    value_pieces = refs[pieces : 2 * pieces]
    q2, middle, wpo, bpo, keys, values, probs, mix, summed, bias = refs[2 * pieces :]
    doc, pair = pl.program_id(0), pl.program_id(1)
    offset, length, base = place[0], place[1 + doc], place[1 + pl.num_programs(0)]
    tiles = q2.shape[1] // TILE
    count = keys.shape[1]

    @pl.when(pair == 0)
    def _():
        for where, group, out in ((0, key_pieces, keys), (1, value_pieces, values)):
            at = 0
            for piece in group:
                size = piece.shape[2]
                for block in range(piece.shape[0]):
                    spot = pl.multiple_of(slots[where, at] * size, size)
                    out[0, pl.ds(spot, size), :] = piece[block, 0]
                    at += 1
        for tile in range(tiles):
            shape = (count, TILE)
            spot = base + positions(shape, 0)
            centre = offset // STRIDE + (tile * TILE + positions(shape, 1)) // STRIDE
            allowed = (
                (spot >= centre - REACH)
                & (spot < centre + REACH)
                & (spot >= 0)
                & (spot * STRIDE < length)
            ) | (spot == centre)
            bias[tile] = jnp.where(allowed, 0.0, NEGATIVE)

    lanes = pl.ds(pl.multiple_of(pair * LANES, LANES), LANES)
    pair_keys = keys[0, :, lanes]
    turned = values[0, :, lanes].T
    for tile in range(tiles):
        first = tile * TILE
        queries = stack_heads(q2[0, first : first + TILE, :])
        half_bias = bias[tile]
        scores = nt(pair_keys, queries) * SCALE + jnp.concatenate([half_bias, half_bias], axis=1)
        chance = softmax_columns(scores)
        probs[0, 0, tile] = chance
        mixed = nn(turned, chance.astype(BF16))
        mix[0, first : first + TILE, lanes] = unstack(mixed).astype(BF16)

    @pl.when(pair == pl.num_programs(1) - 1)
    def _():
        summed[0] = middle[0] + (nn(mix[0], wpo[...]) + bpo[...])


def pooled_forward(place, slots, key_pieces, value_pieces, q2, middle, wpo, bpo):
    docs, rows, width = q2.shape
    pairs, tiles = width // LANES, rows // TILE
    size = key_pieces[0].shape[2]
    count = size * slots.shape[1]

    def piece(array):
        return (array, (array.shape[0], 1, size, width), lambda doc, *_: (0, doc, 0, 0))

    return call(
        functools.partial(pooled_forward_body, pieces=len(key_pieces)),
        (docs, pairs),
        (place, slots),
        [piece(a) for a in key_pieces + value_pieces]
        + [
            (q2, (1, rows, LANES), lambda doc, pair, *_: (doc, 0, pair)),
            by_doc(middle),
            whole(wpo),
            whole(bpo),
        ],
        [
            out_doc((docs, count, width), BF16),
            out_doc((docs, count, width), BF16),
            (
                (docs, pairs, tiles, count, 2 * TILE),
                F32,
                (1, 1, tiles, count, 2 * TILE),
                lambda doc, pair, *_: (doc, pair, 0, 0, 0),
            ),
            out_doc((docs, rows, width), BF16),
            out_doc((docs, rows, width), F32),
        ],
        [pltpu.VMEM((tiles, count, TILE), F32)],
        flops=docs * rows * width * (2 * width + 4 * 2 * count),
        moved=3 * 10**7,
        exps=docs * rows * HEADS * count,
    )


def pooled_backward_body(places, q2, keys, values, probs, grads, dq, dk, dv):
    size = dk.shape[2]
    grad_keys = None
    for tile in range(q2.shape[1] // TILE):
        first = tile * TILE
        grad_q, grad_k, grad_v = attention_back(
            keys[0], values[0], q2[0, first : first + TILE], grads[0, first : first + TILE],
            probs[0, 0, tile],
        )
        dq[0, first : first + TILE] = grad_q.astype(BF16)
        if grad_keys is None:
            grad_keys, grad_values = grad_k, grad_v
        else:
            grad_keys, grad_values = grad_keys + grad_k, grad_values + grad_v
    for block in range(dk.shape[0]):
        part = slice(block * size, (block + 1) * size)
        dk[places[0, block], 0] = grad_keys[part].astype(BF16)
        dv[places[1, block], 0] = grad_values[part].astype(BF16)


def pooled_backward(places, q2, keys, values, probs, grads, size):
    docs, rows, width = q2.shape
    count = keys.shape[1]
    blocks = count // size
    tiles = rows // TILE

    def lanes_of(array):
        return (array, (1, array.shape[1], LANES), lambda doc, pair, *_: (doc, 0, pair))

    spread = (
        (blocks, docs, size, width),
        BF16,
        (blocks, 1, size, LANES),
        lambda doc, pair, *_: (0, doc, 0, pair),
    )
    return call(
        pooled_backward_body,
        (docs, width // LANES),
        (places,),
        [
            lanes_of(q2),
            lanes_of(keys),
            lanes_of(values),
            (
                probs,
                (1, 1, tiles, count, 2 * TILE),
                lambda doc, pair, *_: (doc, pair, 0, 0, 0),
            ),
            lanes_of(grads),
        ],
        [
            ((docs, rows, width), BF16, (1, rows, LANES), lambda doc, pair, *_: (doc, 0, pair)),
            spread,
            spread,
        ],
        flops=docs * rows * width * 8 * 2 * count,
        moved=2 * 10**7,
    )


def feed_body(
    place, summed, cotangent, we, be, wr, br, ng, ns, fg, fs, wpo,
    outputs, normed_low, hidden, grad_branch, grad_pre, grad_summed, grad_second, grad_mix,
    vec, vec_wide,
    normed, slope, work, unit,
):
    docs, rows = cotangent.shape[0], cotangent.shape[1]
    width = summed.shape[2]
    wide = we.shape[1]
    steps = rows // ROWS
    blocks = [(doc, step * ROWS, doc * rows + step * ROWS) for doc in range(docs) for step in range(steps)]

    def normal(value):
        centred = value - jnp.mean(value, axis=-1, keepdims=True)
        scale = lax.rsqrt(jnp.mean(centred * centred, axis=-1, keepdims=True) + EPSILON)
        return centred * scale, scale

    scales = []
    for doc, start, row in blocks:
        norm, scale = normal(summed[doc, start : start + ROWS])
        scales.append(scale)
        unit[row : row + ROWS] = norm
        full = norm * ng[...] + ns[...]
        normed[row : row + ROWS] = full
        normed_low[row : row + ROWS] = full.astype(BF16)

    def expand(index, _):
        part = pl.ds(pl.multiple_of(index * CHUNK, CHUNK), CHUNK)
        pre = nn(normed_low[...], we[:, part]) + be[:, part]
        cdf = 0.5 * (1.0 + lax.erf(pre * math.sqrt(0.5)))
        hidden[:, part] = (pre * cdf).astype(BF16)
        slope[:, part] = cdf + pre * (jnp.exp(pre * pre * -0.5) * (1.0 / math.sqrt(2.0 * math.pi)))
        return 0

    lax.fori_loop(0, wide // CHUNK, expand, 0)

    for start in range(0, width, CHUNK):
        part = slice(start, start + CHUNK)
        work[:, part] = normed[:, part] + (nn(hidden[...], wr[:, part]) + br[:, part])

    sums = [jnp.zeros((1, width), F32) for _ in range(6)]
    for doc, start, row in blocks:
        norm, scale = normal(work[row : row + ROWS])
        spot = place[0] + start + positions((ROWS, 1), 0)
        valid = (spot < place[1 + doc]).astype(F32)
        outputs[doc, start : start + ROWS] = (valid * (norm * fg[...] + fs[...])).astype(BF16)
        error = valid * cotangent[doc, start : start + ROWS].astype(F32)
        sums[0] += column_sum(error * norm)
        sums[1] += column_sum(error)
        scaled = error * fg[...]
        rest = (
            scaled
            - jnp.mean(scaled, axis=-1, keepdims=True)
            - norm * jnp.mean(scaled * norm, axis=-1, keepdims=True)
        ) * scale
        work[row : row + ROWS] = rest
        low = rest.astype(BF16)
        grad_branch[row : row + ROWS] = low
        sums[2] += column_sum(low)

    def reduce(index, _):
        part = pl.ds(pl.multiple_of(index * CHUNK, CHUNK), CHUNK)
        low = (nt(grad_branch[...], wr[part, :]) * slope[:, part]).astype(BF16)
        grad_pre[:, part] = low
        vec_wide[:, part] = column_sum(low)
        return 0

    lax.fori_loop(0, wide // CHUNK, reduce, 0)

    for start in range(0, width, CHUNK):
        part = slice(start, start + CHUNK)
        work[:, part] += nt(grad_pre[...], we[part, :])

    for (doc, start, row), scale in zip(blocks, scales):
        error = work[row : row + ROWS]
        norm = unit[row : row + ROWS]
        sums[3] += column_sum(error * norm)
        sums[4] += column_sum(error)
        scaled = error * ng[...]
        grad = (
            scaled
            - jnp.mean(scaled, axis=-1, keepdims=True)
            - norm * jnp.mean(scaled * norm, axis=-1, keepdims=True)
        ) * scale
        grad_summed[doc, start : start + ROWS] = grad
        low = grad.astype(BF16)
        grad_second[row : row + ROWS] = low
        sums[5] += column_sum(low)
        grad_mix[doc, start : start + ROWS] = nt(low, wpo[...]).astype(BF16)
    for index, value in enumerate(sums):
        vec[index : index + 1] = value
    vec[6:8] = jnp.zeros((2, width), F32)


def feed(place, summed, cotangent, we, be, wr, br, ng, ns, fg, fs, wpo):
    docs, rows, width = summed.shape
    wide = we.shape[1]
    tokens = docs * rows
    return call(
        feed_body,
        (1,),
        (place,),
        [whole(a) for a in (summed, cotangent, we, be, wr, br, ng, ns, fg, fs, wpo)],
        [
            out_whole((docs, rows, width), BF16),
            out_whole((tokens, width), BF16),
            out_whole((tokens, wide), BF16),
            out_whole((tokens, width), BF16),
            out_whole((tokens, wide), BF16),
            out_whole((docs, rows, width), F32),
            out_whole((tokens, width), BF16),
            out_whole((docs, rows, width), BF16),
            out_whole((8, width), F32),
            out_whole((1, wide), F32),
        ],
        [
            pltpu.VMEM((tokens, width), F32),
            pltpu.VMEM((tokens, wide), F32),
            pltpu.VMEM((tokens, width), F32),
            pltpu.VMEM((tokens, width), F32),
        ],
        flops=2 * tokens * width * (4 * wide + width),
        moved=3 * 10**7,
        exps=2 * tokens * wide,
    )


def input_body(
    place, own, from_left, from_right, gk_kept, gk_came, gv_kept, gv_came, gk_next, gv_next,
    kx, vx, ck, cv, dq, gmid, wq, wk, wv,
    gk, gv, dx, vec, rows_in, pooled, total,
):
    doc = pl.program_id(0)
    offset, length = place[0], place[1 + doc]
    rows = gk.shape[1]
    count = pooled.shape[0] - 8
    width = gk.shape[2]
    spot = offset - HALF + positions((rows + WIN, 1), 0)
    valid = (spot >= 0) & (spot < length)

    @pl.when(doc == 0)
    def _():
        vec[...] = jnp.zeros_like(vec)

    for which, (kept, came, after, ext, taps, out, row) in enumerate(
        (
            (gk_kept, gk_came, gk_next, kx, ck, gk, 0),
            (gv_kept, gv_came, gv_next, vx, cv, gv, KER),
        )
    ):
        pooled[:count] = kept[0].astype(F32) + came[0].astype(F32)
        pooled[count:] = jnp.broadcast_to(after[0].astype(F32), (8, width))
        masked = jnp.where(valid, ext[0].astype(F32), 0.0)
        for group in range(width // LANES):
            lanes = slice(group * LANES, (group + 1) * LANES)
            grown = pooled[:count, lanes]
            shifted = pooled[1 : count + 1, lanes]
            rows_in[group] = masked[:, lanes]
            for tap in range(KER):
                start = HALF - KER // 2 + tap
                read = rows_in[group, pl.ds(start, count, stride=STRIDE), :]
                vec[row + tap : row + tap + 1, lanes] += column_sum(grown * read)
            if which == 1:
                vec[2 * KER : 2 * KER + 1, lanes] += column_sum(grown)
            total[group] = own[0, which, :, lanes]
            total[group, :HALF] += from_left[0, which, :, lanes].astype(F32)
            total[group, rows - HALF :] += from_right[0, which, :, lanes].astype(F32)
            for phase, terms in enumerate(
                (
                    ((2, grown),),
                    ((3, grown),),
                    ((4, grown), (0, shifted)),
                    ((1, shifted),),
                )
            ):
                part = pl.ds(phase, count, stride=STRIDE)
                added = None
                for tap, values in terms:
                    term = values * taps[tap : tap + 1, lanes]
                    added = term if added is None else added + term
                inside = offset + phase + STRIDE * positions((count, 1), 0) < length
                total[group, part, :] = total[group, part, :] + jnp.where(inside, added, 0.0)
            out[0, :, lanes] = total[group].astype(BF16)
    vec[11:12] += column_sum(dq[0])
    vec[12:13] += column_sum(gv[0])
    dx[0] = (
        gmid[0] + nt(dq[0], wq[...]) + nt(gk[0], wk[...]) + nt(gv[0], wv[...])
    ).astype(BF16)


def input_gradients(
    place, own, from_left, from_right, pooled_grads, next_grads, kx, vx, ck, cv, dq, gmid, wq, wk, wv
):
    docs, rows, width = dq.shape
    return call(
        input_body,
        (docs,),
        (place,),
        [
            by_doc(a)
            for a in (own, from_left, from_right, *pooled_grads, *next_grads, kx, vx)
        ]
        + [whole(ck), whole(cv), by_doc(dq), by_doc(gmid), whole(wq), whole(wk), whole(wv)],
        [
            out_doc((docs, rows, width), BF16),
            out_doc((docs, rows, width), BF16),
            out_doc((docs, rows, width), BF16),
            out_whole((16, width), F32),
        ],
        [
            pltpu.VMEM((width // LANES, rows + WIN, LANES), F32),
            pltpu.VMEM((rows // STRIDE + 8, width), F32),
            pltpu.VMEM((width // LANES, rows, LANES), F32),
        ],
        flops=2 * docs * rows * width * 3 * width,
        moved=2 * 10**7,
    )


def scatter_body(bits, *refs, widths, splits):
    count = len(widths)
    lefts, rights, out = refs[: count * 2 : 2], refs[1 : count * 2 : 2], refs[count * 2]
    base = 0
    for left, right, (tall, wide) in zip(lefts, rights, widths):
        half = wide // 2
        piece = 384
        for block in range(0, tall, 768):
            turned = left[:, block : block + 768].T
            for part in range(half // piece):
                start = pl.multiple_of(bits[0] * half + part * piece, LANES)
                product = nn(turned, right[:, pl.ds(start, piece)])
                size = tall // splits // 2
                for step in range(768 // size):
                    row = block + step * size
                    owner, side = row // (2 * size), (row // size) % 2
                    index = [side ^ bits[1]]
                    for level in range(splits.bit_length() - 1):
                        index.append(((owner >> level) & 1) ^ bits[2 + level])
                    target = base + part * size
                    out[(*index, slice(target, target + size), slice(None))] = product[
                        step * size : (step + 1) * size
                    ].astype(BF16)
        base += (half // piece) * (tall // splits // 2)


def scatter_products(bits, pairs, splits):
    levels = splits.bit_length() - 1
    rows = sum(
        (right.shape[1] // 768) * (left.shape[1] // splits // 2) for left, right in pairs
    )
    shape = (2,) * (levels + 1) + (rows, 384)
    operands = [array for pair in pairs for array in pair]
    widths = tuple((left.shape[1], right.shape[1]) for left, right in pairs)
    (out,) = call(
        functools.partial(scatter_body, widths=widths, splits=splits),
        (1,),
        (bits,),
        [whole(a) for a in operands],
        [out_whole(shape, BF16)],
        flops=sum(left.shape[0] * tall * wide for (left, _), (tall, wide) in zip(pairs, widths)),
        moved=2 * sum(a.size for a in operands) + 2 * math.prod(shape),
    )
    return out


def swap(value, axis, bit):
    count = lax.axis_size(axis)
    return lax.ppermute(value, axis, [(i, i ^ (1 << bit)) for i in range(count)])


def shift(value, axis, by):
    count = lax.axis_size(axis)
    pairs = [(i, i + by) for i in range(count) if 0 <= i + by < count]
    return lax.ppermute(value, axis, pairs)


def reduce_products(bits_of, pairs, levels):
    send = scatter_products(bits_of(1), pairs, 1 << levels)
    came = swap(send, "batch", 0)
    kept = scatter_products(bits_of(0), pairs, 1 << levels)
    for axis, bit in [("batch", 1)] + [("seq", level) for level in range(levels)]:
        low = kept[1] + came[1] if came is not None else kept[1]
        kept = kept[0].astype(F32) + came[0].astype(F32)
        came = swap(low.astype(BF16), axis, bit)
    return kept + came.astype(F32)


def gather_quarters(quarter):
    low = quarter.astype(BF16)
    mine = lax.axis_index("batch")
    other = swap(low, "batch", 1)
    upper = (mine & 2) > 0
    both = jnp.stack([jnp.where(upper, other, low), jnp.where(upper, low, other)])
    across = swap(both, "batch", 0)
    odd = (mine & 1) > 0
    return jnp.stack([jnp.where(odd, across, both), jnp.where(odd, both, across)], axis=1).astype(F32)


def cut_square(quarters, start, size):
    block = quarters[:, :, start : start + size]
    return block.transpose(0, 2, 1, 3).reshape(2 * size, 768)


def cut_wide(quarters, start, size):
    block = quarters[:, :, start : start + 4 * size].reshape(2, 2, 4, size, 384)
    return block.transpose(0, 3, 1, 2, 4).reshape(2 * size, 3072)


def device_step(
    inputs, lengths, cotangent,
    local_query, local_query_bias, local_key, local_value, local_value_bias,
    local_output, local_output_bias, pooled_query, pooled_query_bias,
    pooled_output, pooled_output_bias, conv_key, conv_value, conv_value_bias,
    norm_gain, norm_shift, expand_weight, expand_bias, reduce_weight, reduce_bias,
    final_gain, final_shift,
):
    docs, rows, width = inputs.shape
    devices = lax.axis_size("seq")
    me = lax.axis_index("seq")
    half = lax.axis_index("batch")
    levels = devices.bit_length() - 1
    size = rows // STRIDE
    offset = me * rows
    reach = -(-REACH // size)
    gathered = devices <= 2 * reach
    base = jnp.where(gathered, 0, offset // STRIDE - reach * size)
    place = jnp.concatenate([offset[None], lengths, base[None]]).astype(jnp.int32)

    def line(vector):
        return vector[None]

    taps_key, taps_value = conv_key.T, conv_value.T

    left = shift(inputs[:, rows - HALF :], "seq", 1)
    right = shift(inputs[:, :HALF], "seq", -1)
    q, kx, vx, pooled = project(
        place, inputs, left, right, local_query, line(local_query_bias), local_key, local_value,
        line(local_value_bias), taps_key, taps_value, line(conv_value_bias),
    )

    own = [pooled[:, which][None] for which in range(2)]
    if gathered:
        orders = ([2, 1, 0], [0, 2, 1]) if levels == 3 else (list(range(levels)),) * 2
        pieces, slots = [], []
        for which in range(2):
            have, relative, got = own[which], [0], [own[which]]
            for bit in orders[which]:
                came = swap(have, "seq", bit)
                got.append(came)
                relative = relative + [r ^ (1 << bit) for r in relative]
                if bit != orders[which][-1]:
                    have = jnp.concatenate([have, came])
            pieces.append(got)
            slots.append(me ^ jnp.array(relative, jnp.int32))
        slots = jnp.stack(slots)
    else:
        pieces = [
            [own[which]]
            + [
                shift(own[which], "seq", sign * distance)
                for distance in range(1, reach + 1)
                for sign in (1, -1)
            ]
            for which in range(2)
        ]
        spots = [reach] + [
            reach - sign * distance for distance in range(1, reach + 1) for sign in (1, -1)
        ]
        slots = jnp.array([spots, spots], jnp.int32)

    mix_one, probs_one, middle, middle_low, q2 = local_forward(
        place, q, kx, vx, inputs, local_output, line(local_output_bias),
        pooled_query, line(pooled_query_bias),
    )
    keys, values, probs_two, mix_two, summed = pooled_forward(
        place, slots, pieces[0], pieces[1], q2, middle, pooled_output, line(pooled_output_bias)
    )
    (
        outputs, normed_low, hidden, grad_branch, grad_pre, grad_summed, grad_second, grad_mix_two,
        vec_feed, vec_wide,
    ) = feed(
        place, summed, cotangent, expand_weight, line(expand_bias), reduce_weight,
        line(reduce_bias), line(norm_gain), line(norm_shift), line(final_gain),
        line(final_shift), pooled_output,
    )

    fast = devices == 8 and width == 768 and lax.axis_size("batch") == 4
    bit_list = [half >> 1 & 1] + [me >> level & 1 for level in range(levels)]

    def bits_of(flip):
        return jnp.stack([(half & 1) ^ flip] + bit_list).astype(jnp.int32)

    flat = docs * rows

    def tokens(array):
        return array.reshape(flat, array.shape[-1])

    pairs_feed = [(normed_low, grad_pre), (hidden, grad_branch)]
    if fast:
        sum_feed = reduce_products(bits_of, pairs_feed, levels)

    if gathered:
        back = ([0, 1, 2], [1, 2, 0]) if levels == 3 else (list(range(levels)),) * 2
        places = []
        for which in range(2):
            relative = jnp.arange(devices, dtype=jnp.int32) ^ me
            index = 0
            for bit in back[which]:
                index = index * 2 + (relative >> bit & 1)
            places.append(index)
        places = jnp.stack(places)
    else:
        places = jnp.tile(jnp.arange(2 * reach + 1, dtype=jnp.int32)[None], (2, 1))
    grad_q2, grad_keys, grad_values = pooled_backward(
        places, q2, keys, values, probs_two, grad_mix_two, size
    )

    pooled_grads = []
    if gathered:
        for which, part in enumerate((grad_keys, grad_values)):
            kept = part.reshape((2,) * levels + part.shape[1:])
            came = swap(kept[1], "seq", back[which][0])
            kept = kept[0]
            for bit in back[which][1:]:
                low = (kept[1].astype(F32) + came[1].astype(F32)).astype(BF16)
                kept = kept[0].astype(F32) + came[0].astype(F32)
                came = swap(low, "seq", bit)
            pooled_grads += [kept, came]
    else:
        for part in (grad_keys, grad_values):
            total = part[reach].astype(F32)
            for distance in range(1, reach + 1):
                total = total + shift(part[reach - distance], "seq", -distance).astype(F32)
                total = total + shift(part[reach + distance], "seq", distance).astype(F32)
            pooled_grads += [total, jnp.zeros_like(part[reach])]

    dq, own_grads, low_left, low_right, grad_middle, grad_first, vec_local = local_backward(
        place, q, kx, vx, probs_one, grad_q2, grad_summed, pooled_query, local_output
    )
    from_left = shift(low_right, "seq", 1)
    from_right = shift(low_left, "seq", -1)
    pairs_middle = [
        (tokens(mix_two), grad_second),
        (tokens(middle_low), tokens(grad_q2)),
        (tokens(mix_one), tokens(grad_first)),
        (tokens(inputs), tokens(dq)),
    ]
    if fast:
        sum_middle = reduce_products(bits_of, pairs_middle, levels)

    heads = [
        (pooled_grads[2 * which][:, :1].astype(F32) + pooled_grads[2 * which + 1][:, :1].astype(F32))
        for which in range(2)
    ]
    after = shift(jnp.stack(heads).astype(BF16), "seq", -1)
    grad_k, grad_v, input_grad, vec_input = input_gradients(
        place, own_grads, from_left, from_right, pooled_grads, [after[0], after[1]], kx, vx,
        taps_key, taps_value, dq, grad_middle, local_query, local_key, local_value,
    )
    pairs_last = [(tokens(inputs), tokens(grad_k)), (tokens(inputs), tokens(grad_v))]

    if fast:
        sum_last = reduce_products(bits_of, pairs_last, levels)
        feed_quarters = gather_quarters(sum_feed)
        middle_quarters = gather_quarters(sum_middle)
        last_quarters = gather_quarters(sum_last)
        small = width // devices // 2
        grad_expand = cut_wide(feed_quarters, 0, small)
        grad_reduce = cut_square(feed_quarters, 4 * small, 4 * small)
        grad_po, grad_pq, grad_lo, grad_lq = [
            cut_square(middle_quarters, index * small, small) for index in range(4)
        ]
        grad_lk, grad_lv = [cut_square(last_quarters, index * small, small) for index in range(2)]
    else:

        def plain(pair):
            product = tn(*pair)
            part = lax.psum_scatter(product, "seq", scatter_dimension=0, tiled=True)
            return lax.psum(part.astype(BF16), "batch").astype(F32)

        grad_expand, grad_reduce = map(plain, pairs_feed)
        grad_po, grad_pq, grad_lo, grad_lq = map(plain, pairs_middle)
        grad_lk, grad_lv = map(plain, pairs_last)

    vectors = jnp.concatenate(
        [vec_feed, vec_local, vec_input, vec_wide.reshape(-1, width)], axis=0
    )
    vectors = lax.psum(vectors, ("seq", "batch"))
    share = width // devices
    mine = lax.dynamic_slice_in_dim(vectors, me * share, share, axis=1)
    wide = vectors[32:].reshape(-1)
    wide_share = wide.shape[0] // devices
    grad_eb = lax.dynamic_slice_in_dim(wide, me * wide_share, wide_share, axis=0)
    (fg, fs, rb, ng, ns, pob) = [mine[index] for index in range(6)]
    pqb, lob = mine[8], mine[9]
    grad_ck = mine[16 : 16 + KER].T
    grad_cv = mine[16 + KER : 16 + 2 * KER].T
    cvb, lqb, lvb = mine[26], mine[27], mine[28]
    return (
        outputs, input_grad,
        grad_lq, lqb, grad_lk, grad_lv, lvb, grad_lo, lob, grad_pq, pqb, grad_po, pob,
        grad_ck, grad_cv, cvb, ng, ns, grad_expand, grad_eb, grad_reduce, rb, fg, fs,
    )


def solution(mesh):
    vector = P("seq")
    matrix = P("seq", None)
    return jax.shard_map(
        device_step,
        mesh=mesh,
        in_specs=(P("batch", "seq", None), P("batch"), P("batch", "seq", None)) + (P(),) * 22,
        out_specs=(
            P("batch", "seq", None), P("batch", "seq", None),
            matrix, vector, matrix, matrix, vector, matrix, vector, matrix, vector, matrix, vector,
            matrix, matrix, vector, vector, vector, matrix, vector, matrix, vector, vector, vector,
        ),
        check_vma=False,
    )
```

time: 1370 us -> 541 us (0.39)
  waiting for transfers between devices: 565 us -> 240 us
  matrix products: 307 us -> 0 us
  Pallas kernels: 0 us -> 160 us
  other arithmetic: 174 us -> 22 us
  local copies, waits for them, and re-layouts: 134 us -> 32.9 us
  starting transfers between devices: 114 us -> 61.4 us
  blocking collectives: 46.2 us -> 0 us
    reduce_scatter x5 -> x0, waiting for transfers between devices: 329 us -> none  [the longest x1 165 us: on_device(): lax.psum_scatter(grad_expand_weight, 'seq', scatter_dimension=0, tiled=True)]
    dot_general x72 -> x0, matrix products: 307 us -> none  [the longest x4 77.3 us: attend_backward(): jnp.einsum('hqk,qhd->khd', grad_raw, query_heads, preferred_element_type=...]
    unnamed x16 -> x1, waiting for transfers between devices: 193 us -> 0.02 us
    pallas_call x0 -> x13, Pallas kernels: none -> 160 us  [call(): pl.pallas_call(body, grid_spec=pltpu.PrefetchScalarGridSpec(num_scalar_pr...]
    psum x1, waiting for transfers between devices: 0.01 us -> 115 us  [device_step(): vectors = lax.psum(vectors, ('seq', 'batch'))]
    scatter-add x14 -> x0, other arithmetic: 81.7 us -> none  [the longest x10 79.7 us: backward_part(): local_grads.at[:, tap_start:tap_start + row_count:STRIDE]]
    ppermute x40 -> x38, waiting for transfers between devices: 43.5 us -> 125 us  [the longest x33 121 us: swap(): return lax.ppermute(value, axis, [(i, i ^ 1 << bit) for i in range(count)])]
    ppermute x40 -> x38, starting transfers between devices: 113 us -> 61.3 us  [the longest x33 52.1 us: swap(): return lax.ppermute(value, axis, [(i, i ^ 1 << bit) for i in range(count)])]
  transfers between devices with their start and end apart: 51 -> 39, of which waited for: 14 -> 17; matrix products, arithmetic and copies ran while one was open for 34% -> 9% of each run, Pallas kernels for 0% -> 17%
where the time goes in v1:
time: 541 us; the launch traced here: 531 us
  waiting for transfers between devices  240 us (44%)
  Pallas kernels  160 us (30%)
  starting transfers between devices  61.4 us (11%)
  local copies, waits for them, and re-layouts  32.9 us (6%)
  other arithmetic  22 us (4%)
  between operations  15.1 us (3%)
    pallas_call x13, Pallas kernels, call(): pl.pallas_call(body, grid_spec=pltpu.PrefetchScalarGridSpec(num_scalar_pr...  160 us
    ppermute x33, waiting for transfers between devices, swap(): return lax.ppermute(value, axis, [(i, i ^ 1 << bit) for i in range(count)])  121 us
    psum x1, waiting for transfers between devices, device_step(): vectors = lax.psum(vectors, ('seq', 'batch'))  115 us
    ppermute x33, starting transfers between devices, swap(): return lax.ppermute(value, axis, [(i, i ^ 1 << bit) for i in range(count)])  52.1 us
  transfers between devices with their start and end apart: 39, of which 17 were waited for; matrix products, arithmetic and copies ran while one was open for 9% of the time, Pallas kernels for 17%

profile of v1, /device:TPU:1, one launch (start us, length us, event | category | flops | bytes accessed | tf_op | source)
XLA Modules:
  0.0 531.2 jit_solution(4335086311977375672)
XLA Ops:
  20.3 7.0 %shard_map.442 = (bf16[2,256,768]{2,1,0:T(8,128)(2,1)}, bf16[2,384,768]{2,1,0:T(8,128)(2,1)}, bf16[2,384,768]{2,1,0:T(8,128)(2,1)}, bf16[2,2,64,768]{3,2,1,0:T(8,128)(2,1)}) custom-call(s32[4]{0:T(128)} %pad_add_fusion.2.place, bf16[2,256,768]{2,1,0:T(8,128)(2,1)} %x.3, bf16[2,64,768]{2,1,0:T(8,128)(2,1)} %copy-done.32, bf16[2,64,768]{2,1,0:T(8,128)(2,1)} %copy-done.33, ...), custom_call_target="tpu_custom_call" | custom-call | flops 2415919104 | bytes 10000000 | tf_op jit(solution)/shard_map/pallas_call | solution.py:53
  28.4 5.7 %collective-permute-start.2 = (bf16[1,2,64,768]{3,2,1,0:T(8,128)(2,1)S(1)}, bf16[1,2,64,768]{3,2,1,0:T(8,128)(2,1)S(1)}, u32[]{:S(2)}, u32[]{:S(2)}) collective-permute-start(bf16[1,2,64,768]{3,2,1,0:T(8,128)(2,1)S(1)} %get-tuple-element.137.refs_0_), channel_id=1, source_target_pairs={{0,16},{4,20},{8,24},{12,28},{16,0},{20,4},{24,8},{28,12},{1,17},{... | collective-permute-start | bytes 589832 | tf_op jit(solution)/shard_map/ppermute | solution.py:716
  34.1 9.0 %collective-permute-done.2.refs_1_ = bf16[1,2,64,768]{3,2,1,0:T(8,128)(2,1)S(1)} collective-permute-done((bf16[1,2,64,768]{3,2,1,0:T(8,128)(2,1)S(1)}, bf16[1,2,64,768]{3,2,1,0:T(8,128)(2,1)S(1)}, u32[]{:S(2)}, u32[]{:S(2)}) %collective-permute-start.2) | collective-permute-done | bytes 196640 | tf_op jit(solution)/shard_map/ppermute | solution.py:716
  47.4 13.5 %collective-permute-done.3.refs_2_ = bf16[2,2,64,768]{3,2,1,0:T(8,128)(2,1)S(1)} collective-permute-done((bf16[2,2,64,768]{3,2,1,0:T(8,128)(2,1)S(1)}, bf16[2,2,64,768]{3,2,1,0:T(8,128)(2,1)S(1)}, u32[]{:S(2)}, u32[]{:S(2)}) %collective-permute-start.3) | collective-permute-done | bytes 393248 | tf_op jit(solution)/shard_map/ppermute | solution.py:716
  71.5 15.1 %shard_map.443 = (bf16[2,256,768]{2,1,0:T(8,128)(2,1)}, f32[2,6,2,256,256]{4,3,2,1,0:T(8,128)}, f32[2,256,768]{2,1,0:T(8,128)}, bf16[2,256,768]{2,1,0:T(8,128)(2,1)}, bf16[2,256,768]{2,1,0:T(8,128)(2,1)}) custom-call(s32[4]{0:T(128)} %pad_add_fusion.2.place, bf16[2,256,768]{2,1,0:T(8,128)(2,1)} %get-tuple-element.63.q, ...), custom_call_target="tpu_custom_call" | custom-call | flops 2013265920 | bytes 20000000 | tf_op jit(solution)/shard_map/pallas_call | solution.py:53
  86.7 22.7 %shard_map.444 = (bf16[2,512,768]{2,1,0:T(8,128)(2,1)}, bf16[2,512,768]{2,1,0:T(8,128)(2,1)}, f32[2,6,2,512,256]{4,3,2,1,0:T(8,128)}, bf16[2,256,768]{2,1,0:T(8,128)(2,1)}, f32[2,256,768]{2,1,0:T(8,128)}) custom-call(s32[4]{0:T(128)} %pad_add_fusion.2.place, s32[2,8]{1,0:T(2,128)} %pad_add_fusion.slots, bf16[1,2,64,768]{3,2,1,0:T(8,128)(2,1)} %copy-done.4, ...), custom_call_target="tpu_custom_call" | custom-call | flops 2214592512 | bytes 30000000 | tf_op jit(solution)/shard_map/pallas_call | solution.py:53
  109.4 28.0 %shard_map.445 = (bf16[2,256,768]{2,1,0:T(8,128)(2,1)}, bf16[512,768]{1,0:T(8,128)(2,1)}, bf16[512,3072]{1,0:T(8,128)(2,1)}, bf16[512,768]{1,0:T(8,128)(2,1)}, b...) custom-call(s32[4]{0:T(128)} %pad_add_fusion.2.place, ...), custom_call_target="tpu_custom_call" | custom-call | flops 10267656192 | bytes 30000000 | tf_op jit(solution)/shard_map/pallas_call | solution.py:53
  137.4 9.5 %shard_map.454 = bf16[2,2,2,2,384,384]{5,4,3,2,1,0:T(8,128)(2,1)} custom-call(s32[5]{0:T(128)} %stack.143.bits, bf16[512,768]{1,0:T(8,128)(2,1)} %get-tuple-element.96.refs_0_, bf16[512,3072]{1,0:T(8,128)(2,1)} %get-tuple-element.97.refs_1_, bf16[512,3072]{1,0:T(8,128)(2,1)} %get-tuple-element.98.refs_2_, bf16[512,768]{1,0:T(8,128)(2,1)} %get-tuple-element.99.refs_3_), custom_call_target="tpu_custom_call" | custom-call | flops 2415919104 | bytes 12582912 | tf_op jit(solution)/shard_map/pallas_call | solution.py:53
  148.3 18.7 %shard_map.446 = (bf16[2,256,768]{2,1,0:T(8,128)(2,1)}, bf16[8,2,64,768]{3,2,1,0:T(8,128)(2,1)}, bf16[8,2,64,768]{3,2,1,0:T(8,128)(2,1)}) custom-call(s32[2,8]{1,0:T(2,128)} %pad_add_fusion.1.places, bf16[2,256,768]{2,1,0:T(8,128)(2,1)} %get-tuple-element.66.refs_8_.q2, bf16[2,512,768]{2,1,0:T(8,128)(2,1)} %get-tuple-element.71.keys, ...), custom_call_target="tpu_custom_call" | custom-call | flops 3221225472 | bytes 20000000 | tf_op jit(solution)/shard_map/pallas_call | solution.py:53
  170.0 17.7 %collective-permute-done.13 = bf16[2,2,2,64,768]{4,3,2,1,0:T(8,128)(2,1)S(1)} collective-permute-done((bf16[2,2,2,64,768]{4,3,2,1,0:T(8,128)(2,1)S(1)}, bf16[2,2,2,64,768]{4,3,2,1,0:T(8,128)(2,1)S(1)}, u32[]{:S(2)}, u32[]{:S(2)}) %collective-permute-start.13) | collective-permute-done | bytes 786464 | tf_op jit(solution)/shard_map/ppermute | solution.py:716
  190.7 16.9 %shard_map.447 = (bf16[2,256,768]{2,1,0:T(8,128)(2,1)}, f32[2,2,256,768]{3,2,1,0:T(8,128)}, bf16[2,2,64,768]{3,2,1,0:T(8,128)(2,1)}, bf16[2,2,64,768]{3,2,1,0:T(...) custom-call(s32[4]{0:T(128)} %pad_add_fusion.2.place, ...), custom_call_target="tpu_custom_call" | custom-call | flops 2818572288 | bytes 20000000 | tf_op jit(solution)/shard_map/pallas_call | solution.py:53
  215.3 13.7 %collective-permute-done.15.gv_came = bf16[2,64,768]{2,1,0:T(8,128)(2,1)S(1)} collective-permute-done((bf16[2,64,768]{2,1,0:T(8,128)(2,1)S(1)}, bf16[2,64,768]{2,1,0:T(8,128)(2,1)S(1)}, u32[]{:S(2)}, u32[]{:S(2)}) %collective-permute-start.15) | collective-permute-done | bytes 196640 | tf_op jit(solution)/shard_map/ppermute | solution.py:716
  237.8 9.0 %shard_map.448 = (bf16[2,256,768]{2,1,0:T(8,128)(2,1)}, bf16[2,256,768]{2,1,0:T(8,128)(2,1)}, bf16[2,256,768]{2,1,0:T(8,128)(2,1)}, f32[16,768]{1,0:T(8,128)}) custom-call(s32[4]{0:T(128)} %pad_add_fusion.2.place, f32[2,2,256,768]{3,2,1,0:T(8,128)} %get-tuple-element.77.own, bf16[2,2,64,768]{3,2,1,0:T(8,128)(2,1)} %copy-done.12, ...), custom_call_target="tpu_custom_call" | custom-call | flops 1811939328 | bytes 20000000 | tf_op jit(solution)/shard_map/pallas_call | solution.py:53
  246.8 4.5 shard_map.452
  255.0 6.9 %shard_map.450 = bf16[2,2,2,2,192,384]{5,4,3,2,1,0:T(8,128)(2,1)} custom-call(s32[5]{0:T(128)} %stack.143.bits, bf16[512,768]{1,0:T(8,128)(2,1)} %bitcast.341, bf16[512,768]{1,0:T(8,128)(2,1)} %get-tuple-element.86.refs_1_, bf16[512,768]{1,0:T(8,128)(2,1)} %bitcast.339, bf16[512,768]{1,0:T(8,128)(2,1)} %bitcast.331, bf16[512,768]{1,0:T(8,128)(2,1)} %bitcast.337, ...), custom_call_target="tpu_custom_call" | custom-call | flops 1207959552 | bytes 8650752 | tf_op jit(solution)/shard_map/pallas_call | solution.py:53
  263.7 9.5 %shard_map.453 = bf16[2,2,2,2,384,384]{5,4,3,2,1,0:T(8,128)(2,1)} custom-call(s32[5]{0:T(128)} %stack.141.bits, bf16[512,768]{1,0:T(8,128)(2,1)} %get-tuple-element.96.refs_0_, bf16[512,3072]{1,0:T(8,128)(2,1)} %get-tuple-element.97.refs_1_, bf16[512,3072]{1,0:T(8,128)(2,1)} %get-tuple-element.98.refs_2_, bf16[512,768]{1,0:T(8,128)(2,1)} %get-tuple-element.99.refs_3_), custom_call_target="tpu_custom_call" | custom-call | flops 2415919104 | bytes 12582912 | tf_op jit(solution)/shard_map/pallas_call | solution.py:53
  273.2 5.1 shard_map.451
  286.3 6.8 %shard_map.449 = bf16[2,2,2,2,192,384]{5,4,3,2,1,0:T(8,128)(2,1)} custom-call(s32[5]{0:T(128)} %stack.141.bits, bf16[512,768]{1,0:T(8,128)(2,1)} %bitcast.342, bf16[512,768]{1,0:T(8,128)(2,1)} %get-tuple-element.86.refs_1_, bf16[512,768]{1,0:T(8,128)(2,1)} %bitcast.340, bf16[512,768]{1,0:T(8,128)(2,1)} %bitcast.332, bf16[512,768]{1,0:T(8,128)(2,1)} %bitcast.338, ...), custom_call_target="tpu_custom_call" | custom-call | flops 1207959552 | bytes 8650752 | tf_op jit(solution)/shard_map/pallas_call | solution.py:53
  293.2 115.0 %all-reduce.2.cloned.1.call-done = f32[36,768]{1,0:T(8,128)} async-done(((f32[36,768]{1,0:T(8,128)}), f32[36,768]{1,0:T(8,128)}) %all-reduce.2.cloned.1.call-update) | async-done | bytes 110608 | tf_op jit(solution)/shard_map/psum | solution.py:936
  418.1 5.4 %collective-permute-done.26 = bf16[2,2,96,384]{3,2,1,0:T(8,128)(2,1)S(1)} collective-permute-done((bf16[2,2,96,384]{3,2,1,0:T(8,128)(2,1)S(1)}, bf16[2,2,96,384]{3,2,1,0:T(8,128)(2,1)S(1)}, u32[]{:S(2)}, u32[]{:S(2)}) %collective-permute-start.26) | collective-permute-done | bytes 294944 | tf_op jit(solution)/shard_map/ppermute | solution.py:716
  433.8 11.0 %collective-permute-done.18 = bf16[2,2,2,192,384]{4,3,2,1,0:T(8,128)(2,1)S(1)} collective-permute-done((bf16[2,2,2,192,384]{4,3,2,1,0:T(8,128)(2,1)S(1)}, bf16[2,2,2,192,384]{4,3,2,1,0:T(8,128)(2,1)S(1)}, u32[]{:S(2)}, u32[]{:S(2)}) %collective-permute-start.18) | collective-permute-done | bytes 1179680 | tf_op jit(solution)/shard_map/ppermute | solution.py:716
  451.7 18.4 %collective-permute-done.19 = bf16[2,2,192,384]{3,2,1,0:T(8,128)(2,1)S(1)} collective-permute-done((bf16[2,2,192,384]{3,2,1,0:T(8,128)(2,1)S(1)}, bf16[2,2,192,384]{3,2,1,0:T(8,128)(2,1)S(1)}, u32[]{:S(2)}, u32[]{:S(2)}) %collective-permute-start.19) | collective-permute-done | bytes 589856 | tf_op jit(solution)/shard_map/ppermute | solution.py:716
  478.8 10.6 %collective-permute-done.34 = bf16[2,384,384]{2,1,0:T(8,128)(2,1)S(1)} collective-permute-done((bf16[2,384,384]{2,1,0:T(8,128)(2,1)S(1)}, bf16[2,384,384]{2,1,0:T(8,128)(2,1)S(1)}, u32[]{:S(2)}, u32[]{:S(2)}) %collective-permute-start.34) | collective-permute-done | bytes 589856 | tf_op jit(solution)/shard_map/ppermute | solution.py:716
  494.7 10.8 %collective-permute-done.35 = bf16[384,384]{1,0:T(8,128)(2,1)S(1)} collective-permute-done((bf16[384,384]{1,0:T(8,128)(2,1)S(1)}, bf16[384,384]{1,0:T(8,128)(2,1)S(1)}, u32[]{:S(2)}, u32[]{:S(2)}) %collective-permute-start.35) | collective-permute-done | bytes 294944 | tf_op jit(solution)/shard_map/ppermute | solution.py:716
  (237 shorter events, 125.4 us)
Async XLA Ops:
  7.2 401.0 %all-reduce.2.cloned.1.call-start = ((), (), s32[]{:S(2)}) async-start(), calls=%async_computation | async-start | bytes 245760 | tf_op jit(solution)/shard_map/psum | solution.py:936
  43.2 17.7 %collective-permute-start.3 = (bf16[2,2,64,768]{3,2,1,0:T(8,128)(2,1)S(1)}, bf16[2,2,64,768]{3,2,1,0:T(8,128)(2,1)S(1)}, u32[]{:S(2)}, u32[]{:S(2)}) collective-permute-start(bf16[2,2,64,768]{3,2,1,0:T(8,128)(2,1)S(1)} %pad_maximum_fusion.3), channel_id=1, source_target_pairs={{0,8},{4,12},{8,0},{12,4},{16,24},{20,28},{24,16},{28,20},{1,9},{5... | collective-permute-start | bytes 1179656 | tf_op jit(solution)/shard_map/ppermute | solution.py:716
  61.1 25.5 %collective-permute-start.4 = (bf16[4,2,64,768]{3,2,1,0:T(8,128)(2,1)S(1)}, bf16[4,2,64,768]{3,2,1,0:T(8,128)(2,1)}, u32[]{:S(2)}, u32[]{:S(2)}) collective-permute-start(bf16[4,2,64,768]{3,2,1,0:T(8,128)(2,1)S(1)} %pad_maximum_fusion), channel_id=1, source_target_pairs={{0,4},{4,0},{8,12},{12,8},{16,20},{20,16},{24,28},{28,24},{1,5},{5... | collective-permute-start | bytes 2359304 | tf_op jit(solution)/shard_map/ppermute | solution.py:716
  61.6 25.0 %collective-permute-start.7 = (bf16[4,2,64,768]{3,2,1,0:T(8,128)(2,1)S(1)}, bf16[4,2,64,768]{3,2,1,0:T(8,128)(2,1)}, u32[]{:S(2)}, u32[]{:S(2)}) collective-permute-start(bf16[4,2,64,768]{3,2,1,0:T(8,128)(2,1)S(1)} %pad_maximum_fusion.1), channel_id=1, source_target_pairs={{0,8},{4,12},{8,0},{12,4},{16,24},{20,28},{24,16},{28,20},{1,9},{5... | collective-permute-start | bytes 2359304 | tf_op jit(solution)/shard_map/ppermute | solution.py:716
  146.9 135.0 %collective-permute-start.31 = (bf16[2,2,2,2,384,384]{5,4,3,2,1,0:T(8,128)(2,1)}, bf16[2,2,2,2,384,384]{5,4,3,2,1,0:T(8,128)(2,1)}, u32[]{:S(2)}, u32[]{:S(2)}) collective-permute-start(bf16[2,2,2,2,384,384]{5,4,3,2,1,0:T(8,128)(2,1)} %shard_map.454), channel_id=1, source_target_pairs={{0,1},{1,0},{2,3},{3,2},{4,5},{5,4},{6,7},{7,6},{8,9},{9,8},{10,11... | collective-permute-start | bytes 14155784 | tf_op jit(solution)/shard_map/ppermute | solution.py:716
  168.3 19.4 %collective-permute-start.13 = (bf16[2,2,2,64,768]{4,3,2,1,0:T(8,128)(2,1)S(1)}, bf16[2,2,2,64,768]{4,3,2,1,0:T(8,128)(2,1)S(1)}, u32[]{:S(2)}, u32[]{:S(2)}) collective-permute-start(bf16[2,2,2,64,768]{4,3,2,1,0:T(8,128)(2,1)S(1)} %bitcast.357), channel_id=1, source_target_pairs={{0,8},{4,12},{8,0},{12,4},{16,24},{20,28},{24,16},{28,20},{1,9},{5... | collective-permute-start | bytes 2359304 | tf_op jit(solution)/shard_map/ppermute | solution.py:716
  169.9 20.3 %collective-permute-start.10 = (bf16[2,2,2,64,768]{4,3,2,1,0:T(8,128)(2,1)S(1)}, bf16[2,2,2,64,768]{4,3,2,1,0:T(8,128)(2,1)S(1)}, u32[]{:S(2)}, u32[]{:S(2)}) collective-permute-start(bf16[2,2,2,64,768]{4,3,2,1,0:T(8,128)(2,1)S(1)} %bitcast.356), channel_id=1, source_target_pairs={{0,4},{4,0},{8,12},{12,8},{16,20},{20,16},{24,28},{28,24},{1,5},{5... | collective-permute-start | bytes 2359304 | tf_op jit(solution)/shard_map/ppermute | solution.py:716
  187.8 22.3 %collective-permute-start.14 = (bf16[2,2,64,768]{3,2,1,0:T(8,128)(2,1)S(1)}, bf16[2,2,64,768]{3,2,1,0:T(8,128)(2,1)S(1)}, u32[]{:S(2)}, u32[]{:S(2)}) collective-permute-start(bf16[2,2,64,768]{3,2,1,0:T(8,128)(2,1)S(1)} %get-tuple-element.108), channel_id=1, source_target_pairs={{0,16},{4,20},{8,24},{12,28},{16,0},{20,4},{24,8},{28,12},{1,17},{... | collective-permute-start | bytes 1179656 | tf_op jit(solution)/shard_map/ppermute | solution.py:716
  190.4 23.6 %collective-permute-start.11 = (bf16[2,2,64,768]{3,2,1,0:T(8,128)(2,1)S(1)}, bf16[2,2,64,768]{3,2,1,0:T(8,128)(2,1)S(1)}, u32[]{:S(2)}, u32[]{:S(2)}) collective-permute-start(bf16[2,2,64,768]{3,2,1,0:T(8,128)(2,1)S(1)} %get-tuple-element.110), channel_id=1, source_target_pairs={{0,8},{4,12},{8,0},{12,4},{16,24},{20,28},{24,16},{28,20},{1,9},{5... | collective-permute-start | bytes 1179656 | tf_op jit(solution)/shard_map/ppermute | solution.py:716
  207.6 29.3 %collective-permute-start.8 = (bf16[2,2,64,768]{3,2,1,0:T(8,128)(2,1)}, bf16[2,2,64,768]{3,2,1,0:T(8,128)(2,1)S(1)}, u32[]{:S(2)}, u32[]{:S(2)}) collective-permute-start(bf16[2,2,64,768]{3,2,1,0:T(8,128)(2,1)} %get-tuple-element.78), channel_id=1, source_target_pairs={{0,4},{4,8},{8,12},{12,16},{16,20},{20,24},{24,28},{1,5},{5,9},{9,... | collective-permute-start | bytes 1179656 | tf_op jit(solution)/shard_map/ppermute | solution.py:722
  208.9 28.0 %collective-permute-start.9 = (bf16[2,2,64,768]{3,2,1,0:T(8,128)(2,1)}, bf16[2,2,64,768]{3,2,1,0:T(8,128)(2,1)S(1)}, u32[]{:S(2)}, u32[]{:S(2)}) collective-permute-start(bf16[2,2,64,768]{3,2,1,0:T(8,128)(2,1)} %get-tuple-element.79), channel_id=1, source_target_pairs={{4,0},{8,4},{12,8},{16,12},{20,16},{24,20},{28,24},{5,1},{9,5},{13... | collective-permute-start | bytes 1179656 | tf_op jit(solution)/shard_map/ppermute | solution.py:722
  210.3 18.8 %collective-permute-start.15 = (bf16[2,64,768]{2,1,0:T(8,128)(2,1)S(1)}, bf16[2,64,768]{2,1,0:T(8,128)(2,1)S(1)}, u32[]{:S(2)}, u32[]{:S(2)}) collective-permute-start(bf16[2,64,768]{2,1,0:T(8,128)(2,1)S(1)} %get-tuple-element.122), channel_id=1, source_target_pairs={{0,4},{4,0},{8,12},{12,8},{16,20},{20,16},{24,28},{28,24},{1,5},{5... | collective-permute-start | bytes 589832 | tf_op jit(solution)/shard_map/ppermute | solution.py:716
  214.1 17.1 %collective-permute-start.12 = (bf16[2,64,768]{2,1,0:T(8,128)(2,1)S(1)}, bf16[2,64,768]{2,1,0:T(8,128)(2,1)S(1)}, u32[]{:S(2)}, u32[]{:S(2)}) collective-permute-start(bf16[2,64,768]{2,1,0:T(8,128)(2,1)S(1)} %get-tuple-element.124), channel_id=1, source_target_pairs={{0,16},{4,20},{8,24},{12,28},{16,0},{20,4},{24,8},{28,12},{1,17},{... | collective-permute-start | bytes 589832 | tf_op jit(solution)/shard_map/ppermute | solution.py:716
  251.3 27.0 %collective-permute-start.24 = (bf16[2,2,2,2,96,384]{5,4,3,2,1,0:T(8,128)(2,1)}, bf16[2,2,2,2,96,384]{5,4,3,2,1,0:T(8,128)(2,1)S(1)}, u32[]{:S(2)}, u32[]{:S(2)}) collective-permute-start(bf16[2,2,2,2,96,384]{5,4,3,2,1,0:T(8,128)(2,1)} %shard_map.452), channel_id=1, source_target_pairs={{0,1},{1,0},{2,3},{3,2},{4,5},{5,4},{6,7},{7,6},{8,9},{9,8},{10,11... | collective-permute-start | bytes 3538952 | tf_op jit(solution)/shard_map/ppermute | solution.py:716
  261.9 154.5 %collective-permute-start.17 = (bf16[2,2,2,2,192,384]{5,4,3,2,1,0:T(8,128)(2,1)}, bf16[2,2,2,2,192,384]{5,4,3,2,1,0:T(8,128)(2,1)}, u32[]{:S(2)}, u32[]{:S(2)}) collective-permute-start(bf16[2,2,2,2,192,384]{5,4,3,2,1,0:T(8,128)(2,1)} %shard_map.450), channel_id=1, source_target_pairs={{0,1},{1,0},{2,3},{3,2},{4,5},{5,4},{6,7},{7,6},{8,9},{9,8},{10,11... | collective-permute-start | bytes 7077896 | tf_op jit(solution)/shard_map/ppermute | solution.py:716
  280.7 133.1 %collective-permute-start.25 = (bf16[2,2,2,96,384]{4,3,2,1,0:T(8,128)(2,1)}, bf16[2,2,2,96,384]{4,3,2,1,0:T(8,128)(2,1)}, u32[]{:S(2)}, u32[]{:S(2)}) collective-permute-start(bf16[2,2,2,96,384]{4,3,2,1,0:T(8,128)(2,1)} %fusion.24), channel_id=1, source_target_pairs={{0,2},{1,3},{2,0},{3,1},{4,6},{5,7},{6,4},{7,5},{8,10},{9,11},{10,... | collective-permute-start | bytes 1769480 | tf_op jit(solution)/shard_map/ppermute | solution.py:716
  285.3 145.0 %collective-permute-start.32 = (bf16[2,2,2,384,384]{4,3,2,1,0:T(8,128)(2,1)}, bf16[2,2,2,384,384]{4,3,2,1,0:T(8,128)(2,1)}, u32[]{:S(2)}, u32[]{:S(2)}) collective-permute-start(bf16[2,2,2,384,384]{4,3,2,1,0:T(8,128)(2,1)} %fusion.2), channel_id=1, source_target_pairs={{0,2},{1,3},{2,0},{3,1},{4,6},{5,7},{6,4},{7,5},{8,10},{9,11},{10,... | collective-permute-start | bytes 7077896 | tf_op jit(solution)/shard_map/ppermute | solution.py:716
  417.8 27.1 %collective-permute-start.18 = (bf16[2,2,2,192,384]{4,3,2,1,0:T(8,128)(2,1)S(1)}, bf16[2,2,2,192,384]{4,3,2,1,0:T(8,128)(2,1)S(1)}, u32[]{:S(2)}, u32[]{:S(2)}) collective-permute-start(bf16[2,2,2,192,384]{4,3,2,1,0:T(8,128)(2,1)S(1)} %fusion.10), channel_id=1, source_target_pairs={{0,2},{1,3},{2,0},{3,1},{4,6},{5,7},{6,4},{7,5},{8,10},{9,11},{10,... | collective-permute-start | bytes 3538952 | tf_op jit(solution)/shard_map/ppermute | solution.py:716
  428.1 17.4 %collective-permute-start.28 = (bf16[96,384]{1,0:T(8,128)(2,1)S(1)}, bf16[96,384]{1,0:T(8,128)(2,1)S(1)}, u32[]{:S(2)}, u32[]{:S(2)}) collective-permute-start(bf16[96,384]{1,0:T(8,128)(2,1)S(1)} %fusion.55), channel_id=1, source_target_pairs={{0,16},{4,20},{8,24},{12,28},{16,0},{20,4},{24,8},{28,12},{1,17},{... | collective-permute-start | bytes 221192 | tf_op jit(solution)/shard_map/ppermute | solution.py:716
  432.6 37.7 %collective-permute-start.33 = (bf16[2,2,384,384]{3,2,1,0:T(8,128)(2,1)S(1)}, bf16[2,2,384,384]{3,2,1,0:T(8,128)(2,1)S(1)}, u32[]{:S(2)}, u32[]{:S(2)}) collective-permute-start(bf16[2,2,384,384]{3,2,1,0:T(8,128)(2,1)S(1)} %get-tuple-element.100), channel_id=1, source_target_pairs={{0,4},{4,0},{8,12},{12,8},{16,20},{20,16},{24,28},{28,24},{1,5},{5... | collective-permute-start | bytes 3538952 | tf_op jit(solution)/shard_map/ppermute | solution.py:716
  445.1 24.9 %collective-permute-start.19 = (bf16[2,2,192,384]{3,2,1,0:T(8,128)(2,1)S(1)}, bf16[2,2,192,384]{3,2,1,0:T(8,128)(2,1)S(1)}, u32[]{:S(2)}, u32[]{:S(2)}) collective-permute-start(bf16[2,2,192,384]{3,2,1,0:T(8,128)(2,1)S(1)} %get-tuple-element.104), channel_id=1, source_target_pairs={{0,4},{4,0},{8,12},{12,8},{16,20},{20,16},{24,28},{28,24},{1,5},{5... | collective-permute-start | bytes 1769480 | tf_op jit(solution)/shard_map/ppermute | solution.py:716
  449.1 22.9 %collective-permute-start.30 = (bf16[2,96,384]{2,1,0:T(8,128)(2,1)S(1)}, bf16[2,96,384]{2,1,0:T(8,128)(2,1)S(1)}, u32[]{:S(2)}, u32[]{:S(2)}) collective-permute-start(bf16[2,96,384]{2,1,0:T(8,128)(2,1)S(1)} %pad_maximum_fusion.6), channel_id=1, source_target_pairs={{0,1},{1,0},{2,3},{3,2},{4,5},{5,4},{6,7},{7,6},{8,9},{9,8},{10,11... | collective-permute-start | bytes 442376 | tf_op jit(solution)/shard_map/ppermute | solution.py:716
  470.5 18.9 %collective-permute-start.34 = (bf16[2,384,384]{2,1,0:T(8,128)(2,1)S(1)}, bf16[2,384,384]{2,1,0:T(8,128)(2,1)S(1)}, u32[]{:S(2)}, u32[]{:S(2)}) collective-permute-start(bf16[2,384,384]{2,1,0:T(8,128)(2,1)S(1)} %get-tuple-element.102), channel_id=1, source_target_pairs={{0,8},{4,12},{8,0},{12,4},{16,24},{20,28},{24,16},{28,20},{1,9},{5... | collective-permute-start | bytes 1769480 | tf_op jit(solution)/shard_map/ppermute | solution.py:716
  475.9 18.6 %collective-permute-start.21 = (bf16[192,384]{1,0:T(8,128)(2,1)S(1)}, bf16[192,384]{1,0:T(8,128)(2,1)S(1)}, u32[]{:S(2)}, u32[]{:S(2)}) collective-permute-start(bf16[192,384]{1,0:T(8,128)(2,1)S(1)} %fusion.47), channel_id=1, source_target_pairs={{0,16},{4,20},{8,24},{12,28},{16,0},{20,4},{24,8},{28,12},{1,17},{... | collective-permute-start | bytes 442376 | tf_op jit(solution)/shard_map/ppermute | solution.py:716
  (51 other events, 620.3 us)
Sparse Core Ops, SparseCore 0:
  286.4 121.7 all-reduce.1

commit v2 on v1

v2 whole, which is shorter than its diff:
```python
import functools
import math

import jax
import jax.numpy as jnp
from jax import lax
from jax.experimental import pallas as pl
from jax.experimental.pallas import tpu as pltpu
from jax.sharding import PartitionSpec as P

HEADS = 12
HD = 64
WIN = 128
PWIN = 512
KER = 5
STRIDE = 4
HALF = WIN // 2
REACH = PWIN // 2
NEGATIVE = -1e30
SCALE = 1.0 / math.sqrt(HD)
EPSILON = 1e-05
LANES = 128
TILE = 128
ROWS = 128
CHUNK = 256
F32 = jnp.float32
BF16 = jnp.bfloat16


def nn(left, right):
    return jnp.dot(left, right, preferred_element_type=F32)


def nt(left, right):
    return lax.dot_general(left, right, (((1,), (1,)), ((), ())), preferred_element_type=F32)


def tn(left, right):
    return lax.dot_general(left, right, (((0,), (0,)), ((), ())), preferred_element_type=F32)


def column_sum(block):
    return jnp.sum(block.astype(F32), axis=0, keepdims=True)


def call(body, grid, scalars, inputs, outputs, scratch=(), flops=0, moved=0, exps=0, spare=6):
    single = math.prod(grid) == 1
    used = spare * 2**20

    def spec(shape, dtype, block, index):
        nonlocal used
        fixed = single or tuple(block) == tuple(shape)
        used += math.prod(block) * jnp.dtype(dtype).itemsize * (1 if fixed else 2)
        mode = pl.Buffered(1) if fixed else None
        return pl.BlockSpec(block, index, pipeline_mode=mode)

    in_specs = [spec(a.shape, a.dtype, block, index) for a, block, index in inputs]
    out_specs = [spec(shape, dtype, block, index) for shape, dtype, block, index in outputs]
    for item in scratch:
        used += math.prod(item.shape) * jnp.dtype(item.dtype).itemsize
    return pl.pallas_call(
        body,
        grid_spec=pltpu.PrefetchScalarGridSpec(
            num_scalar_prefetch=len(scalars),
            grid=grid,
            in_specs=in_specs,
            out_specs=out_specs,
            scratch_shapes=list(scratch),
        ),
        out_shape=[jax.ShapeDtypeStruct(shape, dtype) for shape, dtype, _, _ in outputs],
        compiler_params=pltpu.CompilerParams(
            dimension_semantics=("arbitrary",) * len(grid), vmem_limit_bytes=used
        ),
        cost_estimate=pl.CostEstimate(flops=1000, bytes_accessed=1000, transcendentals=0),
    )(*scalars, *[array for array, _, _ in inputs])


def whole(array):
    zeros = (0,) * array.ndim
    return (array, array.shape, lambda *_: zeros)


def by_doc(array):
    zeros = (0,) * (array.ndim - 1)
    return (array, (1,) + array.shape[1:], lambda doc, *_: (doc,) + zeros)


def one_doc(array, doc):
    zeros = (0,) * (array.ndim - 1)
    return (array, (1,) + array.shape[1:], lambda *_: (doc,) + zeros)


def out_doc(shape, dtype):
    zeros = (0,) * (len(shape) - 1)
    return (shape, dtype, (1,) + tuple(shape[1:]), lambda doc, *_: (doc,) + zeros)


def out_whole(shape, dtype):
    zeros = (0,) * len(shape)
    return (shape, dtype, shape, lambda *_: zeros)


def sync(*values):
    return lax.optimization_barrier(values)


def stack_heads(block):
    lane = lax.broadcasted_iota(jnp.int32, block.shape, 1)
    zero = jnp.zeros_like(block)
    return jnp.concatenate(
        [jnp.where(lane < HD, block, zero), jnp.where(lane < HD, zero, block)], axis=0
    )


def unstack(block):
    joined = jnp.concatenate([block[:HD, :TILE], block[HD:, TILE:]], axis=0)
    return joined.T


def positions(shape, dim):
    return lax.broadcasted_iota(jnp.int32, shape, dim)


def project_body(place, x, left, right, wq, bq, wk, wv, bv, ck, cv, bcv, q, kx, vx, pooled, rows):
    doc = pl.program_id(0)
    offset, length = place[0], place[1 + doc]
    own = x[0]
    q[0] = (nn(own, wq[...]) + bq[...]).astype(BF16)
    extended = jnp.concatenate([left[0], own, right[0]], axis=0)
    spot = offset - HALF + positions((extended.shape[0], 1), 0)
    valid = (spot >= 0) & (spot < length)
    count = pooled.shape[2]
    for which, (weight, bias, taps, out) in enumerate(((wk, None, ck, kx), (wv, bv, cv, vx))):
        value = nn(extended, weight[...])
        if bias is not None:
            value = value + bias[...]
        value = value.astype(BF16)
        out[0] = value
        masked = jnp.where(valid, value.astype(F32), 0.0)
        for group in range(value.shape[1] // LANES):
            lanes = slice(group * LANES, (group + 1) * LANES)
            rows[group] = masked[:, lanes]
            total = jnp.zeros((count, LANES), F32)
            for tap in range(KER):
                start = HALF - KER // 2 + tap
                read = rows[group, pl.ds(start, count, stride=STRIDE), :]
                total = total + read * taps[tap : tap + 1, lanes]
            if which == 1:
                total = total + bcv[:, lanes]
            pooled[0, which, :, lanes] = total.astype(BF16)


def project(place, x, left, right, wq, bq, wk, wv, bv, ck, cv, bcv):
    docs, rows, width = x.shape
    extended = rows + WIN
    return call(
        project_body,
        (docs,),
        (place,),
        [by_doc(x), by_doc(left), by_doc(right)]
        + [whole(a) for a in (wq, bq, wk, wv, bv, ck, cv, bcv)],
        [
            out_doc((docs, rows, width), BF16),
            out_doc((docs, extended, width), BF16),
            out_doc((docs, extended, width), BF16),
            out_doc((docs, 2, rows // STRIDE, width), BF16),
        ],
        [pltpu.VMEM((width // LANES, extended, LANES), F32)],
        flops=2 * docs * (rows + 2 * extended) * width * width,
        moved=10**7,
    )


def local_bias(tile, offset, length):
    shape = (TILE + WIN, TILE)
    key = positions(shape, 0)
    query = positions(shape, 1)
    spot = offset + tile * TILE - HALF + key
    allowed = (
        (key >= query) & (key < query + WIN) & (spot >= 0) & (spot < length)
    ) | (key == query + HALF)
    return jnp.where(allowed, 0.0, NEGATIVE)


def softmax_columns(scores):
    top = jnp.max(scores, axis=0, keepdims=True)
    grown = jnp.exp(scores - top)
    return grown * (1.0 / jnp.sum(grown, axis=0, keepdims=True))


def local_forward_body(place, q, kx, vx, mix, probs, *, doc):
    offset, length = place[0], place[1 + doc]
    span = TILE + WIN
    for tile in range(q.shape[1] // TILE):
        half_bias = local_bias(tile, offset, length)
        bias = jnp.concatenate([half_bias, half_bias], axis=1)
        first = tile * TILE
        for pair in range(q.shape[2] // LANES):
            lanes = slice(pair * LANES, (pair + 1) * LANES)
            queries = stack_heads(q[0, first : first + TILE, lanes]) * SCALE
            scores = nt(kx[0, first : first + span, lanes], queries) + bias
            chance = softmax_columns(scores)
            probs[pair, tile] = chance
            turned = vx[0, first : first + span, lanes].T
            mixed = nn(turned, chance.astype(BF16))
            mix[first : first + TILE, lanes] = unstack(mixed).astype(BF16)


def local_forward(place, q, kx, vx, doc):
    _, rows, width = q.shape
    pairs, tiles, span = width // LANES, rows // TILE, TILE + WIN
    return call(
        functools.partial(local_forward_body, doc=doc),
        (1,),
        (place,),
        [one_doc(a, doc) for a in (q, kx, vx)],
        [
            out_whole((rows, width), BF16),
            out_whole((pairs, tiles, span, 2 * TILE), F32),
        ],
        flops=rows * width * 4 * 2 * span,
        moved=10**7,
        exps=rows * HEADS * span,
    )


def middle_body(place, x, wo, bo, wpq, bpq, *refs):
    docs, rows = x.shape[0], x.shape[1]
    mixes, (mix, middle, middle_low, q2) = refs[:docs], refs[docs:]
    for doc in range(docs):
        mix[doc] = mixes[doc][...]
    flat = docs * rows
    branch = nn(mix[...].reshape(flat, x.shape[2]), wo[...]) + bo[...]
    total = x[...].reshape(flat, x.shape[2]).astype(F32) + branch
    middle[...] = total.reshape(middle.shape)
    low = total.astype(BF16)
    middle_low[...] = low.reshape(middle_low.shape)
    q2[...] = (nn(low, wpq[...]) + bpq[...]).astype(BF16).reshape(q2.shape)


def middle_forward(place, x, wo, bo, wpq, bpq, mixes):
    docs, rows, width = x.shape
    return call(
        middle_body,
        (1,),
        (place,),
        [whole(a) for a in (x, wo, bo, wpq, bpq, *mixes)],
        [
            out_whole((docs, rows, width), BF16),
            out_whole((docs, rows, width), F32),
            out_whole((docs, rows, width), BF16),
            out_whole((docs, rows, width), BF16),
        ],
        flops=docs * rows * width * width * 4,
        moved=10**7,
    )


def attention_back(keys, values, queries, grads, chance):
    stacked_grads = stack_heads(grads)
    stacked_queries = stack_heads(queries)
    grad_chance = nt(values, stacked_grads * SCALE)
    dots = jnp.sum(chance * grad_chance, axis=0, keepdims=True)
    grad_raw = (chance * (grad_chance - dots)).astype(BF16)
    grad_keys = nn(grad_raw, stacked_queries)
    grad_values = nn(chance.astype(BF16), stacked_grads)
    grad_queries = unstack(nn(keys.T, grad_raw))
    return grad_queries, grad_keys, grad_values


def first_back_body(place, gq2, gsum, wpq, wo, gmid, gfirst, gmix, vec):
    docs, rows, width = gsum.shape
    flat = docs * rows
    grads = gq2[...].reshape(flat, width)
    total = gsum[...].reshape(flat, width) + nt(grads, wpq[...])
    gmid[...] = total.reshape(gmid.shape)
    low = total.astype(BF16)
    gfirst[...] = low
    gmix[...] = nt(low, wo[...]).astype(BF16).reshape(gmix.shape)
    vec[...] = jnp.zeros_like(vec)
    vec[0:1] = column_sum(grads)
    vec[1:2] = column_sum(low)


def first_backward(place, gq2, gsum, wpq, wo):
    docs, rows, width = gsum.shape
    return call(
        first_back_body,
        (1,),
        (place,),
        [whole(a) for a in (gq2, gsum, wpq, wo)],
        [
            out_whole((docs, rows, width), F32),
            out_whole((docs * rows, width), BF16),
            out_whole((docs, rows, width), BF16),
            out_whole((8, width), F32),
        ],
        flops=docs * rows * width * width * 4,
        moved=10**7,
    )


def local_backward_body(place, q, kx, vx, gmix, probs, *refs, doc):
    earlier = refs[: len(refs) - 6]
    dq, own, low_left, low_right, dk, dv = refs[len(refs) - 6 :]
    rows = q.shape[1]
    for old, new in zip(earlier, (dq, own, low_left, low_right)):
        new[:doc] = old[...]
    span = TILE + WIN
    dk[...] = jnp.zeros_like(dk)
    dv[...] = jnp.zeros_like(dv)
    for tile in range(rows // TILE):
        first = tile * TILE
        for pair in range(q.shape[2] // LANES):
            lanes = slice(pair * LANES, (pair + 1) * LANES)
            grad_q, grad_k, grad_v = attention_back(
                kx[0, first : first + span, lanes],
                vx[0, first : first + span, lanes],
                q[0, first : first + TILE, lanes],
                gmix[0, first : first + TILE, lanes],
                probs[pair, tile],
            )
            dq[doc, first : first + TILE, lanes] = grad_q.astype(BF16)
            dk[first : first + span, lanes] += grad_k
            dv[first : first + span, lanes] += grad_v
    for which, part in enumerate((dk, dv)):
        own[doc, which] = part[HALF : HALF + rows]
        low_left[doc, which] = part[:HALF].astype(BF16)
        low_right[doc, which] = part[HALF + rows :].astype(BF16)


def local_backward(place, q, kx, vx, gmix, probs, doc, earlier=()):
    _, rows, width = q.shape
    span = TILE + WIN
    return call(
        functools.partial(local_backward_body, doc=doc),
        (1,),
        (place,),
        [one_doc(a, doc) for a in (q, kx, vx, gmix)] + [whole(a) for a in (probs, *earlier)],
        [
            out_whole((doc + 1, rows, width), BF16),
            out_whole((doc + 1, 2, rows, width), F32),
            out_whole((doc + 1, 2, HALF, width), BF16),
            out_whole((doc + 1, 2, HALF, width), BF16),
        ],
        [
            pltpu.VMEM((rows + WIN, width), F32),
            pltpu.VMEM((rows + WIN, width), F32),
        ],
        flops=rows * width * 8 * 2 * span,
        moved=10**7,
    )


def pooled_forward_body(place, slots, *refs, pieces):
    key_pieces = refs[:pieces]
    value_pieces = refs[pieces : 2 * pieces]
    q2, middle, wpo, bpo, keys, values, probs, mix, summed, bias = refs[2 * pieces :]
    doc, pair = pl.program_id(0), pl.program_id(1)
    offset, length, base = place[0], place[1 + doc], place[1 + pl.num_programs(0)]
    tiles = q2.shape[1] // TILE
    count = keys.shape[1]

    @pl.when(pair == 0)
    def _():
        for where, group, out in ((0, key_pieces, keys), (1, value_pieces, values)):
            at = 0
            for piece in group:
                size = piece.shape[2]
                for block in range(piece.shape[0]):
                    spot = pl.multiple_of(slots[where, at] * size, size)
                    out[0, pl.ds(spot, size), :] = piece[block, 0]
                    at += 1
        for tile in range(tiles):
            shape = (count, TILE)
            spot = base + positions(shape, 0)
            centre = offset // STRIDE + (tile * TILE + positions(shape, 1)) // STRIDE
            allowed = (
                (spot >= centre - REACH)
                & (spot < centre + REACH)
                & (spot >= 0)
                & (spot * STRIDE < length)
            ) | (spot == centre)
            bias[tile] = jnp.where(allowed, 0.0, NEGATIVE)

    lanes = pl.ds(pl.multiple_of(pair * LANES, LANES), LANES)
    pair_keys = keys[0, :, lanes]
    turned = values[0, :, lanes].T
    for tile in range(tiles):
        first = tile * TILE
        queries = stack_heads(q2[0, first : first + TILE, :]) * SCALE
        half_bias = bias[tile]
        scores = nt(pair_keys, queries) + jnp.concatenate([half_bias, half_bias], axis=1)
        chance = softmax_columns(scores)
        probs[0, 0, tile] = chance
        mixed = nn(turned, chance.astype(BF16))
        mix[0, first : first + TILE, lanes] = unstack(mixed).astype(BF16)

    @pl.when(pair == pl.num_programs(1) - 1)
    def _():
        summed[0] = middle[0] + (nn(mix[0], wpo[...]) + bpo[...])


def pooled_forward(place, slots, key_pieces, value_pieces, q2, middle, wpo, bpo):
    docs, rows, width = q2.shape
    pairs, tiles = width // LANES, rows // TILE
    size = key_pieces[0].shape[2]
    count = size * slots.shape[1]

    def piece(array):
        return (array, (array.shape[0], 1, size, width), lambda doc, *_: (0, doc, 0, 0))

    return call(
        functools.partial(pooled_forward_body, pieces=len(key_pieces)),
        (docs, pairs),
        (place, slots),
        [piece(a) for a in key_pieces + value_pieces]
        + [
            (q2, (1, rows, LANES), lambda doc, pair, *_: (doc, 0, pair)),
            by_doc(middle),
            whole(wpo),
            whole(bpo),
        ],
        [
            out_doc((docs, count, width), BF16),
            out_doc((docs, count, width), BF16),
            (
                (docs, pairs, tiles, count, 2 * TILE),
                F32,
                (1, 1, tiles, count, 2 * TILE),
                lambda doc, pair, *_: (doc, pair, 0, 0, 0),
            ),
            out_doc((docs, rows, width), BF16),
            out_doc((docs, rows, width), F32),
        ],
        [pltpu.VMEM((tiles, count, TILE), F32)],
        flops=docs * rows * width * (2 * width + 4 * 2 * count),
        moved=3 * 10**7,
        exps=docs * rows * HEADS * count,
    )


def pooled_backward_body(
    places, token, q2, keys, values, probs, grads, dq, dk_kept, dk_sent, dv_kept, dv_sent, sums
):
    size = dk_kept.shape[2]
    total = None
    for tile in range(q2.shape[1] // TILE):
        first = tile * TILE
        grad_q, *added = attention_back(
            keys[0], values[0], q2[0, first : first + TILE], grads[0, first : first + TILE],
            probs[0, 0, tile],
        )
        dq[0, first : first + TILE] = grad_q.astype(BF16)
        total = added if total is None else [a + b for a, b in zip(total, added)]
    half = dk_kept.shape[0]
    for which, (kept, sent) in enumerate(((dk_kept, dk_sent), (dv_kept, dv_sent))):
        sums[...] = total[which]
        for block in range(half + sent.shape[0]):
            start = pl.multiple_of(places[which, block] * size, size)
            part = sums[pl.ds(start, size), :]
            if block < half:
                kept[block, 0] = part
            else:
                sent[block - half, 0] = part.astype(BF16)


def pooled_backward(places, token, q2, keys, values, probs, grads, size, kept):
    docs, rows, width = q2.shape
    count = keys.shape[1]
    blocks = count // size
    tiles = rows // TILE

    def lanes_of(array):
        return (array, (1, array.shape[1], LANES), lambda doc, pair, *_: (doc, 0, pair))

    def spread(number, dtype):
        return (
            (number, docs, size, width),
            dtype,
            (number, 1, size, LANES),
            lambda doc, pair, *_: (0, doc, 0, pair),
        )

    return call(
        pooled_backward_body,
        (docs, width // LANES),
        (places, token),
        [
            lanes_of(q2),
            lanes_of(keys),
            lanes_of(values),
            (
                probs,
                (1, 1, tiles, count, 2 * TILE),
                lambda doc, pair, *_: (doc, pair, 0, 0, 0),
            ),
            lanes_of(grads),
        ],
        [
            ((docs, rows, width), BF16, (1, rows, LANES), lambda doc, pair, *_: (doc, 0, pair)),
            spread(kept, F32),
            spread(blocks - kept, BF16),
            spread(kept, F32),
            spread(blocks - kept, BF16),
        ],
        [pltpu.VMEM((count, LANES), F32)],
        flops=docs * rows * width * 8 * 2 * count,
        moved=2 * 10**7,
    )


def feed_body(
    place, summed, cotangent, we, be, wr, br, ng, ns, fg, fs, wpo,
    outputs, normed_low, hidden, grad_branch, grad_pre, grad_summed, grad_second, grad_mix,
    vec, vec_wide,
    normed, slope, work, unit,
):
    docs, rows = cotangent.shape[0], cotangent.shape[1]
    width = summed.shape[2]
    wide = we.shape[1]
    steps = rows // ROWS
    blocks = [(doc, step * ROWS, doc * rows + step * ROWS) for doc in range(docs) for step in range(steps)]

    def normal(value):
        centred = value - jnp.mean(value, axis=-1, keepdims=True)
        scale = lax.rsqrt(jnp.mean(centred * centred, axis=-1, keepdims=True) + EPSILON)
        return centred * scale, scale

    scales = []
    for doc, start, row in blocks:
        norm, scale = normal(summed[doc, start : start + ROWS])
        scales.append(scale)
        unit[row : row + ROWS] = norm
        full = norm * ng[...] + ns[...]
        normed[row : row + ROWS] = full
        normed_low[row : row + ROWS] = full.astype(BF16)

    def expand(index, _):
        part = pl.ds(pl.multiple_of(index * CHUNK, CHUNK), CHUNK)
        pre = nn(normed_low[...], we[:, part]) + be[:, part]
        cdf = 0.5 * (1.0 + lax.erf(pre * math.sqrt(0.5)))
        hidden[:, part] = (pre * cdf).astype(BF16)
        slope[:, part] = cdf + pre * (jnp.exp(pre * pre * -0.5) * (1.0 / math.sqrt(2.0 * math.pi)))
        return 0

    lax.fori_loop(0, wide // CHUNK, expand, 0)

    for start in range(0, width, CHUNK):
        part = slice(start, start + CHUNK)
        work[:, part] = normed[:, part] + (nn(hidden[...], wr[:, part]) + br[:, part])

    sums = [jnp.zeros((1, width), F32) for _ in range(6)]
    for doc, start, row in blocks:
        norm, scale = normal(work[row : row + ROWS])
        spot = place[0] + start + positions((ROWS, 1), 0)
        valid = (spot < place[1 + doc]).astype(F32)
        outputs[doc, start : start + ROWS] = (valid * (norm * fg[...] + fs[...])).astype(BF16)
        error = valid * cotangent[doc, start : start + ROWS].astype(F32)
        sums[0] += column_sum(error * norm)
        sums[1] += column_sum(error)
        scaled = error * fg[...]
        rest = (
            scaled
            - jnp.mean(scaled, axis=-1, keepdims=True)
            - norm * jnp.mean(scaled * norm, axis=-1, keepdims=True)
        ) * scale
        work[row : row + ROWS] = rest
        low = rest.astype(BF16)
        grad_branch[row : row + ROWS] = low
        sums[2] += column_sum(low)

    def reduce(index, _):
        part = pl.ds(pl.multiple_of(index * CHUNK, CHUNK), CHUNK)
        low = (nt(grad_branch[...], wr[part, :]) * slope[:, part]).astype(BF16)
        grad_pre[:, part] = low
        vec_wide[:, part] = column_sum(low)
        return 0

    lax.fori_loop(0, wide // CHUNK, reduce, 0)

    for start in range(0, width, CHUNK):
        part = slice(start, start + CHUNK)
        work[:, part] += nt(grad_pre[...], we[part, :])

    for (doc, start, row), scale in zip(blocks, scales):
        error = work[row : row + ROWS]
        norm = unit[row : row + ROWS]
        sums[3] += column_sum(error * norm)
        sums[4] += column_sum(error)
        scaled = error * ng[...]
        grad = (
            scaled
            - jnp.mean(scaled, axis=-1, keepdims=True)
            - norm * jnp.mean(scaled * norm, axis=-1, keepdims=True)
        ) * scale
        grad_summed[doc, start : start + ROWS] = grad
        low = grad.astype(BF16)
        grad_second[row : row + ROWS] = low
        sums[5] += column_sum(low)
        grad_mix[doc, start : start + ROWS] = nt(low, wpo[...]).astype(BF16)
    for index, value in enumerate(sums):
        vec[index : index + 1] = value
    vec[6:8] = jnp.zeros((2, width), F32)


def feed(place, summed, cotangent, we, be, wr, br, ng, ns, fg, fs, wpo):
    docs, rows, width = summed.shape
    wide = we.shape[1]
    tokens = docs * rows
    return call(
        feed_body,
        (1,),
        (place,),
        [whole(a) for a in (summed, cotangent, we, be, wr, br, ng, ns, fg, fs, wpo)],
        [
            out_whole((docs, rows, width), BF16),
            out_whole((tokens, width), BF16),
            out_whole((tokens, wide), BF16),
            out_whole((tokens, width), BF16),
            out_whole((tokens, wide), BF16),
            out_whole((docs, rows, width), F32),
            out_whole((tokens, width), BF16),
            out_whole((docs, rows, width), BF16),
            out_whole((8, width), F32),
            out_whole((1, wide), F32),
        ],
        [
            pltpu.VMEM((tokens, width), F32),
            pltpu.VMEM((tokens, wide), F32),
            pltpu.VMEM((tokens, width), F32),
            pltpu.VMEM((tokens, width), F32),
        ],
        flops=2 * tokens * width * (4 * wide + width),
        moved=3 * 10**7,
        exps=2 * tokens * wide,
    )


def key_value_body(place, *refs, docs):
    (gk_kept, gk_came, gv_kept, gv_came, gk_next, gv_next, kx, vx, ck, cv) = refs[:10]
    own, from_left, from_right, dq = refs[10:14]
    gk, gv, vec, rows_in, pooled, total = refs[14:]
    offset = place[0]
    rows, width = gk.shape[0] // docs, gk.shape[1]
    count = rows // STRIDE
    vec[...] = jnp.zeros_like(vec)
    for doc in range(docs):
        length = place[1 + doc]
        spot = offset - HALF + positions((rows + WIN, 1), 0)
        valid = (spot >= 0) & (spot < length)
        first = doc * rows
        for which, (kept, came, after, ext, taps, out, row) in enumerate(
            (
                (gk_kept, gk_came, gk_next, kx, ck, gk, 0),
                (gv_kept, gv_came, gv_next, vx, cv, gv, KER),
            )
        ):
            pooled[:count] = kept[doc].astype(F32) + came[doc].astype(F32)
            pooled[count:] = jnp.broadcast_to(after[doc].astype(F32), (8, width))
            masked = jnp.where(valid, ext[doc].astype(F32), 0.0)
            for group in range(width // LANES):
                lanes = slice(group * LANES, (group + 1) * LANES)
                grown = pooled[:count, lanes]
                shifted = pooled[1 : count + 1, lanes]
                rows_in[group] = masked[:, lanes]
                for tap in range(KER):
                    start = HALF - KER // 2 + tap
                    read = rows_in[group, pl.ds(start, count, stride=STRIDE), :]
                    vec[row + tap : row + tap + 1, lanes] += column_sum(grown * read)
                if which == 1:
                    vec[2 * KER : 2 * KER + 1, lanes] += column_sum(grown)
                total[group] = own[doc, which, :, lanes]
                total[group, :HALF] += from_left[doc, which, :, lanes].astype(F32)
                total[group, rows - HALF :] += from_right[doc, which, :, lanes].astype(F32)
                for phase, terms in enumerate(
                    (
                        ((2, grown),),
                        ((3, grown),),
                        ((4, grown), (0, shifted)),
                        ((1, shifted),),
                    )
                ):
                    part = pl.ds(phase, count, stride=STRIDE)
                    added = None
                    for tap, values in terms:
                        term = values * taps[tap : tap + 1, lanes]
                        added = term if added is None else added + term
                    inside = offset + phase + STRIDE * positions((count, 1), 0) < length
                    total[group, part, :] = total[group, part, :] + jnp.where(inside, added, 0.0)
                out[first : first + rows, lanes] = total[group].astype(BF16)
        vec[11:12] += column_sum(dq[doc])
    vec[12:13] += column_sum(gv[...])


def key_value_gradients(place, pooled_grads, next_grads, kx, vx, ck, cv, own, left, right, dq):
    docs, rows, width = dq.shape
    return call(
        functools.partial(key_value_body, docs=docs),
        (1,),
        (place,),
        [
            whole(a)
            for a in (*pooled_grads, *next_grads, kx, vx, ck, cv, own, left, right, dq)
        ],
        [out_whole((docs * rows, width), BF16)] * 2 + [out_whole((16, width), F32)],
        [
            pltpu.VMEM((width // LANES, rows + WIN, LANES), F32),
            pltpu.VMEM((rows // STRIDE + 8, width), F32),
            pltpu.VMEM((width // LANES, rows, LANES), F32),
        ],
        flops=docs * rows * width * 40,
        moved=10**7,
    )


def input_body(place, dq, gk, gv, gmid, wq, wk, wv, dx):
    total = nt(dq[...], wq[...]) + nt(gk[...], wk[...]) + nt(gv[...], wv[...])
    dx[...] = (gmid[...] + total.reshape(gmid.shape)).astype(BF16)


def input_gradient(place, dq, gk, gv, gmid, wq, wk, wv):
    docs, rows, width = gmid.shape
    (dx,) = call(
        input_body,
        (1,),
        (place,),
        [whole(a) for a in (dq, gk, gv, gmid, wq, wk, wv)],
        [out_whole((docs, rows, width), BF16)],
        flops=2 * docs * rows * width * 3 * width,
        moved=10**7,
    )
    return dx


def scatter_body(bits, *refs, kinds, order, vectors, quartered):
    count = len(kinds)
    operands = [refs[2 * index : 2 * index + 2] for index in range(count)]
    extra = refs[2 * count : 2 * count + vectors]
    rest = refs[2 * count + vectors :]
    if quartered:
        results, (ordered, rounded, *small) = (rest[0], rest[0]), rest[1:]
    else:
        results, (ordered, rounded, *small) = rest[:2], rest[2:]
    core = bits[0]
    sides = 2 if ("batch", 1) in order else 1
    owners = 8

    def start_of(which, size):
        if quartered:
            return which * size
        return pl.multiple_of((which ^ core) * size, LANES)

    def place_tile(which, side, owner, target, size, value):
        index = []
        for at, (axis, bit) in enumerate(order):
            if axis == "batch":
                index += [side, which] if quartered else [side ^ bits[1 + at]]
            else:
                index.append(((owner >> bit) & 1) ^ bits[1 + at])
        results[which][(*index, slice(target, target + size), slice(None))] = value

    base = 0
    for (left, right), kind in zip(operands, kinds):
        tall = left.shape[1]
        turned = left[...].T
        if kind == "wide":
            half = right.shape[1] // 2
            size = tall // owners // sides
            for which in range(2):
                start = start_of(which, half)
                for part in range(half // 768):
                    rounded[...] = nn(turned, right[:, pl.ds(start + part * 768, 768)]).astype(BF16)
                    for column in range(2):
                        target = base + (2 * part + column) * size
                        for owner in range(owners):
                            for side in range(sides):
                                row = (owner * sides + side) * size
                                value = rounded[row : row + size, column * 384 : column * 384 + 384]
                                place_tile(which, side, owner, target, size, value)
            base += half // 384 * size
        elif kind == "tall":
            ordered[...] = turned
            size = tall // 2 // sides
            for part in range(right.shape[1] // 768):
                product = nn(ordered[...], right[:, part * 768 : part * 768 + 768])
                rounded[...] = product.astype(BF16)
                for column in range(2):
                    owner = 2 * part + column
                    for side in range(sides):
                        for which in range(2):
                            row = start_of(which, 384) + side * size
                            value = rounded[pl.ds(row, size), column * 384 : column * 384 + 384]
                            place_tile(which, side, owner, base, size, value)
            base += size
        else:
            size = tall // owners // sides
            if quartered:
                columns = right[...]
            else:
                columns = jnp.concatenate(
                    [right[:, pl.ds(start_of(which, 384), 384)] for which in range(2)], axis=1
                )
            rounded[...] = nn(turned, columns).astype(BF16)
            for which in range(2):
                for owner in range(owners):
                    for side in range(sides):
                        row = (owner * sides + side) * size
                        value = rounded[row : row + size, which * 384 : which * 384 + 384]
                        place_tile(which, side, owner, base, size, value)
            base += size
    if vectors:
        (block,) = small
        vec_feed, vec_first, vec_input, vec_wide = extra
        for owner in range(owners):
            lanes = slice(owner * 96, owner * 96 + 96)
            block[0, owner] = jnp.zeros(block.shape[2:], F32)
            block[1, owner] = jnp.zeros(block.shape[2:], F32)
            block[0, owner, 0:8, 0:96] = vec_feed[:, lanes]
            block[0, owner, 0:8, LANES : LANES + 96] = vec_first[:, lanes]
            block[1, owner, 0:16, 0:96] = vec_input[:, lanes]
            for part in range(4):
                at = owner * 384 + part * 96
                block[0, owner, 8 + part : 9 + part, 0:96] = vec_wide[:, at : at + 96]
        for owner in range(owners):
            for which in range(2):
                place_tile(which, 0, owner, base, 16, block[which ^ core, owner].astype(BF16))


def scatter_products(bits, order, items, extra=(), quartered=False):
    sides = 2 if ("batch", 1) in order else 1
    rows = 0
    for kind, left, right in items:
        if kind == "wide":
            rows += right.shape[1] // 768 * (left.shape[1] // 8 // sides)
        elif kind == "tall":
            rows += 384 // sides
        else:
            rows += 96 // sides
    rows += 16 if extra else 0
    shape = (2,) * (len(order) + quartered) + (rows, 384)
    operands = [array for _, left, right in items for array in (left, right)]
    return call(
        functools.partial(
            scatter_body,
            kinds=tuple(kind for kind, _, _ in items),
            order=tuple(order),
            vectors=len(extra),
            quartered=quartered,
        ),
        (1,),
        (bits,),
        [whole(a) for a in (*operands, *extra)],
        [out_whole(shape, BF16)] * (1 if quartered else 2),
        [pltpu.VMEM((768, operands[0].shape[0]), BF16), pltpu.VMEM((768, 768), BF16)]
        + ([pltpu.VMEM((2, 8, 16, 384), F32)] if extra else []),
        flops=sum(2 * left.shape[0] * left.shape[1] * right.shape[1] for _, left, right in items),
        moved=2 * sum(a.size for a in operands) + 4 * math.prod(shape),
    )


def swap(value, axis, bit):
    count = lax.axis_size(axis)
    return lax.ppermute(value, axis, [(i, i ^ (1 << bit)) for i in range(count)])


def shift(value, axis, by):
    count = lax.axis_size(axis)
    pairs = [(i, i + by) for i in range(count) if 0 <= i + by < count]
    return lax.ppermute(value, axis, pairs)


def fold(kept, came):
    low = (kept[1].astype(F32) + came[1].astype(F32)).astype(BF16)
    return low, kept[0].astype(F32) + came[0].astype(F32)


def total_of(terms, *index):
    total = None
    for term in terms:
        value = term[index].astype(F32)
        total = value if total is None else total + value
    return total


def advance(terms, hop):
    came = swap(total_of(terms, 1).astype(BF16), *hop)
    return [term[0] for term in terms], came


def cut(quarters, start, size):
    return quarters[:, :, start : start + size]


def device_step(
    inputs, lengths, cotangent,
    local_query, local_query_bias, local_key, local_value, local_value_bias,
    local_output, local_output_bias, pooled_query, pooled_query_bias,
    pooled_output, pooled_output_bias, conv_key, conv_value, conv_value_bias,
    norm_gain, norm_shift, expand_weight, expand_bias, reduce_weight, reduce_bias,
    final_gain, final_shift,
):
    docs, rows, width = inputs.shape
    devices = lax.axis_size("seq")
    me = lax.axis_index("seq")
    mine = lax.axis_index("batch")
    levels = devices.bit_length() - 1
    size = rows // STRIDE
    flat = docs * rows
    offset = me * rows
    reach = -(-REACH // size)
    gathered = devices <= 2 * reach
    fast = devices == 8 and width == 768 and lax.axis_size("batch") == 4
    base = jnp.where(gathered, 0, offset // STRIDE - reach * size)
    place = jnp.concatenate([offset[None], lengths, base[None]]).astype(jnp.int32)

    def line(vector):
        return vector[None]

    def tokens(array):
        return array.reshape(flat, array.shape[-1])

    taps_key, taps_value = conv_key.T, conv_value.T

    left = shift(inputs[:, rows - HALF :], "seq", 1)
    right = shift(inputs[:, :HALF], "seq", -1)
    q, kx, vx, pooled = project(
        place, inputs, left, right, local_query, line(local_query_bias), local_key, local_value,
        line(local_value_bias), taps_key, taps_value, line(conv_value_bias),
    )
    own = [pooled[:, which][None] for which in range(2)]

    mixes, probs_one = [], []

    def local_step(doc, token):
        mix, probs = local_forward(token, q, kx, vx, doc)
        mixes.append(mix)
        probs_one.append(probs)
        return mix

    if gathered:
        orders = ([2, 1, 0], [0, 2, 1]) if levels == 3 else (list(range(levels)),) * 2
        have = own
        pieces = [[own[0]], [own[1]]]
        relative = [[0], [0]]
        token = place
        for stage in range(levels):
            came = [swap(have[which], "seq", orders[which][stage]) for which in range(2)]
            if stage < docs:
                done = local_step(stage, token)
            else:
                mix_one, middle, middle_low, q2 = middle_forward(
                    token, inputs, local_output, line(local_output_bias), pooled_query,
                    line(pooled_query_bias), mixes,
                )
                done = q2
            came[0], came[1], done, token = sync(came[0], came[1], done, token)
            if stage < docs:
                mixes[stage] = done
            else:
                q2 = done
            for which in range(2):
                pieces[which].append(came[which])
                relative[which] += [r ^ (1 << orders[which][stage]) for r in relative[which]]
                if stage < levels - 1:
                    have[which] = jnp.concatenate([have[which], came[which]])
        slots = jnp.stack([me ^ jnp.array(r, jnp.int32) for r in relative])
    else:
        pieces = [
            [own[which]]
            + [
                shift(own[which], "seq", sign * distance)
                for distance in range(1, reach + 1)
                for sign in (1, -1)
            ]
            for which in range(2)
        ]
        spots = [reach] + [
            reach - sign * distance for distance in range(1, reach + 1) for sign in (1, -1)
        ]
        slots = jnp.array([spots, spots], jnp.int32)
        token = place
        for doc in range(docs):
            local_step(doc, token)
        mix_one, middle, middle_low, q2 = middle_forward(
            token, inputs, local_output, line(local_output_bias), pooled_query,
            line(pooled_query_bias), mixes,
        )

    keys, values, probs_two, mix_two, summed = pooled_forward(
        token, slots, pieces[0], pieces[1], q2, middle, pooled_output, line(pooled_output_bias)
    )
    (
        outputs, normed_low, hidden, grad_branch, grad_pre, grad_summed, grad_second, grad_mix_two,
        vec_feed, vec_wide,
    ) = feed(
        token, summed, cotangent, expand_weight, line(expand_bias), reduce_weight,
        line(reduce_bias), line(norm_gain), line(norm_shift), line(final_gain),
        line(final_shift), pooled_output,
    )

    order_first = [("batch", 1)] + [("seq", level) for level in range(levels)]
    order_last = order_first[1:]

    def bits_of(order):
        ids = [mine & 1] + [(mine if axis == "batch" else me) >> bit & 1 for axis, bit in order]
        return jnp.stack(ids).astype(jnp.int32)

    if fast:
        (feed_blocks,) = scatter_products(
            bits_of(order_first),
            order_first,
            [
                ("wide", normed_low, grad_pre),
                ("tall", grad_branch, hidden),
                ("square", tokens(mix_two), grad_second),
            ],
            quartered=True,
        )
        feed_blocks, grad_mix_two, token = sync(feed_blocks, grad_mix_two, token)
        feed_rows = feed_blocks.shape[-2]
        feed_mine = lax.psum_scatter(
            feed_blocks.reshape(4 * devices * feed_rows, 384),
            "batch",
            scatter_dimension=0,
            tiled=True,
        ).reshape((2,) * levels + (feed_rows, 384))

    blocks = devices if gathered else 2 * reach + 1
    if gathered:
        back = ([0, 1, 2], [1, 2, 0]) if levels == 3 else (list(range(levels)),) * 2
        places = []
        for which in range(2):
            spots = []
            for block in range(devices):
                relative = 0
                for at, bit in enumerate(back[which]):
                    relative |= (block >> (levels - 1 - at) & 1) << bit
                spots.append(relative)
            places.append(me ^ jnp.array(spots, jnp.int32))
        places = jnp.stack(places)
        half_blocks = devices // 2
    else:
        middle_first = [reach] + [spot for spot in range(blocks) if spot != reach]
        places = jnp.array([middle_first, middle_first], jnp.int32)
        half_blocks = 1
    grad_q2, dk_kept, dk_sent, dv_kept, dv_sent = pooled_backward(
        places, token, q2, keys, values, probs_two, grad_mix_two, size, half_blocks
    )
    back_parts = ()

    def back_step(doc, token, earlier):
        return local_backward(token, q, kx, vx, grad_mix_one, probs_one[doc], doc, earlier)

    grad_middle, grad_first, grad_mix_one, vec_first = first_backward(
        token, grad_q2, grad_summed, pooled_query, local_output
    )
    if gathered:
        kept = [part.reshape((2,) * (levels - 1) + part.shape[1:]) for part in (dk_kept, dv_kept)]
        sent = [part.reshape((2,) * (levels - 1) + part.shape[1:]) for part in (dk_sent, dv_sent)]
        for stage in range(levels):
            came = [swap(sent[which], "seq", back[which][stage]) for which in range(2)]
            if stage < docs:
                back_parts = list(back_step(stage, token, back_parts))
                came[0], came[1], back_parts[0], token = sync(
                    came[0], came[1], back_parts[0], token
                )
            if stage < levels - 1:
                for which in range(2):
                    sent[which], kept[which] = fold(kept[which], came[which])
        pooled_grads = [kept[0], came[0], kept[1], came[1]]
    else:
        pooled_grads = []
        for kept, sent in ((dk_kept, dk_sent), (dv_kept, dv_sent)):
            total = kept[0]
            for distance in range(1, reach + 1):
                total = total + shift(sent[reach - distance], "seq", -distance).astype(F32)
                total = total + shift(sent[reach + distance - 1], "seq", distance).astype(F32)
            pooled_grads += [total, jnp.zeros_like(total)]
        for doc in range(docs):
            back_parts = back_step(doc, token, back_parts)
    dq, own_grads, low_left, low_right = back_parts
    from_left = shift(low_right, "seq", 1)
    from_right = shift(low_left, "seq", -1)
    if fast:
        middle_kept, middle_sent = scatter_products(
            bits_of(order_first) + 0 * token[0],
            order_first,
            [
                ("square", tokens(middle_low), tokens(grad_q2)),
                ("square", tokens(mix_one), grad_first),
                ("square", tokens(inputs), tokens(dq)),
            ],
        )
        pooled_grads[1], pooled_grads[3], middle_sent, from_left, from_right, token = sync(
            pooled_grads[1], pooled_grads[3], middle_sent, from_left, from_right, token
        )
    heads = [
        pooled_grads[2 * which][:, :1].astype(F32) + pooled_grads[2 * which + 1][:, :1].astype(F32)
        for which in range(2)
    ]
    after = shift(jnp.stack(heads).astype(BF16), "seq", -1)
    if fast:
        middle_came = swap(middle_sent, "batch", 0)
        after, middle_came, token = sync(after, middle_came, token)
        middle_terms, middle_came = advance([middle_kept, middle_came], order_first[0])
        feed_terms, feed_came = advance([feed_mine], order_first[1])
    grad_k, grad_v, vec_input = key_value_gradients(
        token, pooled_grads, [after[0], after[1]], kx, vx, taps_key, taps_value,
        own_grads, from_left, from_right, dq,
    )
    if fast:
        last_kept, last_sent = scatter_products(
            bits_of(order_last),
            order_last,
            [("square", tokens(inputs), grad_k), ("square", tokens(inputs), grad_v)],
            (vec_feed, vec_first, vec_input, vec_wide),
        )
        last_sent, middle_came, token = sync(last_sent, middle_came, token)
        last_came = swap(last_sent, "batch", 0)
    input_grad = input_gradient(
        token, tokens(dq), grad_k, grad_v, grad_middle, local_query, local_key, local_value
    )

    if fast:
        upper = (mine & 2) > 0
        odd = (mine & 1) > 0

        def pair_up(flag, low, other):
            return jnp.stack([jnp.where(flag, other, low), jnp.where(flag, low, other)])

        input_grad, last_came, feed_came = sync(input_grad, last_came, feed_came)
        cut_at = middle_kept.shape[-2]

        def joined(axis):
            left_part = total_of(middle_terms + [middle_came], 1)
            right_part = total_of(last_terms, 1)
            return jnp.concatenate([left_part, right_part], axis=-2).astype(BF16)

        last_terms = [last_kept, last_came]
        came = swap(joined(0), "seq", 0)
        feed_terms, feed_came = advance(feed_terms + [feed_came], order_first[2])
        came, feed_came = sync(came, feed_came)
        middle_terms = [term[0] for term in middle_terms + [middle_came]] + [
            came[..., :cut_at, :]
        ]
        last_terms = [term[0] for term in last_terms] + [came[..., cut_at:, :]]
        for hop in range(1, levels):
            send = jnp.concatenate(
                [total_of(middle_terms, 1), total_of(last_terms, 1)], axis=-2
            ).astype(BF16)
            came = swap(send, "seq", hop)
            if hop == 1:
                feed_terms, feed_came = advance(feed_terms + [feed_came], order_first[3])
                came, feed_came = sync(came, feed_came)
            if hop == 2:
                feed_low = total_of(feed_terms + [feed_came], Ellipsis).astype(BF16)
                feed_other = swap(feed_low, "batch", 1)
                came, feed_other = sync(came, feed_other)
            middle_terms = [term[0] for term in middle_terms] + [came[..., :cut_at, :]]
            last_terms = [term[0] for term in last_terms] + [came[..., cut_at:, :]]
        final = jnp.concatenate(
            [total_of(middle_terms, Ellipsis), total_of(last_terms, Ellipsis)], axis=-2
        ).astype(BF16)
        other = swap(final, "batch", 1)
        feed_both = pair_up(upper, feed_low, feed_other)
        feed_across = swap(feed_both, "batch", 0)
        other, feed_across = sync(other, feed_across)
        middle_both = pair_up(upper, final[:cut_at], other[:cut_at]).reshape(2 * cut_at, 384)
        last_half = (final[cut_at:].astype(F32) + other[cut_at:].astype(F32)).astype(BF16)
        both = jnp.concatenate([middle_both, last_half])
        across = swap(both, "batch", 0)
        full_feed = pair_up(odd, feed_both, feed_across)
        full = pair_up(odd, both, across)
        full_middle = full[:, : 2 * cut_at].reshape(2, 2, cut_at, 384)
        last = full[:, 2 * cut_at :]
        small = width // devices // 2

        wide = cut(full_feed, 0, 4 * small).reshape(2, 2, 4, small, 384)
        grad_expand = wide.transpose(1, 3, 0, 2, 4).reshape(2 * small, 8 * 384).astype(F32)
        tall = cut(full_feed, 4 * small, 192).reshape(768, 384)
        grad_reduce = tall.T.astype(F32)

        def square(quarters, start):
            block = cut(quarters, start, small).transpose(1, 2, 0, 3)
            return block.reshape(2 * small, 768).astype(F32)

        grad_po = square(full_feed, 4 * small + 192)
        grad_pq, grad_lo, grad_lq = [square(full_middle, index * small) for index in range(3)]
        grad_lk, grad_lv = [
            last[:, index * 96 : index * 96 + 96].transpose(1, 0, 2).reshape(96, 768).astype(F32)
            for index in range(2)
        ]
        lines = last[:, 192:208].astype(F32)
        vec_low, vec_high = lines[0, :, :96], lines[1, :, :96]
        (fg, fs, rb, ng, ns, pob) = [vec_low[index] for index in range(6)]
        pqb, lob = lines[0, 0, LANES : LANES + 96], lines[0, 1, LANES : LANES + 96]
        grad_eb = vec_low[8:12].reshape(-1)
    else:

        def plain(left_array, right_array):
            product = tn(left_array, right_array)
            part = lax.psum_scatter(product, "seq", scatter_dimension=0, tiled=True)
            return lax.psum(part.astype(BF16), "batch").astype(F32)

        grad_expand = plain(normed_low, grad_pre)
        grad_reduce = plain(hidden, grad_branch)
        grad_po = plain(tokens(mix_two), grad_second)
        grad_pq = plain(tokens(middle_low), tokens(grad_q2))
        grad_lo = plain(tokens(mix_one), grad_first)
        grad_lq = plain(tokens(inputs), tokens(dq))
        grad_lk = plain(tokens(inputs), grad_k)
        grad_lv = plain(tokens(inputs), grad_v)
        vectors = jnp.concatenate(
            [vec_feed, vec_first, vec_input, vec_wide.reshape(-1, width)], axis=0
        )
        vectors = lax.psum(vectors, ("seq", "batch"))
        share = width // devices
        part = lax.dynamic_slice_in_dim(vectors, me * share, share, axis=1)
        wide = vectors[32:].reshape(-1)
        wide_share = wide.shape[0] // devices
        grad_eb = lax.dynamic_slice_in_dim(wide, me * wide_share, wide_share, axis=0)
        (fg, fs, rb, ng, ns, pob) = [part[index] for index in range(6)]
        pqb, lob = part[8], part[9]
        vec_high = part[16:32]
    grad_ck = vec_high[:KER].T
    grad_cv = vec_high[KER : 2 * KER].T
    cvb, lqb, lvb = vec_high[10], vec_high[11], vec_high[12]
    return (
        outputs, input_grad,
        grad_lq, lqb, grad_lk, grad_lv, lvb, grad_lo, lob, grad_pq, pqb, grad_po, pob,
        grad_ck, grad_cv, cvb, ng, ns, grad_expand, grad_eb, grad_reduce, rb, fg, fs,
    )


def solution(mesh):
    vector = P("seq")
    matrix = P("seq", None)
    return jax.shard_map(
        device_step,
        mesh=mesh,
        in_specs=(P("batch", "seq", None), P("batch"), P("batch", "seq", None)) + (P(),) * 22,
        out_specs=(
            P("batch", "seq", None), P("batch", "seq", None),
            matrix, vector, matrix, matrix, vector, matrix, vector, matrix, vector, matrix, vector,
            matrix, matrix, vector, vector, vector, matrix, vector, matrix, vector, vector, vector,
        ),
        check_vma=False,
    )
```

time: 541 us -> 390 us (0.72)
  waiting for transfers between devices: 240 us -> 124 us
  Pallas kernels: 160 us -> 119 us
  local copies, waits for them, and re-layouts: 32.9 us -> 73.1 us
  starting transfers between devices: 61.4 us -> 34.4 us
    psum x1 -> x0, waiting for transfers between devices: 115 us -> none  [device_step(): vectors = lax.psum(vectors, ('seq', 'batch'))]
    unnamed x81 -> x207, local copies, waits for them, and re-layouts: 7.47 us -> 54.5 us
    pallas_call x13 -> x15, Pallas kernels: 160 us -> 119 us  [call(): pl.pallas_call(body, grid_spec=pltpu.PrefetchScalarGridSpec(num_scalar_pr...]
    ppermute x33 -> x25, starting transfers between devices: 52.1 us -> 23.2 us  [swap(): return lax.ppermute(value, axis, [(i, i ^ 1 << bit) for i in range(count)])]
    add x7 -> x3, other arithmetic: 12.2 us -> 0.42 us  [the longest x2 0.26 us: fold(): return (low, kept[0].astype(F32) + came[0].astype(F32))]
    another operation x14 -> x18, other arithmetic: 1.68 us -> 9.62 us  [the longest x8 4.44 us: pair_up(): return jnp.stack([jnp.where(flag, other, low), jnp.where(flag, low, other)])]
    ppermute x33 -> x25, waiting for transfers between devices: 121 us -> 116 us  [swap(): return lax.ppermute(value, axis, [(i, i ^ 1 << bit) for i in range(count)])]
  transfers between devices with their start and end apart: 39 -> 31, of which waited for: 17 -> 19; matrix products, arithmetic and copies ran while one was open for 9% -> 6% of each run, Pallas kernels for 17% -> 14%
where the time goes in v2:
time: 390 us; the launch traced here: 384 us
  waiting for transfers between devices  124 us (32%)
  Pallas kernels  119 us (31%)
  local copies, waits for them, and re-layouts  73.1 us (19%)
  starting transfers between devices  34.4 us (9%)
  other arithmetic  18.5 us (5%)
  between operations  15.3 us (4%)
    pallas_call x15, Pallas kernels, call(): pl.pallas_call(body, grid_spec=pltpu.PrefetchScalarGridSpec(num_scalar_pr...  119 us
    ppermute x25, waiting for transfers between devices, swap(): return lax.ppermute(value, axis, [(i, i ^ 1 << bit) for i in range(count)])  116 us
    unnamed x207, local copies, waits for them, and re-layouts  54.5 us
    ppermute x25, starting transfers between devices, swap(): return lax.ppermute(value, axis, [(i, i ^ 1 << bit) for i in range(count)])  23.2 us
    ppermute x5, starting transfers between devices, shift(): return lax.ppermute(value, axis, pairs)  11.1 us
    broadcast_in_dim x11, local copies, waits for them, and re-layouts, line(): return vector[None]  8.41 us
    ppermute x5, waiting for transfers between devices, shift(): return lax.ppermute(value, axis, pairs)  8.02 us
  transfers between devices with their start and end apart: 31, of which 19 were waited for; matrix products, arithmetic and copies ran while one was open for 6% of the time, Pallas kernels for 14%

profile of v2, /device:TPU:1, one launch (start us, length us, event | category | flops | bytes accessed | tf_op | source)
XLA Modules:
  0.0 384.4 jit_solution(4749307097592319627)
XLA Ops:
  9.7 4.6 %collective-permute-start = (bf16[2,64,768]{2,1,0:T(8,128)(2,1)S(1)}, bf16[2,64,768]{2,1,0:T(8,128)(2,1)S(1)}, u32[]{:S(2)}, u32[]{:S(2)}) collective-permute-start(bf16[2,64,768]{2,1,0:T(8,128)(2,1)S(1)} %get-tuple-element.327), channel_id=1, source_target_pairs={{0,4},{4,8},{8,12},{12,16},{16,20},{20,24},{24,28},{1,5},{5,9},{9,... | collective-permute-start | bytes 589832 | tf_op jit(solution)/shard_map/ppermute | solution.py:870
  17.1 5.0 %collective-permute-done.left = bf16[2,64,768]{2,1,0:T(8,128)(2,1)S(1)} collective-permute-done((bf16[2,64,768]{2,1,0:T(8,128)(2,1)S(1)}, bf16[2,64,768]{2,1,0:T(8,128)(2,1)S(1)}, u32[]{:S(2)}, u32[]{:S(2)}) %collective-permute-start) | collective-permute-done | bytes 196640 | tf_op jit(solution)/shard_map/ppermute | solution.py:870
  35.7 4.8 %shard_map.461 = (bf16[256,768]{1,0:T(8,128)(2,1)S(1)}, f32[6,2,256,256]{3,2,1,0:T(8,128)S(1)}) custom-call(s32[4]{0:T(128)S(1)} %pad_add_fusion.1.place.token, bf16[2,256,768]{2,1,0:T(8,128)(2,1)S(1)} %get-tuple-element.122.q, bf16[2,384,768]{2,1,0:T(8,128)(2,1)S(1)} %get-tuple-element.123.kx.refs_6_, bf16[2,384,768]{2,1,0:T(8,128)(2,1)S(1)} %get-tuple-element.124.vx.refs_7_), custom_call_target="tpu_custom_call" | custom-call | flops 1000 | bytes 1000 | tf_op jit(solution)/shard_map/pallas_call | solution.py:61
  45.6 4.8 %shard_map.462 = (bf16[256,768]{1,0:T(8,128)(2,1)S(1)}, f32[6,2,256,256]{3,2,1,0:T(8,128)S(1)}) custom-call(s32[4]{0:T(128)S(1)} %pad_add_fusion.1.place.token, bf16[2,256,768]{2,1,0:T(8,128)(2,1)S(1)} %get-tuple-element.122.q, bf16[2,384,768]{2,1,0:T(8,128)(2,1)S(1)} %get-tuple-element.123.kx.refs_6_, bf16[2,384,768]{2,1,0:T(8,128)(2,1)S(1)} %get-tuple-element.124.vx.refs_7_), custom_call_target="tpu_custom_call" | custom-call | flops 1000 | bytes 1000 | tf_op jit(solution)/shard_map/pallas_call | solution.py:61
  52.8 10.6 %collective-permute-done.5.refs_6_ = bf16[2,2,64,768]{3,2,1,0:T(8,128)(2,1)S(1)} collective-permute-done((bf16[2,2,64,768]{3,2,1,0:T(8,128)(2,1)S(1)}, bf16[2,2,64,768]{3,2,1,0:T(8,128)(2,1)S(1)}, u32[]{:S(2)}, u32[]{:S(2)}) %collective-permute-start.5) | collective-permute-done | bytes 393248 | tf_op jit(solution)/shard_map/ppermute | solution.py:864
  83.8 18.9 %shard_map.464 = (bf16[2,512,768]{2,1,0:T(8,128)(2,1)S(1)}, bf16[2,512,768]{2,1,0:T(8,128)(2,1)S(1)}, f32[2,6,2,512,256]{4,3,2,1,0:T(8,128)S(1)}, bf16[2,256,768]{2,1,0:T(8,128)(2,1)S(1)}, f32[2,256,768]{2,1,0:T(8,128)S(1)}) custom-call(s32[4]{0:T(128)S(1)} %pad_add_fusion.1.place.token, s32[2,8]{1,0:T(2,128)S(1)} %pad_add_fusion.slots.places, ...), custom_call_target="tpu_custom_call" | custom-call | flops 1000 | bytes 1000 | tf_op jit(solution)/shard_map/pallas_call | solution.py:61
  102.7 4.6 %copy-done.2 = f32[2,6,2,512,256]{4,3,2,1,0:T(8,128)} copy-done((f32[2,6,2,512,256]{4,3,2,1,0:T(8,128)}, f32[2,6,2,512,256]{4,3,2,1,0:T(8,128)S(1)}, u32[]{:S(2)}) %copy-start.2) | copy-done | bytes 12582936
  109.7 36.6 %shard_map.465 = (bf16[2,256,768]{2,1,0:T(8,128)(2,1)}, bf16[512,768]{1,0:T(8,128)(2,1)S(1)}, bf16[512,3072]{1,0:T(8,128)(2,1)S(1)}, bf16[512,768]{1,0:T(8,128)(...) custom-call(s32[4]{0:T(128)S(1)} %pad_add_fusion.1.place.token, ...), custom_call_target="tpu_custom_call" | custom-call | flops 1000 | bytes 1000 | tf_op jit(solution)/shard_map/pallas_call | solution.py:61
  149.6 7.6 %shard_map.466 = bf16[2,2,2,2,2,432,384]{6,5,4,3,2,1,0:T(8,128)(2,1)S(1)} custom-call(s32[5]{0:T(128)S(1)} %copy-done.86, bf16[512,768]{1,0:T(8,128)(2,1)S(1)} %get-tuple-element.143.refs_0_, bf16[512,3072]{1,0:T(8,128)(2,1)S(1)} %copy-done.25, bf16[512,768]{1,0:T(8,128)(2,1)S(1)} %get-tuple-element.145.refs_2_, ...), custom_call_target="tpu_custom_call" | custom-call | flops 1000 | bytes 1000 | tf_op jit(solution)/shard_map/pallas_call | solution.py:61
  161.9 4.6 %copy-done.3 = f32[2,6,2,512,256]{4,3,2,1,0:T(8,128)S(1)} copy-done((f32[2,6,2,512,256]{4,3,2,1,0:T(8,128)S(1)}, f32[2,6,2,512,256]{4,3,2,1,0:T(8,128)}, u32[]{:S(2)}) %copy-start.3) | copy-done | bytes 12582936
  172.3 18.4 %shard_map.467 = (bf16[2,256,768]{2,1,0:T(8,128)(2,1)S(1)}, f32[4,2,64,768]{3,2,1,0:T(8,128)S(1)}, bf16[4,2,64,768]{3,2,1,0:T(8,128)(2,1)S(1)}, f32[4,2,64,768]{3,2,1,0:T(8,128)S(1)}, bf16[4,2,64,768]{3,2,1,0:T(8,128)(2,1)S(1)}) custom-call(s32[2,8]{1,0:T(2,128)S(1)} %copy-done.85, s32[4]{0:T(128)S(1)} %pad_add_fusion.1.place.token, ...), custom_call_target="tpu_custom_call" | custom-call | flops 1000 | bytes 1000 | tf_op jit(solution)/shard_map/pallas_call | solution.py:61
  196.0 4.5 %shard_map.469 = (bf16[1,256,768]{2,1,0:T(8,128)(2,1)S(1)}, f32[1,2,256,768]{3,2,1,0:T(8,128)S(1)}, bf16[1,2,64,768]{3,2,1,0:T(8,128)(2,1)S(1)}, bf16[1,2,64,768]{3,2,1,0:T(8,128)(2,1)S(1)}) custom-call(s32[4]{0:T(128)S(1)} %pad_add_fusion.1.place.token, bf16[2,256,768]{2,1,0:T(8,128)(2,1)S(1)} %copy-done.5, ...), custom_call_target="tpu_custom_call" | custom-call | flops 1000 | bytes 1000 | tf_op jit(solution)/shard_map/pallas_call | solution.py:61
  200.5 7.1 %collective-permute-done.8 = bf16[2,2,2,64,768]{4,3,2,1,0:T(8,128)(2,1)S(1)} collective-permute-done((bf16[2,2,2,64,768]{4,3,2,1,0:T(8,128)(2,1)S(1)}, bf16[2,2,2,64,768]{4,3,2,1,0:T(8,128)(2,1)S(1)}, u32[]{:S(2)}, u32[]{:S(2)}) %collective-permute-start.8) | collective-permute-done | bytes 786464 | tf_op jit(solution)/shard_map/ppermute | solution.py:864
  212.1 4.6 %shard_map.470 = (bf16[2,256,768]{2,1,0:T(8,128)(2,1)S(1)}, f32[2,2,256,768]{3,2,1,0:T(8,128)S(1)}, bf16[2,2,64,768]{3,2,1,0:T(8,128)(2,1)S(1)}, bf16[2,2,64,768]{3,2,1,0:T(8,128)(2,1)S(1)}) custom-call(s32[4]{0:T(128)S(1)} %pad_add_fusion.1.place.token, bf16[2,256,768]{2,1,0:T(8,128)(2,1)S(1)} %copy-done.5, ...), custom_call_target="tpu_custom_call" | custom-call | flops 1000 | bytes 1000 | tf_op jit(solution)/shard_map/pallas_call | solution.py:61
  230.6 8.7 %collective-permute-done.13.refs_3_ = bf16[2,64,768]{2,1,0:T(8,128)(2,1)S(1)} collective-permute-done((bf16[2,64,768]{2,1,0:T(8,128)(2,1)S(1)}, bf16[2,64,768]{2,1,0:T(8,128)(2,1)S(1)}, u32[]{:S(2)}, u32[]{:S(2)}) %collective-permute-start.13) | collective-permute-done | bytes 196640 | tf_op jit(solution)/shard_map/ppermute | solution.py:864
  239.3 7.2 %collective-permute-done.12.refs_1_ = bf16[2,64,768]{2,1,0:T(8,128)(2,1)S(1)} collective-permute-done((bf16[2,64,768]{2,1,0:T(8,128)(2,1)S(1)}, bf16[2,64,768]{2,1,0:T(8,128)(2,1)S(1)}, u32[]{:S(2)}, u32[]{:S(2)}) %collective-permute-start.12) | collective-permute-done | bytes 196640 | tf_op jit(solution)/shard_map/ppermute | solution.py:864
  265.7 10.0 %collective-permute-done.18 = bf16[2,2,2,144,384]{4,3,2,1,0:T(8,128)(2,1)} collective-permute-done((bf16[2,2,2,144,384]{4,3,2,1,0:T(8,128)(2,1)}, bf16[2,2,2,144,384]{4,3,2,1,0:T(8,128)(2,1)}, u32[]{:S(2)}, u32[]{:S(2)}) %collective-permute-start.18) | collective-permute-done | bytes 884768 | tf_op jit(solution)/shard_map/ppermute | solution.py:864
  282.6 5.0 %collective-permute-done.20 = bf16[2,2,432,384]{3,2,1,0:T(8,128)(2,1)S(1)} collective-permute-done((bf16[2,2,432,384]{3,2,1,0:T(8,128)(2,1)S(1)}, bf16[2,2,432,384]{3,2,1,0:T(8,128)(2,1)S(1)}, u32[]{:S(2)}, u32[]{:S(2)}) %collective-permute-start.20) | collective-permute-done | bytes 1327136 | tf_op jit(solution)/shard_map/ppermute | solution.py:864
  289.3 13.8 %collective-permute-done.22 = bf16[2,432,384]{2,1,0:T(8,128)(2,1)S(1)} collective-permute-done((bf16[2,432,384]{2,1,0:T(8,128)(2,1)S(1)}, bf16[2,432,384]{2,1,0:T(8,128)(2,1)S(1)}, u32[]{:S(2)}, u32[]{:S(2)}) %collective-permute-start.22) | collective-permute-done | bytes 663584 | tf_op jit(solution)/shard_map/ppermute | solution.py:864
  303.2 7.8 %collective-permute-done.21 = bf16[2,2,352,384]{3,2,1,0:T(8,128)(2,1)S(1)} collective-permute-done((bf16[2,2,352,384]{3,2,1,0:T(8,128)(2,1)S(1)}, bf16[2,2,352,384]{3,2,1,0:T(8,128)(2,1)S(1)}, u32[]{:S(2)}, u32[]{:S(2)}) %collective-permute-start.21) | collective-permute-done | bytes 1081376 | tf_op jit(solution)/shard_map/ppermute | solution.py:864
  314.8 13.7 %collective-permute-done.24 = bf16[432,384]{1,0:T(8,128)(2,1)S(1)} collective-permute-done((bf16[432,384]{1,0:T(8,128)(2,1)S(1)}, bf16[432,384]{1,0:T(8,128)(2,1)S(1)}, u32[]{:S(2)}, u32[]{:S(2)}) %collective-permute-start.24) | collective-permute-done | bytes 331808 | tf_op jit(solution)/shard_map/ppermute | solution.py:864
  328.4 4.0 %collective-permute-done.23 = bf16[2,352,384]{2,1,0:T(8,128)(2,1)S(1)} collective-permute-done((bf16[2,352,384]{2,1,0:T(8,128)(2,1)S(1)}, bf16[2,352,384]{2,1,0:T(8,128)(2,1)S(1)}, u32[]{:S(2)}, u32[]{:S(2)}) %collective-permute-start.23) | collective-permute-done | bytes 540704 | tf_op jit(solution)/shard_map/ppermute | solution.py:864
  334.5 13.3 %collective-permute-done.25 = bf16[352,384]{1,0:T(8,128)(2,1)S(1)} collective-permute-done((bf16[352,384]{1,0:T(8,128)(2,1)S(1)}, bf16[352,384]{1,0:T(8,128)(2,1)S(1)}, u32[]{:S(2)}, u32[]{:S(2)}) %collective-permute-start.25) | collective-permute-done | bytes 270368 | tf_op jit(solution)/shard_map/ppermute | solution.py:864
  354.4 6.9 %collective-permute-done.27 = bf16[352,384]{1,0:T(8,128)(2,1)S(1)} collective-permute-done((bf16[352,384]{1,0:T(8,128)(2,1)S(1)}, bf16[352,384]{1,0:T(8,128)(2,1)S(1)}, u32[]{:S(2)}, u32[]{:S(2)}) %collective-permute-start.27) | collective-permute-done | bytes 270368 | tf_op jit(solution)/shard_map/ppermute | solution.py:864
  (340 shorter events, 142.0 us)
Async XLA Ops:
  7.2 249.5 %reduce-scatter.2.cloned.1.call-start = ((), (), s32[]{:S(2)}) async-start(), calls=%async_computation.1 | async-start | bytes 13271040 | tf_op jit(solution)/shard_map/reduce_scatter | solution.py:1022
  9.7 12.4 %collective-permute-start = (bf16[2,64,768]{2,1,0:T(8,128)(2,1)S(1)}, bf16[2,64,768]{2,1,0:T(8,128)(2,1)S(1)}, u32[]{:S(2)}, u32[]{:S(2)}) collective-permute-start(bf16[2,64,768]{2,1,0:T(8,128)(2,1)S(1)} %get-tuple-element.327), channel_id=1, source_target_pairs={{0,4},{4,8},{8,12},{12,16},{16,20},{20,24},{24,28},{1,5},{5,9},{9,... | collective-permute-start | bytes 589832 | tf_op jit(solution)/shard_map/ppermute | solution.py:870
  31.1 11.1 %collective-permute-start.3 = (bf16[1,2,64,768]{3,2,1,0:T(8,128)(2,1)S(1)}, bf16[1,2,64,768]{3,2,1,0:T(8,128)(2,1)S(1)}, u32[]{:S(2)}, u32[]{:S(2)}) collective-permute-start(bf16[1,2,64,768]{3,2,1,0:T(8,128)(2,1)S(1)} %get-tuple-element.337.refs_4_), channel_id=1, source_target_pairs={{0,4},{4,0},{8,12},{12,8},{16,20},{20,16},{24,28},{28,24},{1,5},{5... | collective-permute-start | bytes 589832 | tf_op jit(solution)/shard_map/ppermute | solution.py:864
  33.3 10.9 %collective-permute-start.2 = (bf16[1,2,64,768]{3,2,1,0:T(8,128)(2,1)S(1)}, bf16[1,2,64,768]{3,2,1,0:T(8,128)(2,1)S(1)}, u32[]{:S(2)}, u32[]{:S(2)}) collective-permute-start(bf16[1,2,64,768]{3,2,1,0:T(8,128)(2,1)S(1)} %get-tuple-element.338.refs_0_), channel_id=1, source_target_pairs={{0,16},{4,20},{8,24},{12,28},{16,0},{20,4},{24,8},{28,12},{1,17},{... | collective-permute-start | bytes 589832 | tf_op jit(solution)/shard_map/ppermute | solution.py:864
  44.3 19.0 %collective-permute-start.5 = (bf16[2,2,64,768]{3,2,1,0:T(8,128)(2,1)S(1)}, bf16[2,2,64,768]{3,2,1,0:T(8,128)(2,1)S(1)}, u32[]{:S(2)}, u32[]{:S(2)}) collective-permute-start(bf16[2,2,64,768]{3,2,1,0:T(8,128)(2,1)S(1)} %pad_maximum_fusion.8), channel_id=1, source_target_pairs={{0,16},{4,20},{8,24},{12,28},{16,0},{20,4},{24,8},{28,12},{1,17},{... | collective-permute-start | bytes 1179656 | tf_op jit(solution)/shard_map/ppermute | solution.py:864
  44.4 19.0 %collective-permute-start.4 = (bf16[2,2,64,768]{3,2,1,0:T(8,128)(2,1)S(1)}, bf16[2,2,64,768]{3,2,1,0:T(8,128)(2,1)S(1)}, u32[]{:S(2)}, u32[]{:S(2)}) collective-permute-start(bf16[2,2,64,768]{3,2,1,0:T(8,128)(2,1)S(1)} %pad_maximum_fusion.7), channel_id=1, source_target_pairs={{0,8},{4,12},{8,0},{12,4},{16,24},{20,28},{24,16},{28,20},{1,9},{5... | collective-permute-start | bytes 1179656 | tf_op jit(solution)/shard_map/ppermute | solution.py:864
  65.3 18.3 %collective-permute-start.7 = (bf16[4,2,64,768]{3,2,1,0:T(8,128)(2,1)}, bf16[4,2,64,768]{3,2,1,0:T(8,128)(2,1)}, u32[]{:S(2)}, u32[]{:S(2)}) collective-permute-start(bf16[4,2,64,768]{3,2,1,0:T(8,128)(2,1)} %pad_maximum_fusion.2), channel_id=1, source_target_pairs={{0,8},{4,12},{8,0},{12,4},{16,24},{20,28},{24,16},{28,20},{1,9},{5... | collective-permute-start | bytes 2359304 | tf_op jit(solution)/shard_map/ppermute | solution.py:864
  65.4 18.3 %collective-permute-start.6 = (bf16[4,2,64,768]{3,2,1,0:T(8,128)(2,1)}, bf16[4,2,64,768]{3,2,1,0:T(8,128)(2,1)}, u32[]{:S(2)}, u32[]{:S(2)}) collective-permute-start(bf16[4,2,64,768]{3,2,1,0:T(8,128)(2,1)} %pad_maximum_fusion.1), channel_id=1, source_target_pairs={{0,4},{4,0},{8,12},{12,8},{16,20},{20,16},{24,28},{28,24},{1,5},{5... | collective-permute-start | bytes 2359304 | tf_op jit(solution)/shard_map/ppermute | solution.py:864
  190.7 16.9 %collective-permute-start.8 = (bf16[2,2,2,64,768]{4,3,2,1,0:T(8,128)(2,1)S(1)}, bf16[2,2,2,64,768]{4,3,2,1,0:T(8,128)(2,1)S(1)}, u32[]{:S(2)}, u32[]{:S(2)}) collective-permute-start(bf16[2,2,2,64,768]{4,3,2,1,0:T(8,128)(2,1)S(1)} %bitcast.235), channel_id=1, source_target_pairs={{0,4},{4,0},{8,12},{12,8},{16,20},{20,16},{24,28},{28,24},{1,5},{5... | collective-permute-start | bytes 2359304 | tf_op jit(solution)/shard_map/ppermute | solution.py:864
  191.3 17.2 %collective-permute-start.9 = (bf16[2,2,2,64,768]{4,3,2,1,0:T(8,128)(2,1)S(1)}, bf16[2,2,2,64,768]{4,3,2,1,0:T(8,128)(2,1)S(1)}, u32[]{:S(2)}, u32[]{:S(2)}) collective-permute-start(bf16[2,2,2,64,768]{4,3,2,1,0:T(8,128)(2,1)S(1)} %bitcast.234), channel_id=1, source_target_pairs={{0,8},{4,12},{8,0},{12,4},{16,24},{20,28},{24,16},{28,20},{1,9},{5... | collective-permute-start | bytes 2359304 | tf_op jit(solution)/shard_map/ppermute | solution.py:864
  208.7 17.2 %collective-permute-start.10 = (bf16[2,2,64,768]{3,2,1,0:T(8,128)(2,1)S(1)}, bf16[2,2,64,768]{3,2,1,0:T(8,128)(2,1)S(1)}, u32[]{:S(2)}, u32[]{:S(2)}) collective-permute-start(bf16[2,2,64,768]{3,2,1,0:T(8,128)(2,1)S(1)} %get-tuple-element.315), channel_id=1, source_target_pairs={{0,8},{4,12},{8,0},{12,4},{16,24},{20,28},{24,16},{28,20},{1,9},{5... | collective-permute-start | bytes 1179656 | tf_op jit(solution)/shard_map/ppermute | solution.py:864
  210.1 15.8 %collective-permute-start.11 = (bf16[2,2,64,768]{3,2,1,0:T(8,128)(2,1)S(1)}, bf16[2,2,64,768]{3,2,1,0:T(8,128)(2,1)S(1)}, u32[]{:S(2)}, u32[]{:S(2)}) collective-permute-start(bf16[2,2,64,768]{3,2,1,0:T(8,128)(2,1)S(1)} %get-tuple-element.316), channel_id=1, source_target_pairs={{0,16},{4,20},{8,24},{12,28},{16,0},{20,4},{24,8},{28,12},{1,17},{... | collective-permute-start | bytes 1179656 | tf_op jit(solution)/shard_map/ppermute | solution.py:864
  218.4 12.0 %collective-permute-start.14 = (bf16[2,2,64,768]{3,2,1,0:T(8,128)(2,1)S(1)}, bf16[2,2,64,768]{3,2,1,0:T(8,128)(2,1)S(1)}, u32[]{:S(2)}, u32[]{:S(2)}) collective-permute-start(bf16[2,2,64,768]{3,2,1,0:T(8,128)(2,1)S(1)} %get-tuple-element.180), channel_id=1, source_target_pairs={{0,4},{4,8},{8,12},{12,16},{16,20},{20,24},{24,28},{1,5},{5,9},{9,... | collective-permute-start | bytes 1179656 | tf_op jit(solution)/shard_map/ppermute | solution.py:870
  226.0 13.3 %collective-permute-start.13 = (bf16[2,64,768]{2,1,0:T(8,128)(2,1)S(1)}, bf16[2,64,768]{2,1,0:T(8,128)(2,1)S(1)}, u32[]{:S(2)}, u32[]{:S(2)}) collective-permute-start(bf16[2,64,768]{2,1,0:T(8,128)(2,1)S(1)} %get-tuple-element.324), channel_id=1, source_target_pairs={{0,4},{4,0},{8,12},{12,8},{16,20},{20,16},{24,28},{28,24},{1,5},{5... | collective-permute-start | bytes 589832 | tf_op jit(solution)/shard_map/ppermute | solution.py:864
  226.6 19.9 %collective-permute-start.12 = (bf16[2,64,768]{2,1,0:T(8,128)(2,1)S(1)}, bf16[2,64,768]{2,1,0:T(8,128)(2,1)S(1)}, u32[]{:S(2)}, u32[]{:S(2)}) collective-permute-start(bf16[2,64,768]{2,1,0:T(8,128)(2,1)S(1)} %get-tuple-element.323), channel_id=1, source_target_pairs={{0,16},{4,20},{8,24},{12,28},{16,0},{20,4},{24,8},{28,12},{1,17},{... | collective-permute-start | bytes 589832 | tf_op jit(solution)/shard_map/ppermute | solution.py:864
  255.3 20.4 %collective-permute-start.18 = (bf16[2,2,2,144,384]{4,3,2,1,0:T(8,128)(2,1)}, bf16[2,2,2,144,384]{4,3,2,1,0:T(8,128)(2,1)}, u32[]{:S(2)}, u32[]{:S(2)}) collective-permute-start(bf16[2,2,2,144,384]{4,3,2,1,0:T(8,128)(2,1)} %fusion.1), channel_id=1, source_target_pairs={{0,2},{1,3},{2,0},{3,1},{4,6},{5,7},{6,4},{7,5},{8,10},{9,11},{10,... | collective-permute-start | bytes 2654216 | tf_op jit(solution)/shard_map/ppermute | solution.py:864
  258.4 29.2 %collective-permute-start.20 = (bf16[2,2,432,384]{3,2,1,0:T(8,128)(2,1)S(1)}, bf16[2,2,432,384]{3,2,1,0:T(8,128)(2,1)S(1)}, u32[]{:S(2)}, u32[]{:S(2)}) collective-permute-start(bf16[2,2,432,384]{3,2,1,0:T(8,128)(2,1)S(1)} %bitcast.241), channel_id=1, source_target_pairs={{0,4},{4,0},{8,12},{12,8},{16,20},{20,16},{24,28},{28,24},{1,5},{5... | collective-permute-start | bytes 3981320 | tf_op jit(solution)/shard_map/ppermute | solution.py:864
  287.9 23.1 %collective-permute-start.21 = (bf16[2,2,352,384]{3,2,1,0:T(8,128)(2,1)S(1)}, bf16[2,2,352,384]{3,2,1,0:T(8,128)(2,1)S(1)}, u32[]{:S(2)}, u32[]{:S(2)}) collective-permute-start(bf16[2,2,352,384]{3,2,1,0:T(8,128)(2,1)S(1)} %pad_maximum_fusion), channel_id=1, source_target_pairs={{0,4},{4,0},{8,12},{12,8},{16,20},{20,16},{24,28},{28,24},{1,5},{5... | collective-permute-start | bytes 3244040 | tf_op jit(solution)/shard_map/ppermute | solution.py:864
  289.0 14.1 %collective-permute-start.22 = (bf16[2,432,384]{2,1,0:T(8,128)(2,1)S(1)}, bf16[2,432,384]{2,1,0:T(8,128)(2,1)S(1)}, u32[]{:S(2)}, u32[]{:S(2)}) collective-permute-start(bf16[2,432,384]{2,1,0:T(8,128)(2,1)S(1)} %fusion), channel_id=1, source_target_pairs={{0,8},{4,12},{8,0},{12,4},{16,24},{20,28},{24,16},{28,20},{1,9},{5... | collective-permute-start | bytes 1990664 | tf_op jit(solution)/shard_map/ppermute | solution.py:864
  312.8 19.7 %collective-permute-start.23 = (bf16[2,352,384]{2,1,0:T(8,128)(2,1)S(1)}, bf16[2,352,384]{2,1,0:T(8,128)(2,1)S(1)}, u32[]{:S(2)}, u32[]{:S(2)}) collective-permute-start(bf16[2,352,384]{2,1,0:T(8,128)(2,1)S(1)} %pad_maximum_fusion.6), channel_id=1, source_target_pairs={{0,8},{4,12},{8,0},{12,4},{16,24},{20,28},{24,16},{28,20},{1,9},{5... | collective-permute-start | bytes 1622024 | tf_op jit(solution)/shard_map/ppermute | solution.py:864
  313.5 15.0 %collective-permute-start.24 = (bf16[432,384]{1,0:T(8,128)(2,1)S(1)}, bf16[432,384]{1,0:T(8,128)(2,1)S(1)}, u32[]{:S(2)}, u32[]{:S(2)}) collective-permute-start(bf16[432,384]{1,0:T(8,128)(2,1)S(1)} %fusion.7), channel_id=1, source_target_pairs={{0,16},{4,20},{8,24},{12,28},{16,0},{20,4},{24,8},{28,12},{1,17},{... | collective-permute-start | bytes 995336 | tf_op jit(solution)/shard_map/ppermute | solution.py:864
  334.0 14.5 %collective-permute-start.26 = (bf16[432,384]{1,0:T(8,128)(2,1)S(1)}, bf16[432,384]{1,0:T(8,128)(2,1)S(1)}, u32[]{:S(2)}, u32[]{:S(2)}) collective-permute-start(bf16[432,384]{1,0:T(8,128)(2,1)S(1)} %fusion.6), channel_id=1, source_target_pairs={{0,2},{1,3},{2,0},{3,1},{4,6},{5,7},{6,4},{7,5},{8,10},{9,11},{10,... | collective-permute-start | bytes 995336 | tf_op jit(solution)/shard_map/ppermute | solution.py:864
  334.4 13.4 %collective-permute-start.25 = (bf16[352,384]{1,0:T(8,128)(2,1)S(1)}, bf16[352,384]{1,0:T(8,128)(2,1)S(1)}, u32[]{:S(2)}, u32[]{:S(2)}) collective-permute-start(bf16[352,384]{1,0:T(8,128)(2,1)S(1)} %pad_maximum_fusion.10), channel_id=1, source_target_pairs={{0,16},{4,20},{8,24},{12,28},{16,0},{20,4},{24,8},{28,12},{1,17},{... | collective-permute-start | bytes 811016 | tf_op jit(solution)/shard_map/ppermute | solution.py:864
  349.5 11.8 %collective-permute-start.28 = (bf16[2,432,384]{2,1,0:T(8,128)(2,1)}, bf16[2,432,384]{2,1,0:T(8,128)(2,1)}, u32[]{:S(2)}, u32[]{:S(2)}) collective-permute-start(bf16[2,432,384]{2,1,0:T(8,128)(2,1)} %pad_maximum_fusion.3), channel_id=1, source_target_pairs={{0,1},{1,0},{2,3},{3,2},{4,5},{5,4},{6,7},{7,6},{8,9},{9,8},{10,11... | collective-permute-start | bytes 1990664 | tf_op jit(solution)/shard_map/ppermute | solution.py:864
  (108 other events, 854.0 us)
Sparse Core Ops, SparseCore 0:
  161.3 86.9 reduce-scatter.1

commit v3 on v2

--- a/solution.py
+++ b/solution.py
@@ -43,21 +43,31 @@
     return jnp.sum(block.astype(F32), axis=0, keepdims=True)
 
 
-def call(body, grid, scalars, inputs, outputs, scratch=(), flops=0, moved=0, exps=0, spare=6):
-    single = math.prod(grid) == 1
+def call(body, grid, scalars, inputs, outputs, scratch=(), spare=8):
     used = spare * 2**20
+    arrays, in_specs, out_specs, shapes = [], [], [], []
 
     def spec(shape, dtype, block, index):
         nonlocal used
-        fixed = single or tuple(block) == tuple(shape)
-        used += math.prod(block) * jnp.dtype(dtype).itemsize * (1 if fixed else 2)
-        mode = pl.Buffered(1) if fixed else None
-        return pl.BlockSpec(block, index, pipeline_mode=mode)
-
-    in_specs = [spec(a.shape, a.dtype, block, index) for a, block, index in inputs]
-    out_specs = [spec(shape, dtype, block, index) for shape, dtype, block, index in outputs]
+        if block is None:
+            return pl.BlockSpec(memory_space=pltpu.VMEM)
+        if block == "raw":
+            return pl.BlockSpec(memory_space=pl.ANY)
+        used += 2 * math.prod(block) * jnp.dtype(dtype).itemsize
+        return pl.BlockSpec(block, index)
+
+    for array, block, index in inputs:
+        in_specs.append(spec(array.shape, array.dtype, block, index))
+        if block is not None:
+            array = pltpu.with_memory_space_constraint(array, pltpu.HBM)
+        arrays.append(array)
+    for shape, dtype, block, index in outputs:
+        out_specs.append(spec(shape, dtype, block, index))
+        plain = block is None
+        shapes.append((jax.ShapeDtypeStruct if plain else pltpu.HBM)(shape, dtype))
     for item in scratch:
-        used += math.prod(item.shape) * jnp.dtype(item.dtype).itemsize
+        if hasattr(item, "shape") and item.memory_space == pltpu.VMEM:
+            used += math.prod(item.shape) * jnp.dtype(item.dtype).itemsize
     return pl.pallas_call(
         body,
         grid_spec=pltpu.PrefetchScalarGridSpec(
@@ -67,37 +77,28 @@
             out_specs=out_specs,
             scratch_shapes=list(scratch),
         ),
-        out_shape=[jax.ShapeDtypeStruct(shape, dtype) for shape, dtype, _, _ in outputs],
+        out_shape=shapes,
         compiler_params=pltpu.CompilerParams(
             dimension_semantics=("arbitrary",) * len(grid), vmem_limit_bytes=used
         ),
         cost_estimate=pl.CostEstimate(flops=1000, bytes_accessed=1000, transcendentals=0),
-    )(*scalars, *[array for array, _, _ in inputs])
+    )(*scalars, *arrays)
+
+
+def raw(array):
+    return (array, "raw", None)
+
+
+def out_raw(shape, dtype):
+    return (shape, dtype, "raw", None)
 
 
 def whole(array):
-    zeros = (0,) * array.ndim
-    return (array, array.shape, lambda *_: zeros)
-
-
-def by_doc(array):
-    zeros = (0,) * (array.ndim - 1)
-    return (array, (1,) + array.shape[1:], lambda doc, *_: (doc,) + zeros)
-
-
-def one_doc(array, doc):
-    zeros = (0,) * (array.ndim - 1)
-    return (array, (1,) + array.shape[1:], lambda *_: (doc,) + zeros)
-
-
-def out_doc(shape, dtype):
-    zeros = (0,) * (len(shape) - 1)
-    return (shape, dtype, (1,) + tuple(shape[1:]), lambda doc, *_: (doc,) + zeros)
+    return (array, None, None)
 
 
 def out_whole(shape, dtype):
-    zeros = (0,) * len(shape)
-    return (shape, dtype, shape, lambda *_: zeros)
+    return (shape, dtype, None, None)
 
 
 def sync(*values):
@@ -121,53 +122,73 @@
     return lax.broadcasted_iota(jnp.int32, shape, dim)
 
 
-def project_body(place, x, left, right, wq, bq, wk, wv, bv, ck, cv, bcv, q, kx, vx, pooled, rows):
-    doc = pl.program_id(0)
-    offset, length = place[0], place[1 + doc]
-    own = x[0]
-    q[0] = (nn(own, wq[...]) + bq[...]).astype(BF16)
-    extended = jnp.concatenate([left[0], own, right[0]], axis=0)
-    spot = offset - HALF + positions((extended.shape[0], 1), 0)
-    valid = (spot >= 0) & (spot < length)
+def project_body(place, x, wq, bq, wk, wv, bv, q, k, v):
+    docs, rows, width = x.shape
+    flat = x[...].reshape(docs * rows, width)
+    q[...] = (nn(flat, wq[...]) + bq[...]).astype(BF16).reshape(q.shape)
+    k[...] = nn(flat, wk[...]).astype(BF16).reshape(k.shape)
+    v[...] = (nn(flat, wv[...]) + bv[...]).astype(BF16).reshape(v.shape)
+
+
+def project(place, x, wq, bq, wk, wv, bv):
+    return call(
+        project_body,
+        (1,),
+        (place,),
+        [whole(a) for a in (x, wq, bq, wk, wv, bv)],
+        [out_whole(x.shape, BF16)] * 3,
+    )
+
+
+def pool_body(place, left, right, k, v, wk, wv, bv, ck, cv, bcv, kx, vx, pooled, rows):
+    offset = place[0]
+    docs, own_rows, width = k.shape
+    rims = jnp.concatenate(
+        [part[doc] for doc in range(docs) for part in (left, right)], axis=0
+    )
+    size = own_rows + WIN
     count = pooled.shape[2]
-    for which, (weight, bias, taps, out) in enumerate(((wk, None, ck, kx), (wv, bv, cv, vx))):
-        value = nn(extended, weight[...])
+    spot = offset - HALF + positions((size, 1), 0)
+    for which, (weight, bias, taps, own, out) in enumerate(
+        ((wk, None, ck, k, kx), (wv, bv, cv, v, vx))
+    ):
+        value = nn(rims, weight[...])
         if bias is not None:
             value = value + bias[...]
         value = value.astype(BF16)
-        out[0] = value
-        masked = jnp.where(valid, value.astype(F32), 0.0)
-        for group in range(value.shape[1] // LANES):
-            lanes = slice(group * LANES, (group + 1) * LANES)
-            rows[group] = masked[:, lanes]
-            total = jnp.zeros((count, LANES), F32)
-            for tap in range(KER):
-                start = HALF - KER // 2 + tap
-                read = rows[group, pl.ds(start, count, stride=STRIDE), :]
-                total = total + read * taps[tap : tap + 1, lanes]
-            if which == 1:
-                total = total + bcv[:, lanes]
-            pooled[0, which, :, lanes] = total.astype(BF16)
-
-
-def project(place, x, left, right, wq, bq, wk, wv, bv, ck, cv, bcv):
-    docs, rows, width = x.shape
+        for doc in range(docs):
+            at = doc * WIN
+            out[doc, :HALF] = value[at : at + HALF]
+            out[doc, HALF : HALF + own_rows] = own[doc]
+            out[doc, HALF + own_rows :] = value[at + HALF : at + WIN]
+            valid = (spot >= 0) & (spot < place[1 + doc])
+            for group in range(width // LANES):
+                lanes = slice(group * LANES, (group + 1) * LANES)
+                rows[group] = jnp.where(valid, out[doc, :, lanes].astype(F32), 0.0)
+                total = jnp.zeros((count, LANES), F32)
+                for tap in range(KER):
+                    start = HALF - KER // 2 + tap
+                    read = rows[group, pl.ds(start, count, stride=STRIDE), :]
+                    total = total + read * taps[tap : tap + 1, lanes]
+                if which == 1:
+                    total = total + bcv[:, lanes]
+                pooled[which, doc, :, lanes] = total.astype(BF16)
+
+
+def pool(place, left, right, k, v, wk, wv, bv, ck, cv, bcv):
+    docs, rows, width = k.shape
     extended = rows + WIN
     return call(
-        project_body,
-        (docs,),
+        pool_body,
+        (1,),
         (place,),
-        [by_doc(x), by_doc(left), by_doc(right)]
-        + [whole(a) for a in (wq, bq, wk, wv, bv, ck, cv, bcv)],
+        [whole(a) for a in (left, right, k, v, wk, wv, bv, ck, cv, bcv)],
         [
-            out_doc((docs, rows, width), BF16),
-            out_doc((docs, extended, width), BF16),
-            out_doc((docs, extended, width), BF16),
-            out_doc((docs, 2, rows // STRIDE, width), BF16),
+            out_whole((docs, extended, width), BF16),
+            out_whole((docs, extended, width), BF16),
+            out_whole((2, docs, rows // STRIDE, width), BF16),
         ],
         [pltpu.VMEM((width // LANES, extended, LANES), F32)],
-        flops=2 * docs * (rows + 2 * extended) * width * width,
-        moved=10**7,
     )
 
 
@@ -197,11 +218,11 @@
         first = tile * TILE
         for pair in range(q.shape[2] // LANES):
             lanes = slice(pair * LANES, (pair + 1) * LANES)
-            queries = stack_heads(q[0, first : first + TILE, lanes]) * SCALE
-            scores = nt(kx[0, first : first + span, lanes], queries) + bias
+            queries = stack_heads(q[doc, first : first + TILE, lanes]) * SCALE
+            scores = nt(kx[doc, first : first + span, lanes], queries) + bias
             chance = softmax_columns(scores)
             probs[pair, tile] = chance
-            turned = vx[0, first : first + span, lanes].T
+            turned = vx[doc, first : first + span, lanes].T
             mixed = nn(turned, chance.astype(BF16))
             mix[first : first + TILE, lanes] = unstack(mixed).astype(BF16)
 
@@ -213,14 +234,11 @@
         functools.partial(local_forward_body, doc=doc),
         (1,),
         (place,),
-        [one_doc(a, doc) for a in (q, kx, vx)],
+        [whole(a) for a in (q, kx, vx)],
         [
             out_whole((rows, width), BF16),
             out_whole((pairs, tiles, span, 2 * TILE), F32),
         ],
-        flops=rows * width * 4 * 2 * span,
-        moved=10**7,
-        exps=rows * HEADS * span,
     )
 
 
@@ -251,8 +269,6 @@
             out_whole((docs, rows, width), BF16),
             out_whole((docs, rows, width), BF16),
         ],
-        flops=docs * rows * width * width * 4,
-        moved=10**7,
     )
 
 
@@ -295,8 +311,6 @@
             out_whole((docs, rows, width), BF16),
             out_whole((8, width), F32),
         ],
-        flops=docs * rows * width * width * 4,
-        moved=10**7,
     )
 
 
@@ -314,10 +328,10 @@
         for pair in range(q.shape[2] // LANES):
             lanes = slice(pair * LANES, (pair + 1) * LANES)
             grad_q, grad_k, grad_v = attention_back(
-                kx[0, first : first + span, lanes],
-                vx[0, first : first + span, lanes],
-                q[0, first : first + TILE, lanes],
-                gmix[0, first : first + TILE, lanes],
+                kx[doc, first : first + span, lanes],
+                vx[doc, first : first + span, lanes],
+                q[doc, first : first + TILE, lanes],
+                gmix[doc, first : first + TILE, lanes],
                 probs[pair, tile],
             )
             dq[doc, first : first + TILE, lanes] = grad_q.astype(BF16)
@@ -336,7 +350,7 @@
         functools.partial(local_backward_body, doc=doc),
         (1,),
         (place,),
-        [one_doc(a, doc) for a in (q, kx, vx, gmix)] + [whole(a) for a in (probs, *earlier)],
+        [whole(a) for a in (q, kx, vx, gmix, probs, *earlier)],
         [
             out_whole((doc + 1, rows, width), BF16),
             out_whole((doc + 1, 2, rows, width), F32),
@@ -347,16 +361,38 @@
             pltpu.VMEM((rows + WIN, width), F32),
             pltpu.VMEM((rows + WIN, width), F32),
         ],
-        flops=rows * width * 8 * 2 * span,
-        moved=10**7,
     )
 
 
 def pooled_forward_body(place, slots, *refs, pieces):
     key_pieces = refs[:pieces]
     value_pieces = refs[pieces : 2 * pieces]
-    q2, middle, wpo, bpo, keys, values, probs, mix, summed, bias = refs[2 * pieces :]
+    (
+        q2, middle, wpo, bpo, we, wr,
+        keys_out, values_out, probs, mix, summed, we_near, wr_near,
+        keys, values, bias, sems,
+    ) = refs[2 * pieces :]
     doc, pair = pl.program_id(0), pl.program_id(1)
+    fetches = [
+        pltpu.make_async_copy(we, we_near, sems.at[0]),
+        pltpu.make_async_copy(wr, wr_near, sems.at[1]),
+    ]
+    last = (pair == pl.num_programs(1) - 1) & (doc == pl.num_programs(0) - 1)
+    leaves = [
+        pltpu.make_async_copy(keys.at[each], keys_out.at[each], sems.at[2 + each])
+        for each in range(keys.shape[0])
+    ] + [
+        pltpu.make_async_copy(
+            values.at[each], values_out.at[each], sems.at[2 + keys.shape[0] + each]
+        )
+        for each in range(keys.shape[0])
+    ]
+
+    @pl.when((pair == 0) & (doc == 0))
+    def _():
+        for fetch in fetches:
+            fetch.start()
+
     offset, length, base = place[0], place[1 + doc], place[1 + pl.num_programs(0)]
     tiles = q2.shape[1] // TILE
     count = keys.shape[1]
@@ -369,7 +405,7 @@
                 size = piece.shape[2]
                 for block in range(piece.shape[0]):
                     spot = pl.multiple_of(slots[where, at] * size, size)
-                    out[0, pl.ds(spot, size), :] = piece[block, 0]
+                    out[doc, pl.ds(spot, size), :] = piece[block, doc]
                     at += 1
         for tile in range(tiles):
             shape = (count, TILE)
@@ -382,87 +418,100 @@
                 & (spot * STRIDE < length)
             ) | (spot == centre)
             bias[tile] = jnp.where(allowed, 0.0, NEGATIVE)
+        for each in range(keys.shape[0]):
+
+            @pl.when(doc == each)
+            def _():
+                leaves[each].start()
+                leaves[keys.shape[0] + each].start()
 
     lanes = pl.ds(pl.multiple_of(pair * LANES, LANES), LANES)
-    pair_keys = keys[0, :, lanes]
-    turned = values[0, :, lanes].T
+    pair_keys = keys[doc, :, lanes]
+    turned = values[doc, :, lanes].T
     for tile in range(tiles):
         first = tile * TILE
-        queries = stack_heads(q2[0, first : first + TILE, :]) * SCALE
+        queries = stack_heads(q2[doc, first : first + TILE, lanes]) * SCALE
         half_bias = bias[tile]
         scores = nt(pair_keys, queries) + jnp.concatenate([half_bias, half_bias], axis=1)
         chance = softmax_columns(scores)
         probs[0, 0, tile] = chance
         mixed = nn(turned, chance.astype(BF16))
-        mix[0, first : first + TILE, lanes] = unstack(mixed).astype(BF16)
-
-    @pl.when(pair == pl.num_programs(1) - 1)
+        mix[doc, first : first + TILE, lanes] = unstack(mixed).astype(BF16)
+
+    @pl.when(last)
     def _():
-        summed[0] = middle[0] + (nn(mix[0], wpo[...]) + bpo[...])
-
-
-def pooled_forward(place, slots, key_pieces, value_pieces, q2, middle, wpo, bpo):
+        for copy in fetches + leaves:
+            copy.wait()
+        flat = (mix.shape[0] * mix.shape[1], mix.shape[2])
+        second = nn(mix[...].reshape(flat), wpo[...]) + bpo[...]
+        summed[...] = middle[...] + second.reshape(summed.shape)
+
+
+def pooled_forward(place, slots, key_pieces, value_pieces, q2, middle, wpo, bpo, we, wr):
     docs, rows, width = q2.shape
     pairs, tiles = width // LANES, rows // TILE
     size = key_pieces[0].shape[2]
     count = size * slots.shape[1]
 
-    def piece(array):
-        return (array, (array.shape[0], 1, size, width), lambda doc, *_: (0, doc, 0, 0))
-
     return call(
         functools.partial(pooled_forward_body, pieces=len(key_pieces)),
         (docs, pairs),
         (place, slots),
-        [piece(a) for a in key_pieces + value_pieces]
-        + [
-            (q2, (1, rows, LANES), lambda doc, pair, *_: (doc, 0, pair)),
-            by_doc(middle),
-            whole(wpo),
-            whole(bpo),
-        ],
+        [whole(a) for a in (*key_pieces, *value_pieces, q2, middle, wpo, bpo)]
+        + [raw(we), raw(wr)],
         [
-            out_doc((docs, count, width), BF16),
-            out_doc((docs, count, width), BF16),
+            out_raw((docs, count, width), BF16),
+            out_raw((docs, count, width), BF16),
             (
                 (docs, pairs, tiles, count, 2 * TILE),
                 F32,
                 (1, 1, tiles, count, 2 * TILE),
                 lambda doc, pair, *_: (doc, pair, 0, 0, 0),
             ),
-            out_doc((docs, rows, width), BF16),
-            out_doc((docs, rows, width), F32),
+            out_whole((docs, rows, width), BF16),
+            out_whole((docs, rows, width), F32),
+            out_whole(we.shape, BF16),
+            out_whole(wr.shape, BF16),
         ],
-        [pltpu.VMEM((tiles, count, TILE), F32)],
-        flops=docs * rows * width * (2 * width + 4 * 2 * count),
-        moved=3 * 10**7,
-        exps=docs * rows * HEADS * count,
+        [
+            pltpu.VMEM((docs, count, width), BF16),
+            pltpu.VMEM((docs, count, width), BF16),
+            pltpu.VMEM((tiles, count, TILE), F32),
+            pltpu.SemaphoreType.DMA((2 + 2 * docs,)),
+        ],
     )
 
 
 def pooled_backward_body(
     places, token, q2, keys, values, probs, grads, dq, dk_kept, dk_sent, dv_kept, dv_sent, sums
 ):
+    doc, pair = pl.program_id(0), pl.program_id(1)
+    lanes = pl.ds(pl.multiple_of(pair * LANES, LANES), LANES)
     size = dk_kept.shape[2]
     total = None
-    for tile in range(q2.shape[1] // TILE):
+    for tile in range(probs.shape[2]):
         first = tile * TILE
         grad_q, *added = attention_back(
-            keys[0], values[0], q2[0, first : first + TILE], grads[0, first : first + TILE],
+            keys[0],
+            values[0],
+            q2[0, first : first + TILE],
+            grads[0, first : first + TILE],
             probs[0, 0, tile],
         )
-        dq[0, first : first + TILE] = grad_q.astype(BF16)
+        dq[doc, first : first + TILE, lanes] = grad_q.astype(BF16)
         total = added if total is None else [a + b for a, b in zip(total, added)]
     half = dk_kept.shape[0]
+    rows = keys.shape[1]
     for which, (kept, sent) in enumerate(((dk_kept, dk_sent), (dv_kept, dv_sent))):
-        sums[...] = total[which]
+        sums[:rows] = total[which]
+        sums[rows:] = jnp.zeros((8, LANES), F32)
         for block in range(half + sent.shape[0]):
-            start = pl.multiple_of(places[which, block] * size, size)
+            start = pl.multiple_of(places[which, block] * (size - 8), size - 8)
             part = sums[pl.ds(start, size), :]
             if block < half:
-                kept[block, 0] = part
+                kept[block, doc, :, lanes] = part
             else:
-                sent[block - half, 0] = part.astype(BF16)
+                sent[block - half, doc, :, lanes] = part.astype(BF16)
 
 
 def pooled_backward(places, token, q2, keys, values, probs, grads, size, kept):
@@ -473,14 +522,6 @@
 
     def lanes_of(array):
         return (array, (1, array.shape[1], LANES), lambda doc, pair, *_: (doc, 0, pair))
-
-    def spread(number, dtype):
-        return (
-            (number, docs, size, width),
-            dtype,
-            (number, 1, size, LANES),
-            lambda doc, pair, *_: (0, doc, 0, pair),
-        )
 
     return call(
         pooled_backward_body,
@@ -498,29 +539,42 @@
             lanes_of(grads),
         ],
         [
-            ((docs, rows, width), BF16, (1, rows, LANES), lambda doc, pair, *_: (doc, 0, pair)),
-            spread(kept, F32),
-            spread(blocks - kept, BF16),
-            spread(kept, F32),
-            spread(blocks - kept, BF16),
+            out_whole((docs, rows, width), BF16),
+            out_whole((kept, docs, size + 8, width), F32),
+            out_whole((blocks - kept, docs, size + 8, width), BF16),
+            out_whole((kept, docs, size + 8, width), F32),
+            out_whole((blocks - kept, docs, size + 8, width), BF16),
         ],
-        [pltpu.VMEM((count, LANES), F32)],
-        flops=docs * rows * width * 8 * 2 * count,
-        moved=2 * 10**7,
+        [pltpu.VMEM((count + 8, LANES), F32)],
     )
 
 
 def feed_body(
     place, summed, cotangent, we, be, wr, br, ng, ns, fg, fs, wpo,
-    outputs, normed_low, hidden, grad_branch, grad_pre, grad_summed, grad_second, grad_mix,
-    vec, vec_wide,
-    normed, slope, work, unit,
+    outputs_far, normed_low, hidden, grad_branch, grad_pre, grad_summed_far, grad_second,
+    grad_mix_far, vec, vec_wide,
+    normed, slope, work, unit, outputs, grad_mix, sems,
 ):
     docs, rows = cotangent.shape[0], cotangent.shape[1]
     width = summed.shape[2]
     wide = we.shape[1]
     steps = rows // ROWS
-    blocks = [(doc, step * ROWS, doc * rows + step * ROWS) for doc in range(docs) for step in range(steps)]
+    blocks = [
+        (doc, step * ROWS, doc * rows + step * ROWS)
+        for doc in range(docs)
+        for step in range(steps)
+    ]
+    leaving = []
+
+    def leave(source, target, doc, start, row):
+        copy = pltpu.make_async_copy(
+            source.at[pl.ds(row, ROWS)],
+            target.at[doc, pl.ds(start, ROWS)],
+            sems.at[len(leaving)],
+        )
+        copy.start()
+        leaving.append(copy)
+
 
     def normal(value):
         centred = value - jnp.mean(value, axis=-1, keepdims=True)
@@ -555,7 +609,8 @@
         norm, scale = normal(work[row : row + ROWS])
         spot = place[0] + start + positions((ROWS, 1), 0)
         valid = (spot < place[1 + doc]).astype(F32)
-        outputs[doc, start : start + ROWS] = (valid * (norm * fg[...] + fs[...])).astype(BF16)
+        outputs[row : row + ROWS] = (valid * (norm * fg[...] + fs[...])).astype(BF16)
+        leave(outputs, outputs_far, doc, start, row)
         error = valid * cotangent[doc, start : start + ROWS].astype(F32)
         sums[0] += column_sum(error * norm)
         sums[1] += column_sum(error)
@@ -594,14 +649,18 @@
             - jnp.mean(scaled, axis=-1, keepdims=True)
             - norm * jnp.mean(scaled * norm, axis=-1, keepdims=True)
         ) * scale
-        grad_summed[doc, start : start + ROWS] = grad
+        unit[row : row + ROWS] = grad
+        leave(unit, grad_summed_far, doc, start, row)
         low = grad.astype(BF16)
         grad_second[row : row + ROWS] = low
         sums[5] += column_sum(low)
-        grad_mix[doc, start : start + ROWS] = nt(low, wpo[...]).astype(BF16)
+        grad_mix[row : row + ROWS] = nt(low, wpo[...]).astype(BF16)
+        leave(grad_mix, grad_mix_far, doc, start, row)
     for index, value in enumerate(sums):
         vec[index : index + 1] = value
     vec[6:8] = jnp.zeros((2, width), F32)
+    for copy in leaving:
+        copy.wait()
 
 
 def feed(place, summed, cotangent, we, be, wr, br, ng, ns, fg, fs, wpo):
@@ -614,14 +673,14 @@
         (place,),
         [whole(a) for a in (summed, cotangent, we, be, wr, br, ng, ns, fg, fs, wpo)],
         [
-            out_whole((docs, rows, width), BF16),
+            out_raw((docs, rows, width), BF16),
             out_whole((tokens, width), BF16),
             out_whole((tokens, wide), BF16),
             out_whole((tokens, width), BF16),
             out_whole((tokens, wide), BF16),
-            out_whole((docs, rows, width), F32),
+            out_raw((docs, rows, width), F32),
             out_whole((tokens, width), BF16),
-            out_whole((docs, rows, width), BF16),
+            out_raw((docs, rows, width), BF16),
             out_whole((8, width), F32),
             out_whole((1, wide), F32),
         ],
@@ -630,17 +689,17 @@
             pltpu.VMEM((tokens, wide), F32),
             pltpu.VMEM((tokens, width), F32),
             pltpu.VMEM((tokens, width), F32),
+            pltpu.VMEM((tokens, width), BF16),
+            pltpu.VMEM((tokens, width), BF16),
+            pltpu.SemaphoreType.DMA((3 * tokens // ROWS,)),
         ],
-        flops=2 * tokens * width * (4 * wide + width),
-        moved=3 * 10**7,
-        exps=2 * tokens * wide,
     )
 
 
 def key_value_body(place, *refs, docs):
-    (gk_kept, gk_came, gv_kept, gv_came, gk_next, gv_next, kx, vx, ck, cv) = refs[:10]
-    own, from_left, from_right, dq = refs[10:14]
-    gk, gv, vec, rows_in, pooled, total = refs[14:]
+    gk_kept, gk_came, gv_kept, gv_came, kx, vx, ck, cv = refs[:8]
+    own, from_left, from_right, dq = refs[8:12]
+    gk, gv, vec, rows_in, pooled, total = refs[12:]
     offset = place[0]
     rows, width = gk.shape[0] // docs, gk.shape[1]
     count = rows // STRIDE
@@ -650,14 +709,13 @@
         spot = offset - HALF + positions((rows + WIN, 1), 0)
         valid = (spot >= 0) & (spot < length)
         first = doc * rows
-        for which, (kept, came, after, ext, taps, out, row) in enumerate(
+        for which, (kept, came, ext, taps, out, row) in enumerate(
             (
-                (gk_kept, gk_came, gk_next, kx, ck, gk, 0),
-                (gv_kept, gv_came, gv_next, vx, cv, gv, KER),
+                (gk_kept, gk_came, kx, ck, gk, 0),
+                (gv_kept, gv_came, vx, cv, gv, KER),
             )
         ):
-            pooled[:count] = kept[doc].astype(F32) + came[doc].astype(F32)
-            pooled[count:] = jnp.broadcast_to(after[doc].astype(F32), (8, width))
+            pooled[...] = kept[doc].astype(F32) + came[doc].astype(F32)
             masked = jnp.where(valid, ext[doc].astype(F32), 0.0)
             for group in range(width // LANES):
                 lanes = slice(group * LANES, (group + 1) * LANES)
@@ -693,7 +751,7 @@
     vec[12:13] += column_sum(gv[...])
 
 
-def key_value_gradients(place, pooled_grads, next_grads, kx, vx, ck, cv, own, left, right, dq):
+def key_value_gradients(place, pooled_grads, kx, vx, ck, cv, own, left, right, dq):
     docs, rows, width = dq.shape
     return call(
         functools.partial(key_value_body, docs=docs),
@@ -701,7 +759,7 @@
         (place,),
         [
             whole(a)
-            for a in (*pooled_grads, *next_grads, kx, vx, ck, cv, own, left, right, dq)
+            for a in (*pooled_grads, kx, vx, ck, cv, own, left, right, dq)
         ],
         [out_whole((docs * rows, width), BF16)] * 2 + [out_whole((16, width), F32)],
         [
@@ -709,8 +767,6 @@
             pltpu.VMEM((rows // STRIDE + 8, width), F32),
             pltpu.VMEM((width // LANES, rows, LANES), F32),
         ],
-        flops=docs * rows * width * 40,
-        moved=10**7,
     )
 
 
@@ -727,8 +783,6 @@
         (place,),
         [whole(a) for a in (dq, gk, gv, gmid, wq, wk, wv)],
         [out_whole((docs, rows, width), BF16)],
-        flops=2 * docs * rows * width * 3 * width,
-        moved=10**7,
     )
     return dx
 
@@ -854,9 +908,91 @@
         [out_whole(shape, BF16)] * (1 if quartered else 2),
         [pltpu.VMEM((768, operands[0].shape[0]), BF16), pltpu.VMEM((768, 768), BF16)]
         + ([pltpu.VMEM((2, 8, 16, 384), F32)] if extra else []),
-        flops=sum(2 * left.shape[0] * left.shape[1] * right.shape[1] for _, left, right in items),
-        moved=2 * sum(a.size for a in operands) + 4 * math.prod(shape),
-    )
+    )
+
+
+def quarter_products_body(bits, *refs, kinds, levels):
+    count = len(kinds)
+    operands = [refs[2 * index : 2 * index + 2] for index in range(count)]
+    out, turned, rounded, sems = refs[2 * count :]
+    sides, cores, owners = 2, 2, 1 << levels
+    pending = [[], []]
+    turn = 0
+
+    def product(left, right):
+        nonlocal turn
+        slot = turn % 2
+        turn += 1
+        for copy in pending[slot]:
+            copy.wait()
+        pending[slot] = []
+        rounded[slot] = nn(left, right).astype(BF16)
+        return slot
+
+    def leave(slot, source, side, which, owner, base, size):
+        digits = [((owner >> level) & 1) ^ bits[level] for level in range(levels)]
+        target = out.at[(side, which, *digits, pl.ds(base, size))]
+        copy = pltpu.make_async_copy(source, target, sems.at[slot, len(pending[slot])])
+        copy.start()
+        pending[slot].append(copy)
+
+    def by_rows(slot, which, base, columns):
+        size = 768 // owners // sides
+        for owner in range(owners):
+            for side in range(sides):
+                row = (owner * sides + side) * size
+                source = rounded.at[slot, pl.ds(row, size), pl.ds(columns, 384)]
+                leave(slot, source, side, which, owner, base, size)
+
+    base = 0
+    for (left, right), kind in zip(operands, kinds):
+        turned[...] = left[...].T
+        if kind == "wide":
+            for which in range(cores):
+                for part in range(2):
+                    start = which * 1536 + part * 768
+                    slot = product(turned[...], right[:, start : start + 768])
+                    for column in range(2):
+                        by_rows(slot, which, base + (2 * part + column) * 48, column * 384)
+            base += 192
+        elif kind == "tall":
+            for part in range(4):
+                slot = product(turned[...], right[:, part * 768 : part * 768 + 768])
+                for column in range(2):
+                    for which in range(cores):
+                        for side in range(sides):
+                            row = (which * sides + side) * 192
+                            source = rounded.at[slot, pl.ds(row, 192), pl.ds(column * 384, 384)]
+                            leave(slot, source, side, which, 2 * part + column, base, 192)
+            base += 192
+        else:
+            slot = product(turned[...], right[...])
+            for which in range(cores):
+                by_rows(slot, which, base, which * 384)
+            base += 48
+    for group in pending:
+        for copy in group:
+            copy.wait()
+
+
+def quarter_products(bits, items, levels):
+    rows = sum(48 if kind == "square" else 192 for kind, _, _ in items)
+    operands = [array for _, left, right in items for array in (left, right)]
+    (out,) = call(
+        functools.partial(
+            quarter_products_body, kinds=tuple(kind for kind, _, _ in items), levels=levels
+        ),
+        (1,),
+        (bits,),
+        [whole(a) for a in operands],
+        [out_raw((2, 2) + (2,) * levels + (rows, 384), BF16)],
+        [
+            pltpu.VMEM((768, operands[0].shape[0]), BF16),
+            pltpu.VMEM((2, 768, 768), BF16),
+            pltpu.SemaphoreType.DMA((2, 32)),
+        ],
+    )
+    return out
 
 
 def swap(value, axis, bit):
@@ -924,11 +1060,16 @@
 
     left = shift(inputs[:, rows - HALF :], "seq", 1)
     right = shift(inputs[:, :HALF], "seq", -1)
-    q, kx, vx, pooled = project(
-        place, inputs, left, right, local_query, line(local_query_bias), local_key, local_value,
-        line(local_value_bias), taps_key, taps_value, line(conv_value_bias),
-    )
-    own = [pooled[:, which][None] for which in range(2)]
+    q, k_own, v_own = project(
+        place, inputs, local_query, line(local_query_bias), local_key, local_value,
+        line(local_value_bias),
+    )
+    left, right, k_own = sync(left, right, k_own)
+    kx, vx, pooled = pool(
+        place, left, right, k_own, v_own, local_key, local_value, line(local_value_bias),
+        taps_key, taps_value, line(conv_value_bias),
+    )
+    own = [pooled[which][None] for which in range(2)]
 
     mixes, probs_one = [], []
 
@@ -987,14 +1128,15 @@
             line(pooled_query_bias), mixes,
         )
 
-    keys, values, probs_two, mix_two, summed = pooled_forward(
-        token, slots, pieces[0], pieces[1], q2, middle, pooled_output, line(pooled_output_bias)
+    keys, values, probs_two, mix_two, summed, expand_near, reduce_near = pooled_forward(
+        token, slots, pieces[0], pieces[1], q2, middle, pooled_output, line(pooled_output_bias),
+        expand_weight, reduce_weight,
     )
     (
         outputs, normed_low, hidden, grad_branch, grad_pre, grad_summed, grad_second, grad_mix_two,
         vec_feed, vec_wide,
     ) = feed(
-        token, summed, cotangent, expand_weight, line(expand_bias), reduce_weight,
+        token, summed, cotangent, expand_near, line(expand_bias), reduce_near,
         line(reduce_bias), line(norm_gain), line(norm_shift), line(final_gain),
         line(final_shift), pooled_output,
     )
@@ -1006,25 +1148,26 @@
         ids = [mine & 1] + [(mine if axis == "batch" else me) >> bit & 1 for axis, bit in order]
         return jnp.stack(ids).astype(jnp.int32)
 
+    seq_bits = jnp.stack([me >> level & 1 for level in range(levels)]).astype(jnp.int32)
+
+    def over_batch(blocks):
+        part = blocks.shape[2:]
+        flat_blocks = blocks.reshape(-1, blocks.shape[-1])
+        mine_part = lax.psum_scatter(flat_blocks, "batch", scatter_dimension=0, tiled=True)
+        return mine_part.reshape(part)
+
     if fast:
-        (feed_blocks,) = scatter_products(
-            bits_of(order_first),
-            order_first,
+        feed_blocks = quarter_products(
+            seq_bits,
             [
                 ("wide", normed_low, grad_pre),
                 ("tall", grad_branch, hidden),
                 ("square", tokens(mix_two), grad_second),
             ],
-            quartered=True,
+            levels,
         )
         feed_blocks, grad_mix_two, token = sync(feed_blocks, grad_mix_two, token)
-        feed_rows = feed_blocks.shape[-2]
-        feed_mine = lax.psum_scatter(
-            feed_blocks.reshape(4 * devices * feed_rows, 384),
-            "batch",
-            scatter_dimension=0,
-            tiled=True,
-        ).reshape((2,) * levels + (feed_rows, 384))
+        feed_part = over_batch(feed_blocks)
 
     blocks = devices if gathered else 2 * reach + 1
     if gathered:
@@ -1047,23 +1190,47 @@
     grad_q2, dk_kept, dk_sent, dv_kept, dv_sent = pooled_backward(
         places, token, q2, keys, values, probs_two, grad_mix_two, size, half_blocks
     )
-    back_parts = ()
-
-    def back_step(doc, token, earlier):
-        return local_backward(token, q, kx, vx, grad_mix_one, probs_one[doc], doc, earlier)
-
     grad_middle, grad_first, grad_mix_one, vec_first = first_backward(
         token, grad_q2, grad_summed, pooled_query, local_output
     )
+    back_parts = ()
+
+    def back_step(doc, token):
+        return local_backward(
+            token, q, kx, vx, grad_mix_one, probs_one[doc], doc, back_parts
+        )
+
     if gathered:
         kept = [part.reshape((2,) * (levels - 1) + part.shape[1:]) for part in (dk_kept, dv_kept)]
         sent = [part.reshape((2,) * (levels - 1) + part.shape[1:]) for part in (dk_sent, dv_sent)]
         for stage in range(levels):
             came = [swap(sent[which], "seq", back[which][stage]) for which in range(2)]
             if stage < docs:
-                back_parts = list(back_step(stage, token, back_parts))
+                back_parts = list(back_step(stage, token))
+            if stage == docs - 1:
+                from_left = shift(back_parts[3], "seq", 1)
+                from_right = shift(back_parts[2], "seq", -1)
+            if fast and stage == 0:
                 came[0], came[1], back_parts[0], token = sync(
                     came[0], came[1], back_parts[0], token
+                )
+            if fast and stage == 1:
+                middle_kept, middle_sent = scatter_products(
+                    bits_of(order_first) + 0 * token[0],
+                    order_first,
+                    [
+                        ("square", tokens(middle_low), tokens(grad_q2)),
+                        ("square", tokens(mix_one), grad_first),
+                        ("square", tokens(inputs), tokens(back_parts[0])),
+                    ],
+                )
+                came[0], came[1], from_left, from_right, middle_sent, token = sync(
+                    came[0], came[1], from_left, from_right, middle_sent, token
+                )
+            if fast and stage == 2:
+                middle_came = swap(middle_sent, "batch", 0)
+                came[0], came[1], middle_came, token = sync(
+                    came[0], came[1], middle_came, token
                 )
             if stage < levels - 1:
                 for which in range(2):
@@ -1076,37 +1243,19 @@
             for distance in range(1, reach + 1):
                 total = total + shift(sent[reach - distance], "seq", -distance).astype(F32)
                 total = total + shift(sent[reach + distance - 1], "seq", distance).astype(F32)
+            after = shift(total[:, :1].astype(BF16), "seq", -1).astype(F32)
+            total = jnp.concatenate([total[:, :size], jnp.tile(after, (1, 8, 1))], axis=1)
             pooled_grads += [total, jnp.zeros_like(total)]
         for doc in range(docs):
-            back_parts = back_step(doc, token, back_parts)
-    dq, own_grads, low_left, low_right = back_parts
-    from_left = shift(low_right, "seq", 1)
-    from_right = shift(low_left, "seq", -1)
+            back_parts = back_step(doc, token)
+        from_left = shift(back_parts[3], "seq", 1)
+        from_right = shift(back_parts[2], "seq", -1)
+    dq, own_grads = back_parts[:2]
     if fast:
-        middle_kept, middle_sent = scatter_products(
-            bits_of(order_first) + 0 * token[0],
-            order_first,
-            [
-                ("square", tokens(middle_low), tokens(grad_q2)),
-                ("square", tokens(mix_one), grad_first),
-                ("square", tokens(inputs), tokens(dq)),
-            ],
-        )
-        pooled_grads[1], pooled_grads[3], middle_sent, from_left, from_right, token = sync(
-            pooled_grads[1], pooled_grads[3], middle_sent, from_left, from_right, token
-        )
-    heads = [
-        pooled_grads[2 * which][:, :1].astype(F32) + pooled_grads[2 * which + 1][:, :1].astype(F32)
-        for which in range(2)
-    ]
-    after = shift(jnp.stack(heads).astype(BF16), "seq", -1)
-    if fast:
-        middle_came = swap(middle_sent, "batch", 0)
-        after, middle_came, token = sync(after, middle_came, token)
-        middle_terms, middle_came = advance([middle_kept, middle_came], order_first[0])
-        feed_terms, feed_came = advance([feed_mine], order_first[1])
+        middle_terms = [middle_kept, middle_came]
+        middle_far = swap(total_of(middle_terms, 1, slice(None), 1).astype(BF16), "batch", 1)
     grad_k, grad_v, vec_input = key_value_gradients(
-        token, pooled_grads, [after[0], after[1]], kx, vx, taps_key, taps_value,
+        token, pooled_grads, kx, vx, taps_key, taps_value,
         own_grads, from_left, from_right, dq,
     )
     if fast:
@@ -1116,8 +1265,9 @@
             [("square", tokens(inputs), grad_k), ("square", tokens(inputs), grad_v)],
             (vec_feed, vec_first, vec_input, vec_wide),
         )
-        last_sent, middle_came, token = sync(last_sent, middle_came, token)
+        last_sent, middle_far, token = sync(last_sent, middle_far, token)
         last_came = swap(last_sent, "batch", 0)
+        middle_near = swap(total_of(middle_terms, 1, slice(None), 0).astype(BF16), "batch", 1)
     input_grad = input_gradient(
         token, tokens(dq), grad_k, grad_v, grad_middle, local_query, local_key, local_value
     )
@@ -1125,49 +1275,59 @@
     if fast:
         upper = (mine & 2) > 0
         odd = (mine & 1) > 0
+        cut_feed = feed_part.shape[-2] // 2
+        one = [feed_part[..., :cut_feed, :]]
+        two = [feed_part[..., cut_feed:, :]]
 
         def pair_up(flag, low, other):
             return jnp.stack([jnp.where(flag, other, low), jnp.where(flag, low, other)])
 
-        input_grad, last_came, feed_came = sync(input_grad, last_came, feed_came)
-        cut_at = middle_kept.shape[-2]
-
-        def joined(axis):
-            left_part = total_of(middle_terms + [middle_came], 1)
-            right_part = total_of(last_terms, 1)
-            return jnp.concatenate([left_part, right_part], axis=-2).astype(BF16)
-
-        last_terms = [last_kept, last_came]
-        came = swap(joined(0), "seq", 0)
-        feed_terms, feed_came = advance(feed_terms + [feed_came], order_first[2])
-        came, feed_came = sync(came, feed_came)
-        middle_terms = [term[0] for term in middle_terms + [middle_came]] + [
-            came[..., :cut_at, :]
-        ]
-        last_terms = [term[0] for term in last_terms] + [came[..., cut_at:, :]]
-        for hop in range(1, levels):
-            send = jnp.concatenate(
-                [total_of(middle_terms, 1), total_of(last_terms, 1)], axis=-2
-            ).astype(BF16)
-            came = swap(send, "seq", hop)
-            if hop == 1:
-                feed_terms, feed_came = advance(feed_terms + [feed_came], order_first[3])
-                came, feed_came = sync(came, feed_came)
-            if hop == 2:
-                feed_low = total_of(feed_terms + [feed_came], Ellipsis).astype(BF16)
-                feed_other = swap(feed_low, "batch", 1)
-                came, feed_other = sync(came, feed_other)
-            middle_terms = [term[0] for term in middle_terms] + [came[..., :cut_at, :]]
-            last_terms = [term[0] for term in last_terms] + [came[..., cut_at:, :]]
-        final = jnp.concatenate(
-            [total_of(middle_terms, Ellipsis), total_of(last_terms, Ellipsis)], axis=-2
+        def advance_second(terms, hop):
+            came = swap(total_of(terms, slice(None), 1).astype(BF16), *hop)
+            return [term[:, 0] for term in terms], came
+
+        one, one_came = advance(one, ("seq", 0))
+        two, two_came = advance_second(two, ("seq", 1))
+        input_grad, last_came, middle_near, one_came, two_came = sync(
+            input_grad, last_came, middle_near, one_came, two_came
+        )
+        last_terms, last_came = advance([last_kept, last_came], ("seq", 0))
+        middle_came = swap(
+            total_of([term[0, :, 1] for term in middle_terms] + [middle_far], Ellipsis).astype(BF16),
+            "seq",
+            1,
+        )
+        middle_terms = [term[0, :, 0] for term in middle_terms] + [middle_near]
+        one, one_came = advance(one + [one_came], ("seq", 1))
+        two, two_came = advance(two + [two_came], ("seq", 0))
+        last_came, middle_came, one_came, two_came = sync(
+            last_came, middle_came, one_came, two_came
+        )
+
+        last_terms, last_came = advance(last_terms + [last_came], ("seq", 1))
+        one, two = one + [one_came], two + [two_came]
+        feed_came = swap(
+            jnp.concatenate([total_of(one, 1), total_of(two, 1)]).astype(BF16), "seq", 2
+        )
+        middle_terms, middle_came = advance(middle_terms + [middle_came], ("seq", 0))
+        last_came, middle_came, feed_came = sync(last_came, middle_came, feed_came)
+
+        last_terms, last_came = advance(last_terms + [last_came], ("seq", 2))
+        middle_terms, middle_came = advance(middle_terms + [middle_came], ("seq", 2))
+        feed_low = (
+            jnp.concatenate([total_of(one, 0), total_of(two, 0)]) + feed_came.astype(F32)
         ).astype(BF16)
-        other = swap(final, "batch", 1)
+        feed_other = swap(feed_low, "batch", 1)
+        last_came, middle_came, feed_other = sync(last_came, middle_came, feed_other)
+        last_low = total_of(last_terms + [last_came], Ellipsis).astype(BF16)
+        middle_sum = total_of(middle_terms + [middle_came], Ellipsis).astype(BF16)
+        cut_at = middle_sum.shape[0]
+        other = swap(jnp.concatenate([middle_sum, last_low]), "batch", 1)
         feed_both = pair_up(upper, feed_low, feed_other)
         feed_across = swap(feed_both, "batch", 0)
         other, feed_across = sync(other, feed_across)
-        middle_both = pair_up(upper, final[:cut_at], other[:cut_at]).reshape(2 * cut_at, 384)
-        last_half = (final[cut_at:].astype(F32) + other[cut_at:].astype(F32)).astype(BF16)
+        middle_both = pair_up(upper, middle_sum, other[:cut_at]).reshape(2 * cut_at, 384)
+        last_half = (last_low.astype(F32) + other[cut_at:].astype(F32)).astype(BF16)
         both = jnp.concatenate([middle_both, last_half])
         across = swap(both, "batch", 0)
         full_feed = pair_up(odd, feed_both, feed_across)

time: 390 us -> 371 us (0.951)
  waiting for transfers between devices: 124 us -> 85.8 us
  starting transfers between devices: 34.4 us -> 59.6 us
  local copies, waits for them, and re-layouts: 73.1 us -> 50.9 us
  other arithmetic: 18.5 us -> 27.6 us
  Pallas kernels: 119 us -> 128 us
    ppermute x25 -> x31, waiting for transfers between devices: 116 us -> 85.8 us  [swap(): return lax.ppermute(value, axis, [(i, i ^ 1 << bit) for i in range(count)])]
    ppermute x25 -> x31, starting transfers between devices: 23.2 us -> 49.8 us  [swap(): return lax.ppermute(value, axis, [(i, i ^ 1 << bit) for i in range(count)])]
    unnamed x207 -> x209, local copies, waits for them, and re-layouts: 54.5 us -> 36.7 us
    pallas_call x15 -> x16, Pallas kernels: 119 us -> 128 us  [call(): pl.pallas_call(body, grid_spec=pltpu.PrefetchScalarGridSpec(num_scalar_pr...]
    ppermute x5 -> x4, waiting for transfers between devices: 8.02 us -> 0.01 us  [shift(): return lax.ppermute(value, axis, pairs)]
    convert_element_type x2 -> x7, other arithmetic: 0.22 us -> 5.01 us  [the longest x1 1.26 us: device_step(): total_of(middle_terms, 1, slice(None), 0).astype(BF16)]
    convert_element_type x3 -> x6, other arithmetic: 1.63 us -> 6.18 us  [advance(): came = swap(total_of(terms, 1).astype(BF16), *hop)]
    another operation x8 -> x1, other arithmetic: 4.42 us -> 0.08 us  [device_step(): jnp.stack([me >> level & 1 for level in range(levels)]).astype(jnp.int32)]
  transfers between devices with their start and end apart: 31 -> 36, of which waited for: 19 -> 20; matrix products, arithmetic and copies ran while one was open for 6% -> 7% of each run, Pallas kernels for 14% -> 16%
where the time goes in v3:
time: 371 us; the launch traced here: 367 us
  Pallas kernels  128 us (35%)
  waiting for transfers between devices  85.8 us (23%)
  starting transfers between devices  59.6 us (16%)
  local copies, waits for them, and re-layouts  50.9 us (14%)
  other arithmetic  27.6 us (7%)
  between operations  15.4 us (4%)
    pallas_call x16, Pallas kernels, call(): pl.pallas_call(body, grid_spec=pltpu.PrefetchScalarGridSpec(num_scalar_pr...  128 us
    ppermute x31, waiting for transfers between devices, swap(): return lax.ppermute(value, axis, [(i, i ^ 1 << bit) for i in range(count)])  85.8 us
    ppermute x31, starting transfers between devices, swap(): return lax.ppermute(value, axis, [(i, i ^ 1 << bit) for i in range(count)])  49.8 us
    unnamed x209, local copies, waits for them, and re-layouts  36.7 us
    ppermute x4, starting transfers between devices, shift(): return lax.ppermute(value, axis, pairs)  9.84 us
  transfers between devices with their start and end apart: 36, of which 20 were waited for; matrix products, arithmetic and copies ran while one was open for 7% of the time, Pallas kernels for 16%

profile of v3, /device:TPU:1, one launch (start us, length us, event | category | flops | bytes accessed | tf_op | source)
XLA Modules:
  0.0 367.1 jit_solution(1140093722907837434)
XLA Ops:
  8.3 4.0 %collective-permute-start = (bf16[2,64,768]{2,1,0:T(8,128)(2,1)S(1)}, bf16[2,64,768]{2,1,0:T(8,128)(2,1)S(1)}, u32[]{:S(2)}, u32[]{:S(2)}) collective-permute-start(bf16[2,64,768]{2,1,0:T(8,128)(2,1)S(1)} %get-tuple-element.307), channel_id=1, source_target_pairs={{0,4},{4,8},{8,12},{12,16},{16,20},{20,24},{24,28},{1,5},{5,9},{9,... | collective-permute-start | bytes 589832 | tf_op jit(solution)/shard_map/ppermute | solution.py:1006
  25.3 4.1 %collective-permute-start.2 = (bf16[1,2,64,768]{3,2,1,0:T(8,128)(2,1)S(1)}, bf16[1,2,64,768]{3,2,1,0:T(8,128)(2,1)S(1)}, u32[]{:S(2)}, u32[]{:S(2)}) collective-permute-start(bf16[1,2,64,768]{3,2,1,0:T(8,128)(2,1)S(1)} %get-tuple-element.318.refs_0_), channel_id=1, source_target_pairs={{0,16},{4,20},{8,24},{12,28},{16,0},{20,4},{24,8},{28,12},{1,17},{... | collective-permute-start | bytes 589832 | tf_op jit(solution)/shard_map/ppermute | solution.py:1000
  29.7 4.8 %shard_map.462 = (bf16[256,768]{1,0:T(8,128)(2,1)S(1)}, f32[6,2,256,256]{3,2,1,0:T(8,128)S(1)}) custom-call(s32[4]{0:T(128)S(1)} %pad_add_fusion.1.place.token, bf16[2,256,768]{2,1,0:T(8,128)(2,1)S(1)} %get-tuple-element.137.q, bf16[2,384,768]{2,1,0:T(8,128)(2,1)S(1)} %get-tuple-element.138.kx.refs_4_, bf16[2,384,768]{2,1,0:T(8,128)(2,1)S(1)} %get-tuple-element.139.vx.refs_5_), custom_call_target="tpu_custom_call" | custom-call | flops 1000 | bytes 1000 | tf_op jit(solution)/shard_map/pallas_call | solution.py:71
  38.0 4.7 %collective-permute-start.4 = (bf16[2,2,64,768]{3,2,1,0:T(8,128)(2,1)S(1)}, bf16[2,2,64,768]{3,2,1,0:T(8,128)(2,1)S(1)}, u32[]{:S(2)}, u32[]{:S(2)}) collective-permute-start(bf16[2,2,64,768]{3,2,1,0:T(8,128)(2,1)S(1)} %pad_maximum_fusion.5), channel_id=1, source_target_pairs={{0,8},{4,12},{8,0},{12,4},{16,24},{20,28},{24,16},{28,20},{1,9},{5... | collective-permute-start | bytes 1179656 | tf_op jit(solution)/shard_map/ppermute | solution.py:1000
  42.7 4.8 %shard_map.463 = (bf16[256,768]{1,0:T(8,128)(2,1)S(1)}, f32[6,2,256,256]{3,2,1,0:T(8,128)S(1)}) custom-call(s32[4]{0:T(128)S(1)} %pad_add_fusion.1.place.token, bf16[2,256,768]{2,1,0:T(8,128)(2,1)S(1)} %get-tuple-element.137.q, bf16[2,384,768]{2,1,0:T(8,128)(2,1)S(1)} %get-tuple-element.138.kx.refs_4_, bf16[2,384,768]{2,1,0:T(8,128)(2,1)S(1)} %get-tuple-element.139.vx.refs_5_), custom_call_target="tpu_custom_call" | custom-call | flops 1000 | bytes 1000 | tf_op jit(solution)/shard_map/pallas_call | solution.py:71
  49.9 6.4 %collective-permute-done.5.refs_6_ = bf16[2,2,64,768]{3,2,1,0:T(8,128)(2,1)S(1)} collective-permute-done((bf16[2,2,64,768]{3,2,1,0:T(8,128)(2,1)S(1)}, bf16[2,2,64,768]{3,2,1,0:T(8,128)(2,1)S(1)}, u32[]{:S(2)}, u32[]{:S(2)}) %collective-permute-start.5) | collective-permute-done | bytes 393248 | tf_op jit(solution)/shard_map/ppermute | solution.py:1000
  75.3 32.7 %shard_map.465 = (bf16[2,512,768]{2,1,0:T(8,128)(2,1)}, bf16[2,512,768]{2,1,0:T(8,128)(2,1)}, f32[2,6,2,512,256]{4,3,2,1,0:T(8,128)}, bf16[2,256,768]{2,1,0:T(8,...) custom-call(s32[4]{0:T(128)S(1)} %pad_add_fusion.1.place.token, ...), custom_call_target="tpu_custom_call" | custom-call | flops 1000 | bytes 1000 | tf_op jit(solution)/shard_map/pallas_call | solution.py:71
  108.1 22.8 %shard_map.466 = (bf16[2,256,768]{2,1,0:T(8,128)(2,1)}, bf16[512,768]{1,0:T(8,128)(2,1)S(1)}, bf16[512,3072]{1,0:T(8,128)(2,1)S(1)}, bf16[512,768]{1,0:T(8,128)(...) custom-call(s32[4]{0:T(128)S(1)} %pad_add_fusion.1.place.token, ...), custom_call_target="tpu_custom_call" | custom-call | flops 1000 | bytes 1000 | tf_op jit(solution)/shard_map/pallas_call | solution.py:71
  130.9 11.3 %shard_map.467 = bf16[2,2,2,2,2,432,384]{6,5,4,3,2,1,0:T(8,128)(2,1)} custom-call(s32[3]{0:T(128)S(1)} %pad_add_fusion.3.bits, bf16[512,768]{1,0:T(8,128)(2,1)S(1)} %get-tuple-element.160.refs_0_, bf16[512,3072]{1,0:T(8,128)(2,1)S(1)} %get-tuple-element.161.refs_1_, bf16[512,768]{1,0:T(8,128)(2,1)S(1)} %get-tuple-element.162.refs_2_, ...), custom_call_target="tpu_custom_call" | custom-call | flops 1000 | bytes 1000 | tf_op jit(solution)/shard_map/pallas_call | solution.py:71
  142.9 19.3 %shard_map.468 = (bf16[2,256,768]{2,1,0:T(8,128)(2,1)S(1)}, f32[4,2,72,768]{3,2,1,0:T(8,128)S(1)}, bf16[4,2,72,768]{3,2,1,0:T(8,128)(2,1)S(1)}, f32[4,2,72,768]{3,2,1,0:T(8,128)S(1)}, bf16[4,2,72,768]{3,2,1,0:T(8,128)(2,1)S(1)}) custom-call(s32[2,8]{1,0:T(2,128)S(1)} %copy-done.77, s32[4]{0:T(128)S(1)} %pad_add_fusion.1.place.token, ...), custom_call_target="tpu_custom_call" | custom-call | flops 1000 | bytes 1000 | tf_op jit(solution)/shard_map/pallas_call | solution.py:71
  168.1 4.5 %shard_map.470 = (bf16[1,256,768]{2,1,0:T(8,128)(2,1)S(1)}, f32[1,2,256,768]{3,2,1,0:T(8,128)S(1)}, bf16[1,2,64,768]{3,2,1,0:T(8,128)(2,1)S(1)}, bf16[1,2,64,768]{3,2,1,0:T(8,128)(2,1)S(1)}) custom-call(s32[4]{0:T(128)S(1)} %pad_add_fusion.1.place.token, bf16[2,256,768]{2,1,0:T(8,128)(2,1)S(1)} %copy-done.3, ...), custom_call_target="tpu_custom_call" | custom-call | flops 1000 | bytes 1000 | tf_op jit(solution)/shard_map/pallas_call | solution.py:71
  172.5 6.9 %collective-permute-done.8 = bf16[2,2,2,72,768]{4,3,2,1,0:T(8,128)(2,1)S(1)} collective-permute-done((bf16[2,2,2,72,768]{4,3,2,1,0:T(8,128)(2,1)S(1)}, bf16[2,2,2,72,768]{4,3,2,1,0:T(8,128)(2,1)S(1)}, u32[]{:S(2)}, u32[]{:S(2)}) %collective-permute-start.8) | collective-permute-done | bytes 884768 | tf_op jit(solution)/shard_map/ppermute | solution.py:1000
  181.5 7.0 %collective-permute-start.11 = (bf16[2,2,72,768]{3,2,1,0:T(8,128)(2,1)}, bf16[2,2,72,768]{3,2,1,0:T(8,128)(2,1)}, u32[]{:S(2)}, u32[]{:S(2)}) collective-permute-start(bf16[2,2,72,768]{3,2,1,0:T(8,128)(2,1)} %get-tuple-element.295), channel_id=1, source_target_pairs={{0,16},{4,20},{8,24},{12,28},{16,0},{20,4},{24,8},{28,12},{1,17},{... | collective-permute-start | bytes 1327112 | tf_op jit(solution)/shard_map/ppermute | solution.py:1000
  191.0 5.5 %shard_map.471 = (bf16[2,256,768]{2,1,0:T(8,128)(2,1)S(1)}, f32[2,2,256,768]{3,2,1,0:T(8,128)S(1)}, bf16[2,2,64,768]{3,2,1,0:T(8,128)(2,1)}, bf16[2,2,64,768]{3,2,1,0:T(8,128)(2,1)}) custom-call(s32[4]{0:T(128)S(1)} %pad_add_fusion.1.place.token, bf16[2,256,768]{2,1,0:T(8,128)(2,1)S(1)} %copy-done.3, bf16[2,384,768]{2,1,0:T(8,128)(2,1)S(1)} %get-tuple-element.138.kx.refs_4_, ...), custom_call_target="tpu_custom_call" | custom-call | flops 1000 | bytes 1000 | tf_op jit(solution)/shard_map/pallas_call | solution.py:71
  212.4 8.0 %collective-permute-start.16 = (bf16[2,2,2,2,144,384]{5,4,3,2,1,0:T(8,128)(2,1)S(1)}, bf16[2,2,2,2,144,384]{5,4,3,2,1,0:T(8,128)(2,1)S(1)}, u32[]{:S(2)}, u32[]{:S(2)}) collective-permute-start(bf16[2,2,2,2,144,384]{5,4,3,2,1,0:T(8,128)(2,1)S(1)} %get-tuple-element.198), channel_id=1, source_target_pairs={{0,1},{1,0},{2,3},{3,2},{4,5},{5,4},{6,7},{7,6},{8,9},{9,8},{10,11... | collective-permute-start | bytes 5308424 | tf_op jit(solution)/shard_map/ppermute | solution.py:1000
  229.8 7.7 %collective-permute-done.14.refs_1_ = bf16[2,72,768]{2,1,0:T(8,128)(2,1)S(1)} collective-permute-done((bf16[2,72,768]{2,1,0:T(8,128)(2,1)S(1)}, bf16[2,72,768]{2,1,0:T(8,128)(2,1)S(1)}, u32[]{:S(2)}, u32[]{:S(2)}) %collective-permute-start.14) | collective-permute-done | bytes 221216 | tf_op jit(solution)/shard_map/ppermute | solution.py:1000
  239.0 3.8 %shard_map.473 = (bf16[512,768]{1,0:T(8,128)(2,1)S(1)}, bf16[512,768]{1,0:T(8,128)(2,1)S(1)}, f32[16,768]{1,0:T(8,128)S(1)}) custom-call(s32[4]{0:T(128)S(1)} %pad_add_fusion.1.place.token, f32[2,72,768]{2,1,0:T(8,128)S(1)} %get-tuple-element.304.refs_0_, bf16[2,72,768]{2,1,0:T(8,128)(2,1)S(1)} %collective-permute-done.14.refs_1_, ...), custom_call_target="tpu_custom_call" | custom-call | flops 1000 | bytes 1000 | tf_op jit(solution)/shard_map/pallas_call | solution.py:71
  263.8 4.3 %collective-permute-done.19 = bf16[2,2,144,384]{3,2,1,0:T(8,128)(2,1)S(1)} collective-permute-done((bf16[2,2,144,384]{3,2,1,0:T(8,128)(2,1)S(1)}, bf16[2,2,144,384]{3,2,1,0:T(8,128)(2,1)S(1)}, u32[]{:S(2)}, u32[]{:S(2)}) %collective-permute-start.19) | collective-permute-done | bytes 442400 | tf_op jit(solution)/shard_map/ppermute | solution.py:1000
  277.2 7.6 %collective-permute-done.23 = bf16[2,2,144,384]{3,2,1,0:T(8,128)(2,1)S(1)} collective-permute-done((bf16[2,2,144,384]{3,2,1,0:T(8,128)(2,1)S(1)}, bf16[2,2,144,384]{3,2,1,0:T(8,128)(2,1)S(1)}, u32[]{:S(2)}, u32[]{:S(2)}) %collective-permute-start.23) | collective-permute-done | bytes 442400 | tf_op jit(solution)/shard_map/ppermute | solution.py:1000
  284.8 7.1 %collective-permute-done.24 = bf16[2,216,384]{2,1,0:T(8,128)(2,1)S(1)} collective-permute-done((bf16[2,216,384]{2,1,0:T(8,128)(2,1)S(1)}, bf16[2,216,384]{2,1,0:T(8,128)(2,1)S(1)}, u32[]{:S(2)}, u32[]{:S(2)}) %collective-permute-start.24) | collective-permute-done | bytes 331808 | tf_op jit(solution)/shard_map/ppermute | solution.py:1000
  300.1 4.7 %collective-permute-done.27 = bf16[2,144,384]{2,1,0:T(8,128)(2,1)S(1)} collective-permute-done((bf16[2,144,384]{2,1,0:T(8,128)(2,1)S(1)}, bf16[2,144,384]{2,1,0:T(8,128)(2,1)S(1)}, u32[]{:S(2)}, u32[]{:S(2)}) %collective-permute-start.27) | collective-permute-done | bytes 221216 | tf_op jit(solution)/shard_map/ppermute | solution.py:1000
  304.8 4.2 %collective-permute-done.26 = bf16[2,208,384]{2,1,0:T(8,128)(2,1)S(1)} collective-permute-done((bf16[2,208,384]{2,1,0:T(8,128)(2,1)S(1)}, bf16[2,208,384]{2,1,0:T(8,128)(2,1)S(1)}, u32[]{:S(2)}, u32[]{:S(2)}) %collective-permute-start.26) | collective-permute-done | bytes 319520 | tf_op jit(solution)/shard_map/ppermute | solution.py:1000
  318.8 10.6 %collective-permute-done.30 = bf16[144,384]{1,0:T(8,128)(2,1)} collective-permute-done((bf16[144,384]{1,0:T(8,128)(2,1)}, bf16[144,384]{1,0:T(8,128)(2,1)}, u32[]{:S(2)}, u32[]{:S(2)}) %collective-permute-start.30) | collective-permute-done | bytes 110624 | tf_op jit(solution)/shard_map/ppermute | solution.py:1000
  335.0 7.9 %collective-permute-done.32 = bf16[352,384]{1,0:T(8,128)(2,1)S(1)} collective-permute-done((bf16[352,384]{1,0:T(8,128)(2,1)S(1)}, bf16[352,384]{1,0:T(8,128)(2,1)S(1)}, u32[]{:S(2)}, u32[]{:S(2)}) %collective-permute-start.32) | collective-permute-done | bytes 270368 | tf_op jit(solution)/shard_map/ppermute | solution.py:1000
  (346 shorter events, 147.1 us)
Async XLA Ops:
  7.2 243.9 %reduce-scatter.2.cloned.1.call-start = ((), (), s32[]{:S(2)}) async-start(), calls=%async_computation.1 | async-start | bytes 13271040 | tf_op jit(solution)/shard_map/reduce_scatter | solution.py:1156
  8.3 15.0 %collective-permute-start = (bf16[2,64,768]{2,1,0:T(8,128)(2,1)S(1)}, bf16[2,64,768]{2,1,0:T(8,128)(2,1)S(1)}, u32[]{:S(2)}, u32[]{:S(2)}) collective-permute-start(bf16[2,64,768]{2,1,0:T(8,128)(2,1)S(1)} %get-tuple-element.307), channel_id=1, source_target_pairs={{0,4},{4,8},{8,12},{12,16},{16,20},{20,24},{24,28},{1,5},{5,9},{9,... | collective-permute-start | bytes 589832 | tf_op jit(solution)/shard_map/ppermute | solution.py:1006
  25.3 12.6 %collective-permute-start.2 = (bf16[1,2,64,768]{3,2,1,0:T(8,128)(2,1)S(1)}, bf16[1,2,64,768]{3,2,1,0:T(8,128)(2,1)S(1)}, u32[]{:S(2)}, u32[]{:S(2)}) collective-permute-start(bf16[1,2,64,768]{3,2,1,0:T(8,128)(2,1)S(1)} %get-tuple-element.318.refs_0_), channel_id=1, source_target_pairs={{0,16},{4,20},{8,24},{12,28},{16,0},{20,4},{24,8},{28,12},{1,17},{... | collective-permute-start | bytes 589832 | tf_op jit(solution)/shard_map/ppermute | solution.py:1000
  37.9 18.4 %collective-permute-start.5 = (bf16[2,2,64,768]{3,2,1,0:T(8,128)(2,1)S(1)}, bf16[2,2,64,768]{3,2,1,0:T(8,128)(2,1)S(1)}, u32[]{:S(2)}, u32[]{:S(2)}) collective-permute-start(bf16[2,2,64,768]{3,2,1,0:T(8,128)(2,1)S(1)} %pad_maximum_fusion.6), channel_id=1, source_target_pairs={{0,16},{4,20},{8,24},{12,28},{16,0},{20,4},{24,8},{28,12},{1,17},{... | collective-permute-start | bytes 1179656 | tf_op jit(solution)/shard_map/ppermute | solution.py:1000
  38.0 18.3 %collective-permute-start.4 = (bf16[2,2,64,768]{3,2,1,0:T(8,128)(2,1)S(1)}, bf16[2,2,64,768]{3,2,1,0:T(8,128)(2,1)S(1)}, u32[]{:S(2)}, u32[]{:S(2)}) collective-permute-start(bf16[2,2,64,768]{3,2,1,0:T(8,128)(2,1)S(1)} %pad_maximum_fusion.5), channel_id=1, source_target_pairs={{0,8},{4,12},{8,0},{12,4},{16,24},{20,28},{24,16},{28,20},{1,9},{5... | collective-permute-start | bytes 1179656 | tf_op jit(solution)/shard_map/ppermute | solution.py:1000
  57.4 16.6 %collective-permute-start.7 = (bf16[4,2,64,768]{3,2,1,0:T(8,128)(2,1)}, bf16[4,2,64,768]{3,2,1,0:T(8,128)(2,1)}, u32[]{:S(2)}, u32[]{:S(2)}) collective-permute-start(bf16[4,2,64,768]{3,2,1,0:T(8,128)(2,1)} %pad_maximum_fusion.1), channel_id=1, source_target_pairs={{0,8},{4,12},{8,0},{12,4},{16,24},{20,28},{24,16},{28,20},{1,9},{5... | collective-permute-start | bytes 2359304 | tf_op jit(solution)/shard_map/ppermute | solution.py:1000
  58.5 16.7 %collective-permute-start.6 = (bf16[4,2,64,768]{3,2,1,0:T(8,128)(2,1)}, bf16[4,2,64,768]{3,2,1,0:T(8,128)(2,1)}, u32[]{:S(2)}, u32[]{:S(2)}) collective-permute-start(bf16[4,2,64,768]{3,2,1,0:T(8,128)(2,1)} %pad_maximum_fusion), channel_id=1, source_target_pairs={{0,4},{4,0},{8,12},{12,8},{16,20},{20,16},{24,28},{28,24},{1,5},{5... | collective-permute-start | bytes 2359304 | tf_op jit(solution)/shard_map/ppermute | solution.py:1000
  162.3 17.1 %collective-permute-start.8 = (bf16[2,2,2,72,768]{4,3,2,1,0:T(8,128)(2,1)S(1)}, bf16[2,2,2,72,768]{4,3,2,1,0:T(8,128)(2,1)S(1)}, u32[]{:S(2)}, u32[]{:S(2)}) collective-permute-start(bf16[2,2,2,72,768]{4,3,2,1,0:T(8,128)(2,1)S(1)} %bitcast.270), channel_id=1, source_target_pairs={{0,4},{4,0},{8,12},{12,8},{16,20},{20,16},{24,28},{28,24},{1,5},{5... | collective-permute-start | bytes 2654216 | tf_op jit(solution)/shard_map/ppermute | solution.py:1000
  163.1 17.2 %collective-permute-start.9 = (bf16[2,2,2,72,768]{4,3,2,1,0:T(8,128)(2,1)S(1)}, bf16[2,2,2,72,768]{4,3,2,1,0:T(8,128)(2,1)S(1)}, u32[]{:S(2)}, u32[]{:S(2)}) collective-permute-start(bf16[2,2,2,72,768]{4,3,2,1,0:T(8,128)(2,1)S(1)} %bitcast.269), channel_id=1, source_target_pairs={{0,8},{4,12},{8,0},{12,4},{16,24},{20,28},{24,16},{28,20},{1,9},{5... | collective-permute-start | bytes 2654216 | tf_op jit(solution)/shard_map/ppermute | solution.py:1000
  181.5 30.9 %collective-permute-start.11 = (bf16[2,2,72,768]{3,2,1,0:T(8,128)(2,1)}, bf16[2,2,72,768]{3,2,1,0:T(8,128)(2,1)}, u32[]{:S(2)}, u32[]{:S(2)}) collective-permute-start(bf16[2,2,72,768]{3,2,1,0:T(8,128)(2,1)} %get-tuple-element.295), channel_id=1, source_target_pairs={{0,16},{4,20},{8,24},{12,28},{16,0},{20,4},{24,8},{28,12},{1,17},{... | collective-permute-start | bytes 1327112 | tf_op jit(solution)/shard_map/ppermute | solution.py:1000
  189.8 22.7 %collective-permute-start.10 = (bf16[2,2,72,768]{3,2,1,0:T(8,128)(2,1)}, bf16[2,2,72,768]{3,2,1,0:T(8,128)(2,1)}, u32[]{:S(2)}, u32[]{:S(2)}) collective-permute-start(bf16[2,2,72,768]{3,2,1,0:T(8,128)(2,1)} %get-tuple-element.296), channel_id=1, source_target_pairs={{0,8},{4,12},{8,0},{12,4},{16,24},{20,28},{24,16},{28,20},{1,9},{5... | collective-permute-start | bytes 1327112 | tf_op jit(solution)/shard_map/ppermute | solution.py:1000
  199.0 13.4 %collective-permute-start.12 = (bf16[2,2,64,768]{3,2,1,0:T(8,128)(2,1)}, bf16[2,2,64,768]{3,2,1,0:T(8,128)(2,1)S(1)}, u32[]{:S(2)}, u32[]{:S(2)}) collective-permute-start(bf16[2,2,64,768]{3,2,1,0:T(8,128)(2,1)} %get-tuple-element.189), channel_id=1, source_target_pairs={{0,4},{4,8},{8,12},{12,16},{16,20},{20,24},{24,28},{1,5},{5,9},{9,... | collective-permute-start | bytes 1179656 | tf_op jit(solution)/shard_map/ppermute | solution.py:1006
  212.4 25.1 %collective-permute-start.16 = (bf16[2,2,2,2,144,384]{5,4,3,2,1,0:T(8,128)(2,1)S(1)}, bf16[2,2,2,2,144,384]{5,4,3,2,1,0:T(8,128)(2,1)S(1)}, u32[]{:S(2)}, u32[]{:S(2)}) collective-permute-start(bf16[2,2,2,2,144,384]{5,4,3,2,1,0:T(8,128)(2,1)S(1)} %get-tuple-element.198), channel_id=1, source_target_pairs={{0,1},{1,0},{2,3},{3,2},{4,5},{5,4},{6,7},{7,6},{8,9},{9,8},{10,11... | collective-permute-start | bytes 5308424 | tf_op jit(solution)/shard_map/ppermute | solution.py:1000
  225.1 12.4 %collective-permute-start.14 = (bf16[2,72,768]{2,1,0:T(8,128)(2,1)S(1)}, bf16[2,72,768]{2,1,0:T(8,128)(2,1)S(1)}, u32[]{:S(2)}, u32[]{:S(2)}) collective-permute-start(bf16[2,72,768]{2,1,0:T(8,128)(2,1)S(1)} %get-tuple-element.305), channel_id=1, source_target_pairs={{0,16},{4,20},{8,24},{12,28},{16,0},{20,4},{24,8},{28,12},{1,17},{... | collective-permute-start | bytes 663560 | tf_op jit(solution)/shard_map/ppermute | solution.py:1000
  249.0 19.1 %collective-permute-start.18 = (bf16[2,2,2,208,384]{4,3,2,1,0:T(8,128)(2,1)}, bf16[2,2,2,208,384]{4,3,2,1,0:T(8,128)(2,1)}, u32[]{:S(2)}, u32[]{:S(2)}) collective-permute-start(bf16[2,2,2,208,384]{4,3,2,1,0:T(8,128)(2,1)} %get-tuple-element.217), channel_id=1, source_target_pairs={{0,1},{1,0},{2,3},{3,2},{4,5},{5,4},{6,7},{7,6},{8,9},{9,8},{10,11... | collective-permute-start | bytes 3833864 | tf_op jit(solution)/shard_map/ppermute | solution.py:1000
  252.4 16.9 %collective-permute-start.20 = (bf16[2,2,216,384]{3,2,1,0:T(8,128)(2,1)S(1)}, bf16[2,2,216,384]{3,2,1,0:T(8,128)(2,1)S(1)}, u32[]{:S(2)}, u32[]{:S(2)}) collective-permute-start(bf16[2,2,216,384]{3,2,1,0:T(8,128)(2,1)S(1)} %slice_bitcast_fusion.1), channel_id=1, source_target_pairs={{0,4},{4,0},{8,12},{12,8},{16,20},{20,16},{24,28},{28,24},{1,5},{5... | collective-permute-start | bytes 1990664 | tf_op jit(solution)/shard_map/ppermute | solution.py:1000
  255.2 16.3 %collective-permute-start.21 = (bf16[2,2,216,384]{3,2,1,0:T(8,128)(2,1)S(1)}, bf16[2,2,216,384]{3,2,1,0:T(8,128)(2,1)S(1)}, u32[]{:S(2)}, u32[]{:S(2)}) collective-permute-start(bf16[2,2,216,384]{3,2,1,0:T(8,128)(2,1)S(1)} %slice_bitcast_fusion), channel_id=1, source_target_pairs={{0,8},{4,12},{8,0},{12,4},{16,24},{20,28},{24,16},{28,20},{1,9},{5... | collective-permute-start | bytes 1990664 | tf_op jit(solution)/shard_map/ppermute | solution.py:1000
  272.7 21.9 %collective-permute-start.22 = (bf16[2,2,208,384]{3,2,1,0:T(8,128)(2,1)S(1)}, bf16[2,2,208,384]{3,2,1,0:T(8,128)(2,1)S(1)}, u32[]{:S(2)}, u32[]{:S(2)}) collective-permute-start(bf16[2,2,208,384]{3,2,1,0:T(8,128)(2,1)S(1)} %fusion.6), channel_id=1, source_target_pairs={{0,4},{4,0},{8,12},{12,8},{16,20},{20,16},{24,28},{28,24},{1,5},{5... | collective-permute-start | bytes 1916936 | tf_op jit(solution)/shard_map/ppermute | solution.py:1000
  274.8 17.1 %collective-permute-start.24 = (bf16[2,216,384]{2,1,0:T(8,128)(2,1)S(1)}, bf16[2,216,384]{2,1,0:T(8,128)(2,1)S(1)}, u32[]{:S(2)}, u32[]{:S(2)}) collective-permute-start(bf16[2,216,384]{2,1,0:T(8,128)(2,1)S(1)} %get-tuple-element.293), channel_id=1, source_target_pairs={{0,8},{4,12},{8,0},{12,4},{16,24},{20,28},{24,16},{28,20},{1,9},{5... | collective-permute-start | bytes 995336 | tf_op jit(solution)/shard_map/ppermute | solution.py:1000
  276.1 18.6 %collective-permute-start.25 = (bf16[2,216,384]{2,1,0:T(8,128)(2,1)S(1)}, bf16[2,216,384]{2,1,0:T(8,128)(2,1)S(1)}, u32[]{:S(2)}, u32[]{:S(2)}) collective-permute-start(bf16[2,216,384]{2,1,0:T(8,128)(2,1)S(1)} %get-tuple-element.292), channel_id=1, source_target_pairs={{0,4},{4,0},{8,12},{12,8},{16,20},{20,16},{24,28},{28,24},{1,5},{5... | collective-permute-start | bytes 995336 | tf_op jit(solution)/shard_map/ppermute | solution.py:1000
  295.0 17.4 %collective-permute-start.28 = (bf16[432,384]{1,0:T(8,128)(2,1)S(1)}, bf16[432,384]{1,0:T(8,128)(2,1)S(1)}, u32[]{:S(2)}, u32[]{:S(2)}) collective-permute-start(bf16[432,384]{1,0:T(8,128)(2,1)S(1)} %pad_maximum_fusion.8), channel_id=1, source_target_pairs={{0,16},{4,20},{8,24},{12,28},{16,0},{20,4},{24,8},{28,12},{1,17},{... | collective-permute-start | bytes 995336 | tf_op jit(solution)/shard_map/ppermute | solution.py:1000
  312.4 16.9 %collective-permute-start.31 = (bf16[432,384]{1,0:T(8,128)(2,1)S(1)}, bf16[432,384]{1,0:T(8,128)(2,1)}, u32[]{:S(2)}, u32[]{:S(2)}) collective-permute-start(bf16[432,384]{1,0:T(8,128)(2,1)S(1)} %fusion.3), channel_id=1, source_target_pairs={{0,2},{1,3},{2,0},{3,1},{4,6},{5,7},{6,4},{7,5},{8,10},{9,11},{10,... | collective-permute-start | bytes 995336 | tf_op jit(solution)/shard_map/ppermute | solution.py:1000
  314.7 14.7 %collective-permute-start.29 = (bf16[208,384]{1,0:T(8,128)(2,1)S(1)}, bf16[208,384]{1,0:T(8,128)(2,1)}, u32[]{:S(2)}, u32[]{:S(2)}) collective-permute-start(bf16[208,384]{1,0:T(8,128)(2,1)S(1)} %fusion.20), channel_id=1, source_target_pairs={{0,16},{4,20},{8,24},{12,28},{16,0},{20,4},{24,8},{28,12},{1,17},{... | collective-permute-start | bytes 479240 | tf_op jit(solution)/shard_map/ppermute | solution.py:1000
  316.4 12.9 %collective-permute-start.30 = (bf16[144,384]{1,0:T(8,128)(2,1)}, bf16[144,384]{1,0:T(8,128)(2,1)}, u32[]{:S(2)}, u32[]{:S(2)}) collective-permute-start(bf16[144,384]{1,0:T(8,128)(2,1)} %fusion.23), channel_id=1, source_target_pairs={{0,16},{4,20},{8,24},{12,28},{16,0},{20,4},{24,8},{28,12},{1,17},{... | collective-permute-start | bytes 331784 | tf_op jit(solution)/shard_map/ppermute | solution.py:1000
  (114 other events, 995.6 us)
Sparse Core Ops, SparseCore 0:
  142.4 90.9 reduce-scatter.1
